TPU v7x, 32 devices: a whole 2x2x4 slice. The times are simulated.
32 devices in a mesh: az: 8 (over z, x), rad: 4 (over y, core).
Axes of the slice: x: 2, y: 2, z: 4, core: 2. Of those that a mesh axis runs over, the one named last changes fastest.
Arguments:
- state: bfloat16 [4, 64, 2048, 512], P(None, None, 'az', 'rad'), may hold values from -6 to 6
- source: bfloat16 [64, 2048, 512], P(None, 'az', 'rad'), may hold values from -6 to 6
- shear: bfloat16 [64, 2048, 512], P(None, 'az', 'rad'), may hold values from 0.5 to 4
- permeability: bfloat16 [64, 2048, 512], P(None, 'az', 'rad'), may hold values from 0.099609375 to 10
- radial_basis: float32 [512, 512], P('rad'), may hold values from -1 to 2
- radial_eigen: float32 [512], replicated, may hold values from 4e-05 to 4
Outputs:
- correction: bfloat16 [4, 64, 2048, 512], P(None, None, 'az', 'rad')
All inputs are finite; a program needn't handle non-finite values.
Results may differ from a plain program's by a relative error of at most 0.001.
Values may be sent and summed in bfloat16 or wider, within the bound.
No kernel may reach another device: no remote copies, remote signals or barrier semaphores. Data moves between devices by JAX's collectives and lax.ppermute only.
A program may use at most 384 MiB of HBM per device.

v0:
```python
import math

import jax
import jax.numpy as jnp
from jax import lax
from jax.sharding import PartitionSpec as P

NH = 64


biot_coupling = 2.0
storage = 1.0


def padded_2(cells, sides, width):
    for axis, dim in sides:
        count = lax.axis_size(axis)
        head = lax.slice_in_dim(cells, 0, width, axis=dim)
        tail = lax.slice_in_dim(cells, cells.shape[dim] - width, cells.shape[dim], axis=dim)
        cells = jnp.concatenate(
            [
                lax.ppermute(tail, axis, [(i, (i + 1) % count) for i in range(count)]),
                cells,
                lax.ppermute(head, axis, [((i + 1) % count, i) for i in range(count)]),
            ],
            axis=dim,
        )
    return cells


def contract(form, left, right):
    return jnp.einsum(
        form, left, right, precision=lax.Precision.HIGHEST, preferred_element_type=jnp.float32
    )


def neighbor(extended, grid_axis, offset):
    lead = extended.ndim - 3
    window = [slice(None)] * lead + [slice(1, -1)] * 3
    length = extended.shape[lead + grid_axis]
    window[lead + grid_axis] = slice(1 + offset, length - 1 + offset)
    return extended[tuple(window)]


def stencil(extended, source_block):
    center = neighbor(extended, 0, 0)
    diagonal = jnp.zeros_like(center[4])
    momentum = [jnp.zeros_like(center[0]), jnp.zeros_like(center[0]), jnp.zeros_like(center[0])]
    fluid = jnp.zeros_like(center[0])
    for grid_axis in (0, 1, 2):
        for offset in (1, -1):
            beside = neighbor(extended, grid_axis, offset)
            shear_face = 0.5 * (center[4] + beside[4])
            flow_face = 0.5 * (center[5] + beside[5])
            diagonal = diagonal + shear_face
            momentum = [
                momentum[channel] + shear_face * (center[channel] - beside[channel])
                for channel in range(3)
            ]
            fluid = fluid + flow_face * (center[3] - beside[3])
    component_axes = (2, 1, 0)
    pressure = extended[3]
    spread = jnp.zeros_like(center[0])
    parts = []
    for channel in range(3):
        grid_axis = component_axes[channel]
        gradient = 0.5 * (neighbor(pressure, grid_axis, 1) - neighbor(pressure, grid_axis, -1))
        parts.append(-(momentum[channel] + biot_coupling * gradient))
        member = extended[channel]
        spread = spread + 0.5 * (neighbor(member, grid_axis, 1) - neighbor(member, grid_axis, -1))
    parts.append(source_block + biot_coupling * spread + storage * center[3] + fluid)
    return (jnp.stack(parts), diagonal)


def cosine_table(extent):
    row_ids = jnp.arange(extent, dtype=jnp.float32)[:, None]
    col_ids = jnp.arange(extent, dtype=jnp.float32)[None, :]
    scaled = jnp.where(row_ids == 0, math.sqrt(1.0 / extent), math.sqrt(2.0 / extent))
    return scaled * jnp.cos(math.pi * (col_ids + 0.5) * row_ids / extent)


def fourier_pair(rows_len, cols_len, period):
    row_ids = jnp.arange(rows_len, dtype=jnp.int32)[:, None]
    col_ids = jnp.arange(cols_len, dtype=jnp.int32)[None, :]
    angle = 2.0 * math.pi / period * (row_ids * col_ids % period).astype(jnp.float32)
    return (jnp.cos(angle), jnp.sin(angle))


def spectral_solve(coeffs, mode_start, height_start, radial_eigen):
    moved = lax.all_to_all(coeffs, "az", split_axis=0, concat_axis=2, tiled=True)
    mode_count, level_count, length = moved.shape
    inner_len = 128
    outer_len = length // inner_len
    lines = moved.reshape(mode_count, level_count, outer_len, inner_len)
    cos_outer, sin_outer = fourier_pair(outer_len, outer_len, outer_len)
    cos_inner, sin_inner = fourier_pair(inner_len, inner_len, inner_len)
    tw_cos, tw_sin = fourier_pair(outer_len, inner_len, length)
    real_one = contract("mlab,ak->mlkb", lines, cos_outer)
    imag_one = -contract("mlab,ak->mlkb", lines, sin_outer)
    turned_real = real_one * tw_cos + imag_one * tw_sin
    turned_imag = imag_one * tw_cos - real_one * tw_sin
    spec_real = contract("mlkb,bj->mlkj", turned_real, cos_inner) + contract(
        "mlkb,bj->mlkj", turned_imag, sin_inner
    )
    spec_imag = contract("mlkb,bj->mlkj", turned_imag, cos_inner) - contract(
        "mlkb,bj->mlkj", turned_real, sin_inner
    )
    mode_eigen = lax.dynamic_slice_in_dim(radial_eigen, mode_start, mode_count)
    levels = (height_start + jnp.arange(level_count, dtype=jnp.int32)).astype(jnp.float32)
    height_eigen = 4.0 * jnp.sin(math.pi * levels / (2.0 * NH)) ** 2
    first_ids = jnp.arange(outer_len, dtype=jnp.float32)[:, None]
    second_ids = jnp.arange(inner_len, dtype=jnp.float32)[None, :]
    waves = first_ids + outer_len * second_ids
    azimuth_eigen = 4.0 * jnp.sin(math.pi * waves / length) ** 2
    totals = (
        storage
        + mode_eigen[:, None, None, None]
        + height_eigen[None, :, None, None]
        + azimuth_eigen[None, None, :, :]
    )
    solved_real = spec_real / totals
    solved_imag = spec_imag / totals
    back_real = contract("mlkj,bj->mlkb", solved_real, cos_inner) - contract(
        "mlkj,bj->mlkb", solved_imag, sin_inner
    )
    back_imag = contract("mlkj,bj->mlkb", solved_imag, cos_inner) + contract(
        "mlkj,bj->mlkb", solved_real, sin_inner
    )
    untwist_real = back_real * tw_cos - back_imag * tw_sin
    untwist_imag = back_imag * tw_cos + back_real * tw_sin
    signal = contract("mlkb,ak->mlab", untwist_real, cos_outer) - contract(
        "mlkb,ak->mlab", untwist_imag, sin_outer
    )
    signal = (signal * (1.0 / length)).reshape(mode_count, level_count, length)
    return lax.all_to_all(signal, "az", split_axis=2, concat_axis=0, tiled=True)


def precondition(residual_p, radial_basis, radial_eigen):
    cosine = cosine_table(NH)
    heights = contract("lh,har->lar", cosine, residual_p)
    basis_full = lax.all_gather(radial_basis, "rad", axis=0, tiled=True)
    slab = lax.all_to_all(heights, "rad", split_axis=0, concat_axis=2, tiled=True)
    coeffs = contract("lar,rm->mla", slab, basis_full)
    mode_start = lax.axis_index("az") * (coeffs.shape[0] // lax.axis_size("az"))
    height_start = lax.axis_index("rad") * slab.shape[0]
    solved = spectral_solve(coeffs, mode_start, height_start, radial_eigen)
    back_slab = contract("mla,rm->lar", solved, basis_full)
    planes = lax.all_to_all(back_slab, "rad", split_axis=2, concat_axis=0, tiled=True)
    return contract("lh,lar->har", cosine, planes)


def body(state, source, shear, permeability, radial_basis, radial_eigen):
    stacked = jnp.concatenate([state, shear[None], permeability[None]], axis=0)
    padded = padded_2(stacked, (("az", 2), ("rad", 3)), 1)
    rad_count = lax.axis_size("rad")
    rad_place = lax.axis_index("rad")
    column = lax.broadcasted_iota(jnp.int32, (padded.shape[3],), 0)
    outside = (column == 0) & (rad_place == 0) | (column == padded.shape[3] - 1) & (
        rad_place == rad_count - 1
    )
    padded = jnp.where(outside, jnp.zeros((), padded.dtype), padded)
    extended = jnp.pad(padded.astype(jnp.float32), ((0, 0), (1, 1), (0, 0), (0, 0)))
    residual, diagonal = stencil(extended, source.astype(jnp.float32))
    moment_step = residual[:3] / diagonal
    press_step = precondition(residual[3], radial_basis, radial_eigen)
    local_rr = jnp.sum(residual * residual)
    local_rz = jnp.sum(residual[:3] * moment_step) + jnp.sum(residual[3] * press_step)
    total_rr, total_rz = lax.psum((local_rr, local_rz), ("az", "rad"))
    alpha = total_rr / total_rz
    return jnp.concatenate(
        [
            (alpha * moment_step).astype(jnp.bfloat16),
            (alpha * press_step).astype(jnp.bfloat16)[None],
        ],
        axis=0,
    )


def solution(mesh):
    placed = (
        P(None, None, "az", "rad"),
        P(None, "az", "rad"),
        P(None, "az", "rad"),
        P(None, "az", "rad"),
        P("rad", None),
        P(),
    )
    return jax.shard_map(
        body, mesh=mesh, in_specs=placed, out_specs=P(None, None, "az", "rad"), check_vma=False
    )
```

profile of v0, /device:TPU:0, one launch (start us, length us, event | category | flops | bytes accessed | tf_op | source)
XLA Modules:
  0.0 1556.1 jit_solution(9631892999986965583)
XLA Ops:
  6.5 15.2 copy.70
  21.8 17.5 %copy_bitcast_fusion.1 = (bf16[1,64,256,128]{3,1,2,0:T(8,128)(2,1)S(1)}, bf16[1,64,256,128]{3,1,2,0:T(8,128)(2,1)S(1)}) fusion(bf16[64,256,128]{2,1,0:T(8,128)(2,1)S(1)} %copy-done.12, bf16[64,256,128]{2,1,0:T(8,128)(2,1)S(1)} %copy-done.13), kind=kLoop, calls=%fused_computation.174 | loop fusion | bytes 16777216 | tf_op jit(solution)/shard_map/broadcast_in_dim | solution.py:153
  56.1 23.4 %pad_maximum_fusion = bf16[6,64,258,128]{3,1,2,0:T(8,128)(2,1)} fusion(bf16[6,64,1,128]{3,1,2,0:T(8,128)(2,1)S(1)} %collective-permute-done.1, bf16[1,64,256,128]{3,1,2,0:T(8,128)(2,1)} %copy-done.8, bf16[1,64,256,128]{3,1,2,0:T(8,128)(2,1)} %copy-done.9, bf16[4,64,256,128]{3,1,2,0:T(8,128)(2,1)} %copy-done, bf16[6,64,1,128]{3,1,2,0:T(8,128)(2,1)S(1)} %collective-permute-done), kind=kLoop, calls=%fused_computation.20 | loop fusion | flops 50724864 | bytes 50724864 | tf_op jit(solution)/shard_map/concatenate | solution.py:20
  79.5 34.0 %fusion.244 = (bf16[6,64,258,1]{3,1,2,0:T(8,128)(2,1)}, bf16[6,64,258,1]{3,1,2,0:T(8,128)(2,1)}) fusion(bf16[6,64,258,128]{3,1,2,0:T(8,128)(2,1)} %pad_maximum_fusion), kind=kLoop, calls=%fused_computation.311 | loop fusion | bytes 792576 | tf_op jit(solution)/shard_map/slice | solution.py:19
  113.5 27.8 %copy.72 = bf16[6,64,258,1]{2,1,3,0:T(8,128)(2,1)S(1)} copy(bf16[6,64,258,1]{3,1,2,0:T(8,128)(2,1)} %get-tuple-element.19) | data formatting | bytes 396288 | tf_op jit(solution)/shard_map/slice | solution.py:18
  141.4 27.8 %copy.71 = bf16[6,64,258,1]{2,1,3,0:T(8,128)(2,1)S(1)} copy(bf16[6,64,258,1]{3,1,2,0:T(8,128)(2,1)} %get-tuple-element.18) | data formatting | bytes 396288 | tf_op jit(solution)/shard_map/slice | solution.py:19
  170.4 27.9 %copy.74 = bf16[6,64,258,1]{3,1,2,0:T(8,128)(2,1)} copy(bf16[6,64,258,1]{2,1,3,0:T(8,128)(2,1)S(1)} %collective-permute-done.3) | data formatting | bytes 396288 | tf_op jit(solution)/shard_map/ppermute | solution.py:24
  198.3 28.0 %copy.73 = bf16[6,64,258,1]{3,1,2,0:T(8,128)(2,1)} copy(bf16[6,64,258,1]{2,1,3,0:T(8,128)(2,1)S(1)} %collective-permute-done.2) | data formatting | bytes 396288 | tf_op jit(solution)/shard_map/ppermute | solution.py:22
  226.2 69.2 %fusion = f32[6,64,258,130]{3,1,2,0:T(8,128)} fusion(bf16[6,64,258,1]{3,1,2,0:T(8,128)(2,1)} %copy.74, bf16[6,64,1,128]{3,1,2,0:T(8,128)(2,1)S(1)} %collective-permute-done.1, bf16[1,64,256,128]{3,1,2,0:T(8,128)(2,1)} %copy-done.8, bf16[1,64,256,128]{3,1,2,0:T(8,128)(2,1)} %copy-done.9, bf16[4,64,256,128]{3,1,2,0:T(8,128)(2,1)} %copy-done, ...), kind=kLoop, calls=%fused_computation.17 | loop fusion | flops 206069760 | bytes 77276288 | tf_op jit(solution)/shard_map/convert_element_type | solution.py:162
  295.4 49.0 %fusion.2 = (f32[66,258,130]{2,0,1:T(8,128)}, f32[66,258,130]{2,0,1:T(8,128)}, f32[66,258,130]{2,0,1:T(8,128)}, f32[66,258,130]{2,0,1:T(8,128)}) fusion(f32[6,64,258,130]{3,1,2,0:T(8,128)} %fusion), kind=kLoop, calls=%fused_computation.24 | loop fusion | bytes 86935680 | tf_op jit(solution)/shard_map/squeeze | solution.py:62
  344.5 120.0 %fusion.44 = f32[64,256,128]{2,0,1:T(8,128)} fusion(f32[6,64,258,130]{3,1,2,0:T(8,128)} %fusion, f32[66,258,130]{2,0,1:T(8,128)} %get-tuple-element.17, f32[66,258,130]{2,0,1:T(8,128)} %get-tuple-element.15, f32[66,258,130]{2,0,1:T(8,128)} %get-tuple-element.16, bf16[64,256,128]{2,1,0:T(8,128)(2,1)} %param.7), kind=kLoop, calls=%fused_computation.69 | loop fusion | flops 79691776 | bytes 248250368 | tf_op jit(solution)/shard_map/add | solution.py:71
  464.5 10.8 fusion.146
  489.9 98.0 %all-to-all-done = f32[64,256,128]{2,1,0:T(8,128)} async-done(((f32[64,256,128]{2,1,0:T(8,128)}), f32[64,256,128]{2,1,0:T(8,128)}, u32[]{:S(2)}, u32[]{:S(2)}) %all-to-all-start) | async-done | bytes 8388640 | tf_op jit(solution)/shard_map/all_to_all | solution.py:142
  587.9 12.4 copy.108
  600.3 10.3 all_to_all.53
  610.5 17.0 %convolution_bitcast_fusion = f32[512,16,256]{0,2,1:T(8,128)} fusion(f32[16,256,512]{2,1,0:T(8,128)} %all_to_all.53, f32[512,512]{1,0:T(8,128)} %all-gather.2.cloned.1.call-done), kind=kOutput, calls=%fused_computation.184 | convolution fusion | flops 12884901888 | bytes 17825792 | tf_op jit(solution)/shard_map/lar,rm->mla/dot_general | solution.py:32
  627.5 10.3 copy.79
  644.0 182.0 %all-to-all-done.1 = f32[512,16,256]{2,1,0:T(8,128)} async-done(((f32[512,16,256]{2,1,0:T(8,128)}), f32[512,16,256]{2,1,0:T(8,128)}, u32[]{:S(2)}, u32[]{:S(2)}) %all-to-all-start.1) | async-done | bytes 8388640 | tf_op jit(solution)/shard_map/all_to_all | solution.py:90
  826.0 14.9 copy.80
  849.8 10.0 fusion.172
  868.1 9.9 fusion.94
  877.9 10.3 fusion.96
  888.2 13.2 add_divide_fusion.1
  901.4 10.1 fusion.131
  911.5 9.5 fusion.140
  921.0 14.5 add_divide_fusion
  935.5 11.7 fusion.137
  947.1 9.6 fusion.133
  956.7 15.3 fusion.102
  972.0 20.9 %multiply_bitcast_fusion = f32[64,16,16,128]{3,2,1,0:T(8,128)} fusion(f32[16,64,16,128]{3,0,2,1:T(8,128)} %fusion.102, f32[16,128]{1,0:T(8,128)S(1)} %get-tuple-element.28, f32[16,128]{1,0:T(8,128)S(1)} %get-tuple-element.29, f32[64,16,16,128]{3,2,1,0:T(8,128)} %fusion.137, f32[64,16,16,128]{3,2,1,0:T(8,128)} %copy-done.2, ...), kind=kOutput, calls=%fused_computation.161 | convolution fusion | flops 417336832 | bytes 50348032 | tf_op jit(solution)/shard_map/mlkb,ak->mlab/dot_general | solution.py:32
  993.0 12.2 copy.100
  1005.2 15.4 reshape.227
  1026.0 58.6 %multiply_bitcast_fusion.1 = (f32[64,256,128]{2,0,1:T(8,128)}, f32[1,64,256,128]{3,1,2,0:T(8,128)}, f32[1,64,256,128]{3,1,2,0:T(8,128)}, f32[1,64,256,128]{3,1,2...) fusion(f32[6,64,258,130]{3,1,2,0:T(8,128)} %fusion), kind=kLoop, calls=%fused_computation.172 | loop fusion | flops 25165824 | bytes 202113024 | tf_op jit(solution)/shard_map/div | solution.py:164
  1084.6 68.7 %fusion.75 = f32[1,64,256,128]{3,1,2,0:T(8,128)} fusion(f32[66,258,130]{2,0,1:T(8,128)} %get-tuple-element.14, f32[6,64,258,130]{3,1,2,0:T(8,128)} %fusion, f32[1,64,256,128]{3,1,2,0:T(8,128)} %get-tuple-element.13, f32[1,64,256,128]{3,1,2,0:T(8,128)} %get-tuple-element.12, f32[1,64,256,128]{3,1,2,0:T(8,128)} %get-tuple-element.11, ...), kind=kLoop, calls=%fused_computation.113 | loop fusion | flops 54525952 | bytes 218890240 | tf_op jit(solution)/shard_map/stack | solution.py:72
  1153.4 70.0 %fusion.82 = f32[1,64,256,128]{3,1,2,0:T(8,128)} fusion(f32[66,258,130]{2,0,1:T(8,128)} %get-tuple-element.14, f32[6,64,258,130]{3,1,2,0:T(8,128)} %fusion, f32[1,64,256,128]{3,1,2,0:T(8,128)} %get-tuple-element.13, f32[1,64,256,128]{3,1,2,0:T(8,128)} %get-tuple-element.12, f32[1,64,256,128]{3,1,2,0:T(8,128)} %get-tuple-element.11, ...), kind=kLoop, calls=%fused_computation.125 | loop fusion | flops 54525952 | bytes 218890240 | tf_op jit(solution)/shard_map/stack | solution.py:72
  1223.9 26.5 %reduce = f32[8,262144]{1,0:T(8,128)} reduce(f32[8,1,262144]{2,1,0:T(1,128)} %all-to-all-done.2, f32[]{:T(128)} %broadcast.264), dimensions={1}, to_apply=%all_to_all.57.reduce_sub_computation | reduce | bytes 16777220 | tf_op jit(solution)/shard_map/all_to_all | solution.py:135
  1250.4 16.1 %reshape.228 = f32[2048,16,64]{2,1,0:T(8,128)} reshape(f32[8,262144]{1,0:T(8,128)} %reduce) | data formatting | bytes 16777216
  1266.4 12.9 copy.103
  1279.3 30.0 %fusion.125 = f32[16,256,512]{2,1,0:T(8,128)} fusion(f32[512,16,256]{2,0,1:T(8,128)} %bitcast.219, f32[512,512]{1,0:T(8,128)S(1)} %copy-done.11), kind=kOutput, calls=%fused_computation.185 | convolution fusion | flops 12884901888 | bytes 17825792 | tf_op jit(solution)/shard_map/mla,rm->lar/dot_general | solution.py:32
  1309.3 10.3 copy.87
  1325.5 66.6 %fusion.89 = f32[1,64,256,128]{3,1,2,0:T(8,128)} fusion(f32[66,258,130]{2,0,1:T(8,128)} %get-tuple-element.14, f32[6,64,258,130]{3,1,2,0:T(8,128)} %fusion, f32[1,64,256,128]{3,1,2,0:T(8,128)} %get-tuple-element.13, f32[1,64,256,128]{3,1,2,0:T(8,128)} %get-tuple-element.12, f32[1,64,256,128]{3,1,2,0:T(8,128)} %get-tuple-element.11, ...), kind=kLoop, calls=%fused_computation.137 | loop fusion | flops 54525952 | bytes 218890240 | tf_op jit(solution)/shard_map/stack | solution.py:72
  1392.1 16.5 %fusion.1 = f32[]{:T(128)} fusion(f32[1,64,256,128]{3,1,2,0:T(8,128)} %bitcast.216, f32[1,64,256,128]{3,1,2,0:T(8,128)} %fusion.75, f32[1,64,256,128]{3,1,2,0:T(8,128)} %fusion.82, f32[1,64,256,128]{3,1,2,0:T(8,128)} %fusion.89), kind=kLoop, calls=%fused_computation.19 | loop fusion | flops 41943040 | bytes 33554436 | tf_op jit(solution)/shard_map/reduce_sum | solution.py:166
  1408.7 12.2 multiply_reduce_fusion
  1420.9 10.7 copy.88
  1431.6 14.5 multiply_reduce_fusion.1
  1447.4 41.7 %all-reduce.1 = (f32[]{:T(128)}, f32[]{:T(128)}) all-reduce(f32[]{:T(128)} %fusion.1, f32[]{:T(128)S(6)} %add.407), channel_id=1, replica_groups=mesh['az'=8,'rad'=4] {'az','rad'}, use_global_device_ids=true, to_apply=%region_1.2 | all-reduce | flops 2 | bytes 16 | tf_op jit(solution)/shard_map/psum | solution.py:168
  1490.4 12.4 multiply_convert_fusion
  1511.9 36.9 %copy.89 = bf16[4,64,256,128]{3,2,1,0:T(8,128)(2,1)} copy(bf16[4,64,256,128]{3,1,2,0:T(8,128)(2,1)S(1)} %pad_maximum_fusion.2) | data formatting | bytes 33554432 | tf_op jit(solution)/shard_map/concatenate | solution.py:170
  (68 shorter events, 76.9 us)
Async XLA Ops:
  6.5 15.2 copy-start.12
  6.5 15.2 copy-start.13
  21.8 17.6 %copy-start = (bf16[4,64,256,128]{3,1,2,0:T(8,128)(2,1)}, bf16[4,64,256,128]{3,1,2,0:T(8,128)(2,1)S(1)}, u32[]{:S(2)}) copy-start(bf16[4,64,256,128]{3,1,2,0:T(8,128)(2,1)S(1)} %copy.70) | copy-start | bytes 50331652
  39.3 2.0 copy-start.8
  39.3 3.3 copy-start.9
  42.6 8.2 collective-permute-start.1
  48.6 7.5 collective-permute-start
  141.3 29.0 %collective-permute-start.3 = (bf16[6,64,258,1]{2,1,3,0:T(8,128)(2,1)S(1)}, bf16[6,64,258,1]{2,1,3,0:T(8,128)(2,1)S(1)}, u32[]{:S(2)}, u32[]{:S(2)}) collective-permute-start(bf16[6,64,258,1]{2,1,3,0:T(8,128)(2,1)S(1)} %copy.72), channel_id=1, source_target_pairs={{1,0},{2,1},{3,2},{0,3},{5,4},{6,5},{7,6},{4,7},{9,8},{10,9},{11,1... | collective-permute-start | bytes 594440 | tf_op jit(solution)/shard_map/ppermute | solution.py:24
  169.2 29.0 %collective-permute-start.2 = (bf16[6,64,258,1]{2,1,3,0:T(8,128)(2,1)S(1)}, bf16[6,64,258,1]{2,1,3,0:T(8,128)(2,1)S(1)}, u32[]{:S(2)}, u32[]{:S(2)}) collective-permute-start(bf16[6,64,258,1]{2,1,3,0:T(8,128)(2,1)S(1)} %copy.71), channel_id=1, source_target_pairs={{0,1},{1,2},{2,3},{3,0},{4,5},{5,6},{6,7},{7,4},{8,9},{9,10},{10,1... | collective-permute-start | bytes 594440 | tf_op jit(solution)/shard_map/ppermute | solution.py:22
  344.4 120.0 %copy-start.14 = (f32[64]{0:T(128)S(1)}, f32[64]{0:T(128)}, u32[]{:S(2)}) copy-start(f32[64]{0:T(128)} %get-tuple-element.26) | copy-start | bytes 772
  344.5 120.0 %copy-start.16 = (f32[64]{0:T(128)S(1)}, f32[64]{0:T(128)}, u32[]{:S(2)}) copy-start(f32[64]{0:T(128)} %get-tuple-element.27) | copy-start | bytes 772
  483.5 104.4 %all-to-all-start = ((f32[64,256,128]{2,1,0:T(8,128)}), f32[64,256,128]{2,1,0:T(8,128)}, u32[]{:S(2)}, u32[]{:S(2)}) async-start(f32[64,256,128]{2,1,0:T(8,128)} %copy.77), calls=%async_computation | async-start | bytes 16777216 | tf_op jit(solution)/shard_map/all_to_all | solution.py:142
  489.2 121.4 %all-gather.2.cloned.1.call-start = ((), (), s32[]{:S(2)}) async-start(), calls=%async_computation.4 | async-start | bytes 1310720 | tf_op jit(solution)/shard_map/all_gather | solution.py:141
  637.8 188.2 %all-to-all-start.1 = ((f32[512,16,256]{2,1,0:T(8,128)}), f32[512,16,256]{2,1,0:T(8,128)}, u32[]{:S(2)}, u32[]{:S(2)}) async-start(f32[512,16,256]{2,1,0:T(8,128)} %copy.79), calls=%async_computation.1 | async-start | bytes 16777216 | tf_op jit(solution)/shard_map/all_to_all | solution.py:90
  849.8 10.0 copy-start.5
  859.8 28.4 %copy-start.6 = (f32[16,64,16,128]{3,0,2,1:T(8,128)}, f32[16,64,16,128]{3,0,2,1:T(8,128)S(1)}, u32[]{:S(2)}) copy-start(f32[16,64,16,128]{3,0,2,1:T(8,128)S(1)} %fusion.172) | copy-start | bytes 25165828
  868.1 9.9 copy-start.7
  901.4 10.1 copy-start.4
  911.5 45.2 %copy-start.2 = (f32[64,16,16,128]{3,2,1,0:T(8,128)}, f32[64,16,16,128]{3,2,1,0:T(8,128)S(1)}, u32[]{:S(2)}) copy-start(f32[64,16,16,128]{3,2,1,0:T(8,128)S(1)} %fusion.131) | copy-start | bytes 25165828
  935.5 11.7 copy-start.3
  1020.6 202.8 %all-to-all-start.2 = ((f32[8,1,262144]{2,1,0:T(1,128)}), f32[8,1,262144]{2,1,0:T(1,128)}, u32[]{:S(2)}, u32[]{:S(2)}) async-start(f32[8,1,262144]{2,1,0:T(1,128)} %reshape.227), calls=%async_computation.2 | async-start | bytes 16777216 | tf_op jit(solution)/shard_map/all_to_all | solution.py:135
  1266.4 12.9 copy-start.11
  1319.6 101.3 %all-to-all-start.3 = ((f32[16,256,512]{1,0,2:T(8,128)}), f32[16,256,512]{1,0,2:T(8,128)}, u32[]{:S(2)}, u32[]{:S(2)}) async-start(f32[16,256,512]{1,0,2:T(8,128)} %copy.87), calls=%async_computation.3 | async-start | bytes 16777216 | tf_op jit(solution)/shard_map/all_to_all | solution.py:148
  1392.1 16.6 %copy-start.1 = (f32[1,64,256,128]{3,1,2,0:T(8,128)S(1)}, f32[1,64,256,128]{3,1,2,0:T(8,128)}, u32[]{:S(2)}) copy-start(f32[1,64,256,128]{3,1,2,0:T(8,128)} %fusion.89) | copy-start | bytes 25165828
  1420.9 10.7 copy-start.15
  1420.9 10.7 copy-start.17
  1490.4 13.1 copy-start.10
Sparse Core Ops, SparseCore 0:
  491.5 20.1 all-gather.1
where the time goes:
time: 1570 us; the launch traced here: 1560 us
  other arithmetic  554 us (35%)
  local copies, waits for them, and re-layouts  411 us (26%)
  waiting for transfers between devices  288 us (18%)
  matrix products  215 us (14%)
  blocking collectives  41.7 us (3%)
  starting transfers between devices  29.4 us (2%)
  between operations  16.8 us (1%)
    dot_general x16, matrix products, contract(): jnp.einsum(form, left, right, precision=lax.Precision.HIGHEST, preferred_...  215 us
    another operation x3, other arithmetic, stencil(): return (jnp.stack(parts), diagonal)  205 us
    all_to_all x1, waiting for transfers between devices, spectral_solve(): lax.all_to_all(coeffs, 'az', split_axis=0, concat_axis=2, tiled=True)  182 us
    add x1, other arithmetic, stencil(): source_block + biot_coupling * spread + storage * center[3] + fluid  120 us
    all_to_all x1, waiting for transfers between devices, precondition(): lax.all_to_all(heights, 'rad', split_axis=0, concat_axis=2, tiled=True)  98 us
    convert_element_type x1, other arithmetic, body(): padded.astype(jnp.float32)  69.2 us
    slice x2, local copies, waits for them, and re-layouts, padded_2(): lax.slice_in_dim(cells, cells.shape[dim] - width, cells.shape[dim], axis=...  61.8 us
    div x1, other arithmetic, body(): moment_step = residual[:3] / diagonal  58.6 us
  transfers between devices with their start and end apart: 9, of which 4 were waited for; matrix products, arithmetic and copies ran while one was open for 23% of the time, Pallas kernels for 0%

commit v1 on v0

v1 whole, which is shorter than its diff:
```python
import math

import jax
import jax.numpy as jnp
from jax import lax
from jax.experimental import pallas as pl
from jax.experimental.pallas import tpu as pltpu
from jax.sharding import PartitionSpec as P


biot_coupling = 2.0
storage = 1.0

f32 = jnp.float32
bf16 = jnp.bfloat16


SLAB = 8
ROWS = 32
TILE = 32
CHUNKS = 2


def params(limit=56):
    return pltpu.CompilerParams(
        dimension_semantics=("arbitrary",), vmem_limit_bytes=limit * 1024 * 1024
    )


def lanes_of(shape):
    return lax.broadcasted_iota(jnp.int32, shape, len(shape) - 1)


def split(x):
    high = x.astype(bf16)
    low = (x - high.astype(f32)).astype(bf16)
    return high, low


def fold(x):
    total = x[0:8]
    for start in range(8, x.shape[0], 8):
        total = total + x[start : start + 8]
    return total


def split_table(x):
    rounded = lax.reduce_precision(x, exponent_bits=8, mantissa_bits=7)
    return rounded.astype(bf16), (x - rounded).astype(bf16)


def edges_kernel(*refs):
    top_ref, end_ref = refs[:2]
    fields = refs[2:5]
    cols_ref, first_ref, last_ref, acc = refs[5:]
    step = pl.program_id(0)
    slab, count, width = fields[2].shape
    rows = min(64, count)
    lane = lanes_of((rows, width))
    for c in range(3):
        src = fields[c].at[0] if len(fields[c].shape) == 4 else fields[c]
        for start in range(0, count, rows):
            value = acc[c, start : start + rows, :]
            for i in range(slab):
                h = step * slab + i
                x = src[i, start : start + rows, :].astype(f32)
                value = jnp.where((lane >> 1) == h, pltpu.roll(x, 2 * h + 1, 1), value)
                if c and start == 0:
                    first_ref[c, pl.ds(h, 1), :] = x[0:1]
                if c and start + rows == count:
                    last_ref[c, pl.ds(h, 1), :] = x[rows - 1 : rows]
            acc[c, start : start + rows, :] = value
    for i in range(slab):
        h = step * slab + i
        strip = end_ref.shape[2]
        first_ref[0, pl.ds(h, 1), :] = top_ref[0, i].astype(f32)[0:1]
        last_ref[0, pl.ds(h, 1), :] = end_ref[0, i].astype(f32)[strip - 1 : strip]

    @pl.when(step == pl.num_programs(0) - 1)
    def _():
        for c in range(3):
            for start in range(0, count, rows):
                v = acc[c, start : start + rows, :]
                swapped = jnp.where(lane % 2 == 0, pltpu.roll(v, width - 1, 1), pltpu.roll(v, 1, 1))
                cols_ref[c, start : start + rows, :] = swapped.astype(bf16)


def edges(state, coefficient, row_only, channels):
    _, height, count, width = state.shape
    strip = 16
    whole = lambda *shape: pl.BlockSpec(shape, lambda i: (0,) * len(shape))
    full = lambda c: pl.BlockSpec((1, SLAB, count, width), lambda i: (c, i, 0, 0))
    return pl.pallas_call(
        edges_kernel,
        grid=(height // SLAB,),
        in_specs=[
            pl.BlockSpec((1, SLAB, strip, width), lambda i: (row_only, i, 0, 0)),
            pl.BlockSpec((1, SLAB, strip, width), lambda i: (row_only, i, count // strip - 1, 0)),
            full(channels[0]),
            full(channels[1]),
            pl.BlockSpec((SLAB, count, width), lambda i: (i, 0, 0)),
        ],
        out_specs=[whole(3, count, width), whole(3, height, width), whole(3, height, width)],
        out_shape=[
            jax.ShapeDtypeStruct((3, count, width), bf16),
            jax.ShapeDtypeStruct((3, height, width), f32),
            jax.ShapeDtypeStruct((3, height, width), f32),
        ],
        scratch_shapes=[pltpu.VMEM((3, count, width), f32)],
        compiler_params=params(),
        name="edges",
    )(state, state, state, state, coefficient)


def neighbours(cols, first, last):
    n_rad = lax.axis_size("rad")
    n_az = lax.axis_size("az")
    from_right = lax.ppermute(cols, "rad", [(i + 1, i) for i in range(n_rad - 1)])
    from_left = lax.ppermute(cols, "rad", [(i, i + 1) for i in range(n_rad - 1)])
    before = lax.ppermute(last, "az", [(i, (i + 1) % n_az) for i in range(n_az)])
    after = lax.ppermute(first, "az", [((i + 1) % n_az, i) for i in range(n_az)])
    beside = jnp.where(lanes_of(cols.shape) % 2 == 0, from_right, from_left)
    return beside, before, after


def stage(scratch, center, above, below, before, after, step, steps, slab, count):
    top = jnp.where(step > 0, 1.0, 0.0)
    bottom = jnp.where(step < steps - 1, 1.0, 0.0)
    scratch[0, 8 : 8 + count, :] = above[...].astype(f32) * top
    scratch[slab + 1, 8 : 8 + count, :] = below[...].astype(f32) * bottom
    for i in range(slab):
        scratch[i + 1, 8 : 8 + count, :] = center[i].astype(f32)
        if before is not None:
            h = step * slab + i
            scratch[i + 1, 7:8, :] = before[pl.ds(h, 1), :]
            scratch[i + 1, 8 + count : 9 + count, :] = after[pl.ds(h, 1), :]


def radial_pair(x, beside, lane):
    width = x.shape[1]
    right = jnp.where(lane == width - 1, beside, pltpu.roll(x, width - 1, 1))
    left = jnp.where(lane == 0, beside, pltpu.roll(x, 1, 1))
    return right, left


def fluid_kernel(
    p_ref, p_up, p_dn, k_ref, k_up, k_dn, z_ref, z_up, z_dn, r_ref, t_ref, src_ref,
    beside_ref, before_ref, after_ref, cos_ref,
    *rest,
):
    outs, (sum_ref, ps, ks, zs, ts, res) = rest[:-6], rest[-6:]
    step = pl.program_id(0)
    slab, count, width = src_ref.shape
    height = before_ref.shape[1]
    steps = height // slab
    tile, levels, _ = outs[0].shape

    @pl.when(step == 0)
    def _():
        sum_ref[...] = jnp.zeros_like(sum_ref)

    @pl.when(step < steps)
    def _():
        stage(ps, p_ref.at[0], p_up.at[0, 0], p_dn.at[0, 0], before_ref.at[1], after_ref.at[1], step, steps, slab, count)
        stage(ks, k_ref, k_up.at[0], k_dn.at[0], before_ref.at[2], after_ref.at[2], step, steps, slab, count)
        stage(zs, z_ref.at[0], z_up.at[0, 0], z_dn.at[0, 0], None, None, step, steps, slab, count)
        for i in range(slab):
            h = step * slab + i
            ts[i, 8 : 8 + count, :] = t_ref[0, i].astype(f32)
            ts[i, 7:8, :] = before_ref[0, pl.ds(h, 1), :]
            ts[i, 8 + count : 9 + count, :] = after_ref[0, pl.ds(h, 1), :]
        lane = lanes_of((ROWS, width))

        def plane(i, total):
            h = step * slab + i
            shift = 2 * height - 1 - 2 * h
            for a in range(0, count, ROWS):
                at = slice(8 + a, 8 + a + ROWS)
                prev = slice(7 + a, 7 + a + ROWS)
                nxt = slice(9 + a, 9 + a + ROWS)
                own = slice(a, a + ROWS)
                p = ps[i + 1, at, :]
                k = ks[i + 1, at, :]
                nb = [pltpu.roll(beside_ref[c, own, :].astype(f32), shift, 1) for c in range(3)]
                p_r, p_l = radial_pair(p, nb[1], lane)
                k_r, k_l = radial_pair(k, nb[2], lane)
                flux = (k + k_r) * (p - p_r) + (k + k_l) * (p - p_l)
                flux += (k + ks[i + 1, nxt, :]) * (p - ps[i + 1, nxt, :])
                flux += (k + ks[i + 1, prev, :]) * (p - ps[i + 1, prev, :])
                flux += (k + ks[i + 2, at, :]) * (p - ps[i + 2, at, :])
                flux += (k + ks[i, at, :]) * (p - ps[i, at, :])
                u_r, u_l = radial_pair(r_ref[0, i, own, :].astype(f32), nb[0], lane)
                spread = (u_r - u_l) + (ts[i, nxt, :] - ts[i, prev, :])
                spread += zs[i + 2, at, :] - zs[i, at, :]
                value = src_ref[i, own, :].astype(f32) + (0.5 * biot_coupling) * spread
                value = value + storage * p + 0.5 * flux
                res[pl.ds(pl.multiple_of(h * count + a, ROWS), ROWS), :] = value
                total = total + fold(value * value)
            return total

        sum_ref[...] += lax.fori_loop(0, slab, plane, jnp.zeros((8, width), f32))

    @pl.when(step >= steps)
    def _():
        base = (step - steps) * tile

        def pair(j, carry):
            highs, lows = [], []
            for s in range(2):
                x = res[pl.ds(base + 2 * j + s, height, stride=count), :]
                high, low = split(x)
                highs.append(high)
                lows.append(low)
            high = jnp.concatenate(highs, axis=1)
            low = jnp.concatenate(lows, axis=1)
            stacked = jnp.concatenate([high, low, high], axis=0)
            y = jnp.dot(cos_ref[...], stacked, preferred_element_type=f32)
            for s in range(2):
                for block, out in enumerate(outs):
                    out[2 * j + s, :, :] = y[
                        block * levels : (block + 1) * levels, s * width : (s + 1) * width
                    ]
            return carry

        lax.fori_loop(0, tile // 2, pair, 0, unroll=4)


def plane_specs(channel, slab, steps, count, width):
    last = steps * slab - 1
    at = lambda i: jnp.minimum(i, steps - 1)
    up = lambda i: jnp.maximum(at(i) * slab - 1, 0)
    down = lambda i: jnp.minimum(at(i) * slab + slab, last)
    if channel is None:
        return [
            pl.BlockSpec((slab, count, width), lambda i: (at(i), 0, 0)),
            pl.BlockSpec((1, count, width), lambda i: (up(i), 0, 0)),
            pl.BlockSpec((1, count, width), lambda i: (down(i), 0, 0)),
        ]
    return [
        pl.BlockSpec((1, slab, count, width), lambda i: (channel, at(i), 0, 0)),
        pl.BlockSpec((1, 1, count, width), lambda i: (channel, up(i), 0, 0)),
        pl.BlockSpec((1, 1, count, width), lambda i: (channel, down(i), 0, 0)),
    ]


def fluid(state, source, perm, beside, before, after, cosine, pieces):
    _, height, count, width = state.shape
    steps = height // SLAB
    tile = min(TILE, count)
    levels = height // pieces
    specs = lambda c: plane_specs(c, SLAB, steps, count, width)
    whole = lambda x: pl.BlockSpec(x.shape, lambda i: (0,) * x.ndim)
    high, low = split_table(cosine)
    table = jnp.concatenate([high, high, low], axis=1)
    return pl.pallas_call(
        fluid_kernel,
        grid=(steps + count // tile,),
        in_specs=[
            *specs(3), *specs(None), *specs(2), specs(0)[0], specs(1)[0], specs(None)[0],
            whole(beside), whole(before), whole(after), whole(table),
        ],
        out_specs=[
            *[pl.BlockSpec((tile, levels, width), lambda i: (jnp.maximum(i - steps, 0), 0, 0))] * pieces,
            pl.BlockSpec((8, width), lambda i: (0, 0)),
        ],
        out_shape=[
            *[jax.ShapeDtypeStruct((count, levels, width), f32)] * pieces,
            jax.ShapeDtypeStruct((8, width), f32),
        ],
        scratch_shapes=[
            pltpu.VMEM((SLAB + 2, count + 16, width), f32),
            pltpu.VMEM((SLAB + 2, count + 16, width), f32),
            pltpu.VMEM((SLAB + 2, count + 16, width), f32),
            pltpu.VMEM((SLAB, count + 16, width), f32),
            pltpu.VMEM((height * count, width), f32),
        ],
        compiler_params=params(),
        name="fluid",
    )(state, state, state, perm, perm, perm, state, state, state, state, state, source,
      beside, before, after, table)


def momentum_kernel(*refs):
    fields = [refs[3 * c : 3 * c + 3] for c in range(5)]
    fluid_edges, solid_edges = refs[15:18], refs[18:21]
    besides = [e[0].at[c] for e, c in zip([fluid_edges, solid_edges, solid_edges, fluid_edges, solid_edges], (0, 0, 1, 1, 2))]
    row_edges = [solid_edges, fluid_edges, solid_edges, fluid_edges, solid_edges]
    befores = [e[1].at[c] for e, c in zip(row_edges, (0, 0, 1, 1, 2))]
    afters = [e[2].at[c] for e, c in zip(row_edges, (0, 0, 1, 1, 2))]
    out_ref, rr_ref, rz_ref = refs[21:24]
    scratch = refs[24:29]
    step = pl.program_id(0)
    steps = pl.num_programs(0)
    _, slab, count, width = out_ref.shape
    height = fluid_edges[1].shape[1]

    @pl.when(step == 0)
    def _():
        rr_ref[...] = jnp.zeros_like(rr_ref)
        rz_ref[...] = jnp.zeros_like(rz_ref)

    for c in range(5):
        center, up, down = fields[c]
        if c < 4:
            center, up, down = center.at[0], up.at[0, 0], down.at[0, 0]
        else:
            up, down = up.at[0], down.at[0]
        stage(scratch[c], center, up, down, befores[c], afters[c], step, steps, slab, count)
    lane = lanes_of((ROWS, width))

    def plane(i, totals):
        rr, rz = totals
        h = step * slab + i
        shift = 2 * height - 1 - 2 * h
        for a in range(0, count, ROWS):
            at = slice(8 + a, 8 + a + ROWS)
            prev = slice(7 + a, 7 + a + ROWS)
            nxt = slice(9 + a, 9 + a + ROWS)
            own = slice(a, a + ROWS)

            def around(c):
                s = scratch[c]
                x = s[i + 1, at, :]
                nb = pltpu.roll(besides[c][own, :].astype(f32), shift, 1)
                right, left = radial_pair(x, nb, lane)
                return x, (right, left, s[i + 1, nxt, :], s[i + 1, prev, :], s[i + 2, at, :], s[i, at, :])

            g, g_around = around(4)
            faces = [g + other for other in g_around]
            diagonal = faces[0]
            for face in faces[1:]:
                diagonal = diagonal + face
            inverse = 1.0 / diagonal
            _, p = around(3)
            for c in range(3):
                u, u_around = around(c)
                moment = faces[0] * (u - u_around[0])
                for face, other in zip(faces[1:], u_around[1:]):
                    moment = moment + face * (u - other)
                gradient = p[2 * c] - p[2 * c + 1]
                value = -(0.5 * moment + (0.5 * biot_coupling) * gradient)
                step_c = (2.0 * value) * inverse
                out_ref[c, i, own, :] = step_c
                rr = rr + fold(value * value)
                rz = rz + fold(value * step_c)
        return rr, rz

    zero = jnp.zeros((8, width), f32)
    rr, rz = lax.fori_loop(0, slab, plane, (zero, zero))
    rr_ref[...] += rr
    rz_ref[...] += rz


def momentum(state, shear, fluid_edges, solid_edges):
    _, height, count, width = state.shape
    steps = height // SLAB
    specs = lambda c: plane_specs(c, SLAB, steps, count, width)
    whole = lambda x: pl.BlockSpec(x.shape, lambda i: (0,) * x.ndim)
    return pl.pallas_call(
        momentum_kernel,
        grid=(steps,),
        in_specs=[
            *specs(0), *specs(1), *specs(2), *specs(3), *specs(None),
            *[whole(x) for x in (*fluid_edges, *solid_edges)],
        ],
        out_specs=[
            pl.BlockSpec((3, SLAB, count, width), lambda i: (0, i, 0, 0)),
            pl.BlockSpec((8, width), lambda i: (0, 0)),
            pl.BlockSpec((8, width), lambda i: (0, 0)),
        ],
        out_shape=[
            jax.ShapeDtypeStruct((3, height, count, width), f32),
            jax.ShapeDtypeStruct((8, width), f32),
            jax.ShapeDtypeStruct((8, width), f32),
        ],
        scratch_shapes=[pltpu.VMEM((SLAB + 2, count + 16, width), f32)] * 5,
        compiler_params=params(),
        name="momentum",
    )(*[state] * 12, shear, shear, shear, *fluid_edges, *solid_edges)


def product(x, high_ref, low_ref):
    high, low = split(x)
    y = jnp.dot(high, high_ref[...], preferred_element_type=f32)
    y = y + jnp.dot(low, high_ref[...], preferred_element_type=f32)
    return y + jnp.dot(high, low_ref[...], preferred_element_type=f32)


def modes_kernel(*refs):
    slabs, (high_ref, low_ref, ratio_ref, x_ref, all_ref, ends_ref, power) = refs[:-7], refs[-7:]
    step = pl.program_id(0)
    tile, levels, width = slabs[0].shape

    @pl.when(step == 0)
    def _():
        ends_ref[...] = jnp.zeros_like(ends_ref)
        power[...] = jnp.ones_like(power)

    lines = jnp.concatenate([slab[...].reshape(tile * levels, width) for slab in slabs], axis=1)
    y = product(lines, high_ref, low_ref)
    x_ref[...] = y.reshape(x_ref.shape)
    ratio = ratio_ref[...]

    def scan(a, carry):
        forward, backward, weight = carry
        x = x_ref[a]
        return x + ratio * forward, backward + weight * x, weight * ratio

    forward, backward, weight = lax.fori_loop(
        0, tile, scan, (ends_ref[0], ends_ref[1], power[...]), unroll=4
    )
    ends_ref[0] = forward
    ends_ref[1] = backward
    power[...] = weight

    @pl.when(step == pl.num_programs(0) - 1)
    def _():
        for shard in range(all_ref.shape[0]):
            all_ref[shard] = ends_ref[...]


def modes(slabs, high, low, ratio, shards):
    count, levels, width = slabs[0].shape
    tile = min(TILE, count)
    total = high.shape[1]
    whole = lambda x: pl.BlockSpec(x.shape, lambda i: (0,) * x.ndim)
    return pl.pallas_call(
        modes_kernel,
        grid=(count // tile,),
        in_specs=[
            *[pl.BlockSpec((tile, levels, width), lambda i: (i, 0, 0))] * len(slabs),
            whole(high), whole(low), whole(ratio),
        ],
        out_specs=[
            pl.BlockSpec((tile, levels, total), lambda i: (i, 0, 0)),
            pl.BlockSpec((shards, 2, levels, total), lambda i: (0, 0, 0, 0)),
        ],
        out_shape=[
            jax.ShapeDtypeStruct((count, levels, total), f32),
            jax.ShapeDtypeStruct((shards, 2, levels, total), f32),
        ],
        scratch_shapes=[pltpu.VMEM((2, levels, total), f32), pltpu.VMEM((levels, total), f32)],
        compiler_params=params(),
        name="modes",
    )(*slabs, high, low, ratio)


def solve_kernel(
    place_ref, x_ref, ends_ref, ratio_ref, gain_ref, span_ref, high_ref, low_ref, prior_ref,
    *rest,
):
    outs, (all_ref, sum_ref, lines, tail, carry_ref, block) = rest[:-6], rest[-6:]
    step = pl.program_id(0)
    half = pl.num_programs(0) // 2
    shards = ends_ref.shape[0]
    tile, levels, total = x_ref.shape
    width = outs[0].shape[2]
    ratio = ratio_ref[...]

    @pl.when(step == 0)
    def _():
        span = span_ref[...]
        place = place_ref[0]
        weight = jnp.ones_like(span)
        forward = jnp.zeros_like(span)
        backward = jnp.zeros_like(span)
        for j in range(1, shards + 1):
            forward += weight * ends_ref[lax.rem(place - j + shards, shards), 0]
            backward += weight * ends_ref[lax.rem(place + j, shards), 1]
            weight = weight * span
        carry_ref[...] = forward / (1.0 - weight)
        tail[...] = backward / (1.0 - weight)
        sum_ref[...] = jnp.zeros_like(sum_ref)

    @pl.when(step < half)
    def _():
        def scan(a, y):
            y = x_ref[a] + ratio * y
            lines[step * tile + a] = y
            return y

        carry_ref[...] = lax.fori_loop(0, tile, scan, carry_ref[...], unroll=4)

    @pl.when(step == half)
    def _():
        carry_ref[...] = gain_ref[...] * (ratio * carry_ref[...] + tail[...])

    @pl.when(step >= half)
    def _():
        base = (2 * half - 1 - step) * tile

        def scan(j, carry):
            q, dot = carry
            a = tile - 1 - j
            q = ratio * (lines[base + a] + q)
            block[a] = q
            return q, dot + x_ref[a] * q

        zero = jnp.zeros((levels, total), f32)
        q, dot = lax.fori_loop(0, tile, scan, (carry_ref[...], zero), unroll=4)
        carry_ref[...] = q
        sum_ref[...] += dot
        back = product(block[...].reshape(tile * levels, total), high_ref, low_ref)
        for part, out in enumerate(outs):
            out[...] = back[:, part * width : (part + 1) * width].reshape(tile, levels, width)

    @pl.when(step == 2 * half - 1)
    def _():
        dots = fold(sum_ref[...])
        lanes = dots[:, :width]
        for start in range(width, total, width):
            lanes = lanes + dots[:, start : start + width]
        row = lax.broadcasted_iota(jnp.int32, (8, width), 0)
        sums = prior_ref[...] + jnp.where(row == 1, jnp.sum(lanes, axis=0, keepdims=True), 0.0)
        for device in range(all_ref.shape[0]):
            all_ref[device] = sums


def solve(place, x, ends, ratio, gain, span, high, low, prior, parts, copies):
    count, levels, total = x.shape
    tile = min(TILE, count)
    half = count // tile
    width = total // parts
    whole = lambda v: pl.BlockSpec(v.shape, lambda i, s: (0,) * v.ndim)
    back = lambda i: jnp.minimum(2 * half - 1 - i, half - 1)
    return pl.pallas_call(
        solve_kernel,
        grid_spec=pltpu.PrefetchScalarGridSpec(
            num_scalar_prefetch=1,
            grid=(2 * half,),
            in_specs=[
                pl.BlockSpec((tile, levels, total), lambda i, s: (jnp.minimum(i, 2 * half - 1 - i), 0, 0)),
                whole(ends), whole(ratio), whole(gain), whole(span), whole(high), whole(low), whole(prior),
            ],
            out_specs=[
                *[pl.BlockSpec((tile, levels, width), lambda i, s: (back(i), 0, 0))] * parts,
                pl.BlockSpec((copies, 8, width), lambda i, s: (0, 0, 0)),
            ],
            scratch_shapes=[
                pltpu.VMEM((levels, total), f32),
                pltpu.VMEM((count, levels, total), f32),
                pltpu.VMEM((levels, total), f32),
                pltpu.VMEM((levels, total), f32),
                pltpu.VMEM((tile, levels, total), f32),
            ],
        ),
        out_shape=[
            *[jax.ShapeDtypeStruct((count, levels, width), f32)] * parts,
            jax.ShapeDtypeStruct((copies, 8, width), f32),
        ],
        compiler_params=params(),
        name="solve",
    )(place, x, ends, ratio, gain, span, high, low, prior)


def scale_kernel(alpha_ref, in_ref, out_ref):
    out_ref[...] = (alpha_ref[0] * in_ref[...]).astype(bf16)


def scale_rows(alpha, moment):
    _, height, count, width = moment.shape
    return pl.pallas_call(
        scale_kernel,
        grid_spec=pltpu.PrefetchScalarGridSpec(
            num_scalar_prefetch=1,
            grid=(3 * height // 16,),
            in_specs=[pl.BlockSpec((1, 16, count, width), lambda i, s: (i // (height // 16), i % (height // 16), 0, 0))],
            out_specs=pl.BlockSpec((1, 16, count, width), lambda i, s: (i // (height // 16), i % (height // 16), 0, 0)),
        ),
        out_shape=jax.ShapeDtypeStruct((4, height, count, width), bf16),
        compiler_params=params(),
        name="scale_rows",
    )(alpha, moment)


def pressure_kernel(alpha_ref, *refs):
    pieces, (cos_ref, rest_ref, out_ref, rows) = refs[:-4], refs[-4:]
    tile, levels, width = pieces[0].shape
    height = levels * len(pieces)
    alpha = alpha_ref[0]

    def pair(j, carry):
        highs, lows = [], []
        for s in range(2):
            x = jnp.concatenate([piece[2 * j + s] for piece in pieces], axis=0)
            high, low = split(x)
            highs.append(high)
            lows.append(low)
        high = jnp.concatenate(highs, axis=1)
        low = jnp.concatenate(lows, axis=1)
        stacked = jnp.concatenate([high, low, high], axis=0)
        y = alpha * jnp.dot(cos_ref[...], stacked, preferred_element_type=f32)
        for s in range(2):
            rows[pl.ds(2 * j + s, height, stride=tile), :] = y[:, s * width : (s + 1) * width]
        return carry

    lax.fori_loop(0, tile // 2, pair, 0, unroll=4)
    for h in range(height):
        out_ref[0, h] = rows[h * tile : (h + 1) * tile, :].astype(bf16)


def pressure_rows(alpha, planes, cosine, rest):
    count, levels, width = planes[0].shape
    height = levels * len(planes)
    tile = min(TILE, count)
    high, low = split_table(cosine)
    table = jnp.concatenate([high, high, low], axis=1)
    return pl.pallas_call(
        pressure_kernel,
        grid_spec=pltpu.PrefetchScalarGridSpec(
            num_scalar_prefetch=1,
            grid=(count // tile,),
            in_specs=[
                *[pl.BlockSpec((tile, levels, width), lambda i, s: (i, 0, 0))] * len(planes),
                pl.BlockSpec(table.shape, lambda i, s: (0, 0)),
                pl.BlockSpec(memory_space=pl.ANY),
            ],
            out_specs=pl.BlockSpec((1, height, tile, width), lambda i, s: (3, 0, i, 0)),
            scratch_shapes=[pltpu.VMEM((height * tile, width), f32)],
        ),
        out_shape=jax.ShapeDtypeStruct(rest.shape, bf16),
        input_output_aliases={len(planes) + 2: 0},
        compiler_params=params(),
        name="pressure_rows",
    )(alpha, *planes, table, rest)


def cosine_table(extent):
    row_ids = jnp.arange(extent, dtype=f32)[:, None]
    col_ids = jnp.arange(extent, dtype=f32)[None, :]
    scaled = jnp.where(row_ids == 0, math.sqrt(1.0 / extent), math.sqrt(2.0 / extent))
    return scaled * jnp.cos(math.pi * (col_ids + 0.5) * row_ids / extent)


def pairwise(pieces, axis):
    count = lax.axis_size(axis)
    return [pieces[0]] + [
        lax.ppermute(pieces[s], axis, [(i, i ^ s) for i in range(count)]) for s in range(1, count)
    ]


def exchanged(copies, axis):
    return lax.all_to_all(copies, axis, split_axis=0, concat_axis=0, tiled=True)


def fence(*values):
    return lax.optimization_barrier(values)


def step(state, source, shear, permeability, radial_basis, radial_eigen):
    _, height, count, width = state.shape
    parts = lax.axis_size("rad")
    levels = height // parts // CHUNKS
    owner = lax.axis_index("rad") ^ jnp.arange(parts, dtype=jnp.int32)
    cosine = cosine_table(height).reshape(parts, CHUNKS, levels, height)
    cosine = jnp.swapaxes(jnp.take(cosine, owner, axis=0), 0, 1).reshape(height, height)

    cols_a = edges(state, permeability, 1, (0, 3))
    cols_b = edges(state, shear, 0, (1, 2))
    fluid_edges = neighbours(*cols_a)
    solid_edges = neighbours(*cols_b)
    *heights, fluid_rr = fluid(
        state, source, permeability, *fluid_edges, cosine, parts * CHUNKS
    )
    slabs = [pairwise(heights[c * parts : (c + 1) * parts], "rad") for c in range(CHUNKS)]
    basis = jnp.concatenate(pairwise([radial_basis] * parts, "rad"))
    high, low = split_table(basis)
    moment, rr, rz = momentum(state, shear, fluid_edges, solid_edges)
    *own, rr = fence(*[pieces[0] for pieces in slabs], rr)
    slabs = [[piece, *pieces[1:]] for piece, pieces in zip(own, slabs)]

    place = lax.axis_index("az").reshape(1)
    shards = lax.axis_size("az")
    sums = jnp.stack([jnp.sum(fluid_rr + rr, axis=0), jnp.sum(rz, axis=0)])
    sums = jnp.concatenate([sums, jnp.zeros((6, width), f32)])
    planes = []
    for chunk in range(CHUNKS):
        first = (lax.axis_index("rad") * CHUNKS + chunk) * levels
        level = (first + jnp.arange(levels, dtype=jnp.int32)).astype(f32)
        height_eigen = 4.0 * jnp.sin(math.pi * level / (2.0 * height)) ** 2
        center = storage + radial_eigen[None, :] + height_eigen[:, None]
        root = jnp.sqrt(center * (center + 4.0))
        ratio = 2.0 / (center + 2.0 + root)
        span = lax.integer_pow(ratio, count)
        x, ends = modes(slabs[chunk], high, low, ratio, shards)
        ends = exchanged(ends, "az")
        last = chunk == CHUNKS - 1
        copies = shards * parts if last else 1
        *back, sums = solve(
            place, x, ends, ratio, 1.0 / root, span, high.T, low.T, sums, parts, copies
        )
        if last:
            sums = exchanged(sums, ("az", "rad"))
        else:
            sums = sums[0]
        planes += pairwise(back, "rad")
    totals = jnp.sum(sums, axis=(0, 2))
    alpha = (totals[0] / totals[1]).reshape(1)
    out = scale_rows(alpha, moment)
    return pressure_rows(alpha, planes, cosine.T, out)


def solution(mesh):
    placed = (
        P(None, None, "az", "rad"),
        P(None, "az", "rad"),
        P(None, "az", "rad"),
        P(None, "az", "rad"),
        P("rad", None),
        P(),
    )
    return jax.shard_map(
        step, mesh=mesh, in_specs=placed, out_specs=P(None, None, "az", "rad"), check_vma=False
    )
```

time: 1570 us -> 382 us (0.24)
  other arithmetic: 554 us -> 4.35 us
  local copies, waits for them, and re-layouts: 411 us -> 7.22 us
  matrix products: 215 us -> 0 us
  Pallas kernels: 0 us -> 181 us
  waiting for transfers between devices: 288 us -> 139 us
  blocking collectives: 41.7 us -> 0 us
  starting transfers between devices: 29.4 us -> 46.8 us
    dot_general x16 -> x0, matrix products: 215 us -> none  [contract(): jnp.einsum(form, left, right, precision=lax.Precision.HIGHEST, preferred_...]
    another operation x3 -> x0, other arithmetic: 205 us -> none  [stencil(): return (jnp.stack(parts), diagonal)]
    all_to_all x4 -> x3, waiting for transfers between devices: 280 us -> 83.7 us  [exchanged(): return lax.all_to_all(copies, axis, split_axis=0, concat_axis=0, tiled=True)]
    pallas_call x0 -> x10, Pallas kernels: none -> 181 us  [the longest x1 46.5 us: momentum(): pl.pallas_call(momentum_kernel, grid=(steps,), in_specs=[*specs(0), *spec...]
    add x3 -> x1, other arithmetic: 121 us -> 0.01 us  [step(): center = storage + radial_eigen[None, :] + height_eigen[:, None]]
    slice x3 -> x1, local copies, waits for them, and re-layouts: 89.6 us -> 0.59 us  [step(): alpha = (totals[0] / totals[1]).reshape(1)]
    convert_element_type x2 -> x3, other arithmetic: 81.6 us -> 0.15 us  [split_table(): return (rounded.astype(bf16), (x - rounded).astype(bf16))]
    all_to_all x6 -> x0, local copies, waits for them, and re-layouts: 61.6 us -> none  [the longest x2 22.6 us: precondition(): lax.all_to_all(heights, 'rad', split_axis=0, concat_axis=2, tiled=True)]
  transfers between devices with their start and end apart: 9 -> 26, of which waited for: 4 -> 6; matrix products, arithmetic and copies ran while one was open for 23% -> 2% of each run, Pallas kernels for 0% -> 28%
where the time goes in v1:
time: 382 us; the launch traced here: 380 us
  Pallas kernels  181 us (47%)
  waiting for transfers between devices  139 us (36%)
  starting transfers between devices  46.8 us (12%)
  local copies, waits for them, and re-layouts  7.22 us (2%)
  other arithmetic  4.35 us (1%)
    all_to_all x3, waiting for transfers between devices, exchanged(): return lax.all_to_all(copies, axis, split_axis=0, concat_axis=0, tiled=True)  83.7 us
    pallas_call x1, Pallas kernels, momentum(): pl.pallas_call(momentum_kernel, grid=(steps,), in_specs=[*specs(0), *spec...  46.5 us
    ppermute x15, waiting for transfers between devices, pairwise(): lax.ppermute(pieces[s], axis, [(i, i ^ s) for i in range(count)])  44.3 us
    pallas_call x1, Pallas kernels, fluid(): pl.pallas_call(fluid_kernel, grid=(steps + count // tile,), in_specs=[*sp...  38.2 us
    pallas_call x2, Pallas kernels, solve(): pl.pallas_call(solve_kernel, grid_spec=pltpu.PrefetchScalarGridSpec(num_s...  28.1 us
    pallas_call x2, Pallas kernels, modes(): pl.pallas_call(modes_kernel, grid=(count // tile,), in_specs=[*[pl.BlockS...  19.8 us
    pallas_call x2, Pallas kernels, edges(): pl.pallas_call(edges_kernel, grid=(height // SLAB,), in_specs=[pl.BlockSp...  18.6 us
    all_to_all x3, starting transfers between devices, exchanged(): return lax.all_to_all(copies, axis, split_axis=0, concat_axis=0, tiled=True)  18.2 us
  transfers between devices with their start and end apart: 26, of which 6 were waited for; matrix products, arithmetic and copies ran while one was open for 2% of the time, Pallas kernels for 28%

profile of v1, /device:TPU:0, one launch (start us, length us, event | category | flops | bytes accessed | tf_op | source)
XLA Modules:
  0.0 380.0 jit_solution(2826451285249362482)
XLA Ops:
  0.0 9.3 %edges.3 = (bf16[3,256,128]{2,1,0:T(8,128)(2,1)}, f32[3,64,128]{2,1,0:T(8,128)}, f32[3,64,128]{2,1,0:T(8,128)}) custom-call(bf16[4,64,256,128]{3,2,1,0:T(8,128)(2,1)} %refs_11_.1, bf16[4,64,256,128]{3,2,1,0:T(8,128)(2,1)} %refs_11_.1, bf16[4,64,256,128]{3,2,1,0:T(8,128)(2,1)} %refs_11_.1, bf16[4,64,256,128]{3,2,1,0:T(8,128)(2,1)} %refs_11_.1, ...), custom_call_target="tpu_custom_call" | custom-call | tf_op jit(solution)/shard_map/edges/pallas_call | solution.py:93
  9.3 2.4 collective-permute-start.5
  11.7 1.3 collective-permute-start.4
  13.0 9.3 %edges.2 = (bf16[3,256,128]{2,1,0:T(8,128)(2,1)}, f32[3,64,128]{2,1,0:T(8,128)}, f32[3,64,128]{2,1,0:T(8,128)}) custom-call(bf16[4,64,256,128]{3,2,1,0:T(8,128)(2,1)} %refs_11_.1, bf16[4,64,256,128]{3,2,1,0:T(8,128)(2,1)} %refs_11_.1, bf16[4,64,256,128]{3,2,1,0:T(8,128)(2,1)} %refs_11_.1, bf16[4,64,256,128]{3,2,1,0:T(8,128)(2,1)} %refs_11_.1, ...), custom_call_target="tpu_custom_call" | custom-call | tf_op jit(solution)/shard_map/edges/pallas_call | solution.py:93
  22.3 5.1 %collective-permute-start.1 = (bf16[3,256,128]{2,1,0:T(8,128)(2,1)}, bf16[3,256,128]{2,1,0:T(8,128)(2,1)S(1)}, u32[]{:S(2)}, u32[]{:S(2)}) collective-permute-start(bf16[3,256,128]{2,1,0:T(8,128)(2,1)} %get-tuple-element.40), channel_id=1, source_target_pairs={{0,1},{1,2},{2,3},{4,5},{5,6},{6,7},{8,9},{9,10},{10,11},{12,13},{... | collective-permute-start | bytes 589832 | tf_op jit(solution)/shard_map/ppermute | solution.py:119
  27.5 1.3 collective-permute-start
  28.8 1.5 collective-permute-start.2
  30.6 0.6 gather_fusion
  31.3 0.7 pad_maximum_fusion.1.cos_ref
  32.0 3.2 collective-permute-start.3
  35.2 0.8 fusion.1
  36.0 0.4 collective-permute-done.2.before_ref.refs_16_
  36.4 2.7 collective-permute-done.3.after_ref.refs_17_
  39.1 0.6 copy-done.10
  39.8 38.2 %fluid.1 = (f32[256,8,128]{2,1,0:T(8,128)}, f32[256,8,128]{2,1,0:T(8,128)}, f32[256,8,128]{2,1,0:T(8,128)}, f32[256,8,128]{2,1,0:T(8,128)}, f32[256,8,128]{2,1,0...) custom-call(bf16[4,64,256,128]{3,2,1,0:T(8,128)(2,1)} %refs_11_.1, ...), custom_call_target="tpu_custom_call" | custom-call | tf_op jit(solution)/shard_map/fluid/pallas_call | solution.py:255
  78.4 2.5 collective-permute-start.13
  80.9 1.5 collective-permute-start.6
  82.4 1.1 collective-permute-start.16
  83.5 5.4 %collective-permute-done.6.refs_19_ = f32[3,64,128]{2,1,0:T(8,128)S(1)} collective-permute-done((f32[3,64,128]{2,1,0:T(8,128)S(1)}, f32[3,64,128]{2,1,0:T(8,128)S(1)}, u32[]{:S(2)}, u32[]{:S(2)}) %collective-permute-start.6) | collective-permute-done | bytes 98336 | tf_op jit(solution)/shard_map/ppermute | solution.py:120
  88.9 1.7 collective-permute-start.7
  90.6 2.9 collective-permute-done.7.refs_20_
  93.5 0.4 collective-permute-start.12
  94.0 44.3 %collective-permute-done.12 = f32[128,512]{0,1:T(8,128)S(1)} collective-permute-done((f32[128,512]{0,1:T(8,128)S(1)}, f32[128,512]{0,1:T(8,128)S(1)}, u32[]{:S(2)}, u32[]{:S(2)}) %collective-permute-start.12) | collective-permute-done | bytes 262176 | tf_op jit(solution)/shard_map/ppermute | solution.py:638
  138.3 1.6 collective-permute-start.9
  140.2 0.8 multiply_multiply_fusion
  141.0 46.5 %momentum.1 = (f32[3,64,256,128]{3,2,1,0:T(8,128)}, f32[8,128]{1,0:T(8,128)}, f32[8,128]{1,0:T(8,128)}) custom-call(bf16[4,64,256,128]{3,2,1,0:T(8,128)(2,1)} %refs_11_.1, bf16[4,64,256,128]{3,2,1,0:T(8,128)(2,1)} %refs_11_.1, bf16[4,64,256,128]{3,2,1,0:T(8,128)(2,1)} %refs_11_.1, bf16[4,64,256,128]{3,2,1,0:T(8,128)(2,1)} %refs_11_.1, ...), custom_call_target="tpu_custom_call" | custom-call | tf_op jit(solution)/shard_map/momentum/pallas_call | solution.py:359
  187.7 1.2 copy.23.refs_5_
  188.9 1.0 copy.22.refs_4_
  189.9 1.0 copy-done.3
  190.9 9.9 %modes.3 = (f32[256,8,512]{2,1,0:T(8,128)}, f32[8,2,8,512]{3,2,1,0:T(8,128)}) custom-call(f32[256,8,128]{2,1,0:T(8,128)} %get-tuple-element.55.refs_0_, f32[256,8,128]{2,1,0:T(8,128)} %copy-done.2, f32[256,8,128]{2,1,0:T(8,128)} %copy-done.3, f32[256,8,128]{2,1,0:T(8,128)} %collective-permute-done.16.refs_3_, bf16[512,512]{1,0:T(8,128)(2,1)} %copy.22.refs_4_, ...), custom_call_target="tpu_custom_call" | custom-call | tf_op jit(solution)/shard_map/modes/pallas_call | solution.py:427
  200.8 6.3 %all-to-all-start.1 = ((f32[8,2,8,512]{3,2,1,0:T(8,128)}), f32[8,2,8,512]{3,2,1,0:T(8,128)S(1)}, u32[]{:S(2)}, u32[]{:S(2)}) async-start(f32[8,2,8,512]{3,2,1,0:T(8,128)} %get-tuple-element.60), calls=%async_computation.1 | async-start | bytes 524288 | tf_op jit(solution)/shard_map/all_to_all | solution.py:643
  207.1 9.9 %modes.2 = (f32[256,8,512]{2,1,0:T(8,128)}, f32[8,2,8,512]{3,2,1,0:T(8,128)}) custom-call(f32[256,8,128]{2,1,0:T(8,128)} %get-tuple-element.49.refs_0_, f32[256,8,128]{2,1,0:T(8,128)} %collective-permute-done.8.refs_1_, f32[256,8,128]{2,1,0:T(8,128)} %collective-permute-done.9.refs_2_, f32[256,8,128]{2,1,0:T(8,128)} %collective-permute-done.10.refs_3_, ...), custom_call_target="tpu_custom_call" | custom-call | tf_op jit(solution)/shard_map/modes/pallas_call | solution.py:427
  217.0 6.0 %all-to-all-start = ((f32[8,2,8,512]{3,2,1,0:T(8,128)}), f32[8,2,8,512]{3,2,1,0:T(8,128)S(1)}, u32[]{:S(2)}, u32[]{:S(2)}) async-start(f32[8,2,8,512]{3,2,1,0:T(8,128)} %get-tuple-element.54), calls=%async_computation | async-start | bytes 524288 | tf_op jit(solution)/shard_map/all_to_all | solution.py:643
  223.2 0.7 maximum_maximum_fusion.prior_ref
  223.8 14.1 %solve.2 = (f32[256,8,128]{2,1,0:T(8,128)}, f32[256,8,128]{2,1,0:T(8,128)}, f32[256,8,128]{2,1,0:T(8,128)}, f32[256,8,128]{2,1,0:T(8,128)}, f32[1,8,128]{2,1,0:T(8,128)}) custom-call(s32[1]{0:T(128)} %bitcast.place_ref, f32[256,8,512]{2,1,0:T(8,128)} %get-tuple-element.59.x_ref, f32[8,2,8,512]{3,2,1,0:T(8,128)} %copy-done.7, ...), custom_call_target="tpu_custom_call" | custom-call | tf_op jit(solution)/shard_map/solve/pallas_call | solution.py:526
  237.9 0.7 copy-done.8
  238.6 14.1 %solve.3 = (f32[256,8,128]{2,1,0:T(8,128)}, f32[256,8,128]{2,1,0:T(8,128)}, f32[256,8,128]{2,1,0:T(8,128)}, f32[256,8,128]{2,1,0:T(8,128)}, f32[32,8,128]{2,1,0:T(8,128)}) custom-call(s32[1]{0:T(128)} %bitcast.place_ref, f32[256,8,512]{2,1,0:T(8,128)} %get-tuple-element.53.x_ref, f32[8,2,8,512]{3,2,1,0:T(8,128)} %copy-done.8, ...), custom_call_target="tpu_custom_call" | custom-call | tf_op jit(solution)/shard_map/solve/pallas_call | solution.py:526
  252.8 1.7 collective-permute-start.21
  254.6 0.4 collective-permute-start.17
  255.0 1.6 collective-permute-start.18
  256.6 0.4 collective-permute-start.19
  257.1 5.9 %all-to-all-start.2 = ((f32[32,8,128]{2,1,0:T(8,128)}), f32[32,8,128]{2,1,0:T(8,128)S(1)}, u32[]{:S(2)}, u32[]{:S(2)}) async-start(f32[32,8,128]{2,1,0:T(8,128)} %get-tuple-element.65), calls=%async_computation.2 | async-start | bytes 262144 | tf_op jit(solution)/shard_map/all_to_all | solution.py:643
  263.0 0.7 pad_maximum_fusion.2.refs_8_
  263.7 83.7 %all-to-all-done.2 = f32[32,8,128]{2,1,0:T(8,128)S(1)} async-done(((f32[32,8,128]{2,1,0:T(8,128)}), f32[32,8,128]{2,1,0:T(8,128)S(1)}, u32[]{:S(2)}, u32[]{:S(2)}) %all-to-all-start.2) | async-done | bytes 131104 | tf_op jit(solution)/shard_map/all_to_all | solution.py:643
  347.5 0.6 fusion.14
  349.4 16.2 %scale_rows.1.refs_9_ = bf16[4,64,256,128]{3,2,1,0:T(8,128)(2,1)} custom-call(f32[1]{0:T(128)S(6)} %div.39.alpha_ref, f32[3,64,256,128]{3,2,1,0:T(8,128)} %get-tuple-element.74.in_ref), custom_call_target="tpu_custom_call" | custom-call | tf_op jit(solution)/shard_map/scale_rows/pallas_call | solution.py:562
  365.6 0.9 copy-done.5
  366.9 13.2 %pressure_rows.1 = bf16[4,64,256,128]{3,2,1,0:T(8,128)(2,1)} custom-call(f32[1]{0:T(128)S(6)} %div.39.alpha_ref, f32[256,8,128]{2,1,0:T(8,128)} %get-tuple-element.66.refs_0_, f32[256,8,128]{2,1,0:T(8,128)} %collective-permute-done.17.refs_1_, f32[256,8,128]{2,1,0:T(8,128)} %collective-permute-done.18.refs_2_, ...), custom_call_target="tpu_custom_call", output_to_operand_aliasing={{}: (10, {})} | custom-call | tf_op jit(solution)/shard_map/pressure_rows/pallas_call | solution.py:608
  (85 shorter events, 2.2 us)
Async XLA Ops:
  9.3 22.7 %collective-permute-start.5 = (bf16[3,256,128]{2,1,0:T(8,128)(2,1)}, bf16[3,256,128]{2,1,0:T(8,128)(2,1)S(1)}, u32[]{:S(2)}, u32[]{:S(2)}) collective-permute-start(bf16[3,256,128]{2,1,0:T(8,128)(2,1)} %get-tuple-element.45), channel_id=1, source_target_pairs={{0,1},{1,2},{2,3},{4,5},{5,6},{6,7},{8,9},{9,10},{10,11},{12,13},{... | collective-permute-start | bytes 589832 | tf_op jit(solution)/shard_map/ppermute | solution.py:119
  11.7 23.5 %collective-permute-start.4 = (bf16[3,256,128]{2,1,0:T(8,128)(2,1)}, bf16[3,256,128]{2,1,0:T(8,128)(2,1)S(1)}, u32[]{:S(2)}, u32[]{:S(2)}) collective-permute-start(bf16[3,256,128]{2,1,0:T(8,128)(2,1)} %get-tuple-element.45), channel_id=1, source_target_pairs={{1,0},{2,1},{3,2},{5,4},{6,5},{7,6},{9,8},{10,9},{11,10},{13,12},{... | collective-permute-start | bytes 589832 | tf_op jit(solution)/shard_map/ppermute | solution.py:118
  22.3 12.9 %collective-permute-start.1 = (bf16[3,256,128]{2,1,0:T(8,128)(2,1)}, bf16[3,256,128]{2,1,0:T(8,128)(2,1)S(1)}, u32[]{:S(2)}, u32[]{:S(2)}) collective-permute-start(bf16[3,256,128]{2,1,0:T(8,128)(2,1)} %get-tuple-element.40), channel_id=1, source_target_pairs={{0,1},{1,2},{2,3},{4,5},{5,6},{6,7},{8,9},{9,10},{10,11},{12,13},{... | collective-permute-start | bytes 589832 | tf_op jit(solution)/shard_map/ppermute | solution.py:119
  27.5 7.7 %collective-permute-start = (bf16[3,256,128]{2,1,0:T(8,128)(2,1)}, bf16[3,256,128]{2,1,0:T(8,128)(2,1)S(1)}, u32[]{:S(2)}, u32[]{:S(2)}) collective-permute-start(bf16[3,256,128]{2,1,0:T(8,128)(2,1)} %get-tuple-element.40), channel_id=1, source_target_pairs={{1,0},{2,1},{3,2},{5,4},{6,5},{7,6},{9,8},{10,9},{11,10},{13,12},{... | collective-permute-start | bytes 589832 | tf_op jit(solution)/shard_map/ppermute | solution.py:118
  28.8 7.6 %collective-permute-start.2 = (f32[3,64,128]{2,1,0:T(8,128)}, f32[3,64,128]{2,1,0:T(8,128)S(1)}, u32[]{:S(2)}, u32[]{:S(2)}) collective-permute-start(f32[3,64,128]{2,1,0:T(8,128)} %get-tuple-element.41), channel_id=1, source_target_pairs={{0,4},{4,8},{8,12},{12,16},{16,20},{20,24},{24,28},{28,0},{1,5},{5... | collective-permute-start | bytes 294920 | tf_op jit(solution)/shard_map/ppermute | solution.py:120
  32.0 7.1 %collective-permute-start.3 = (f32[3,64,128]{2,1,0:T(8,128)}, f32[3,64,128]{2,1,0:T(8,128)S(1)}, u32[]{:S(2)}, u32[]{:S(2)}) collective-permute-start(f32[3,64,128]{2,1,0:T(8,128)} %get-tuple-element.42), channel_id=1, source_target_pairs={{4,0},{8,4},{12,8},{16,12},{20,16},{24,20},{28,24},{0,28},{5,1},{9... | collective-permute-start | bytes 294920 | tf_op jit(solution)/shard_map/ppermute | solution.py:121
  36.4 2.7 copy-start.9
  39.1 0.6 copy-start.10
  39.7 38.5 %copy-start.11 = (f32[128,512]{1,0:T(8,128)S(1)}, f32[128,512]{1,0:T(8,128)}, u32[]{:S(2)}) copy-start(f32[128,512]{1,0:T(8,128)} %param.10) | copy-start | bytes 786436
  39.7 41.2 %copy-start.19 = (f32[3,64,128]{2,1,0:T(8,128)S(1)}, f32[3,64,128]{2,1,0:T(8,128)}, u32[]{:S(2)}) copy-start(f32[3,64,128]{2,1,0:T(8,128)} %get-tuple-element.46) | copy-start | bytes 294916
  39.7 49.1 %copy-start.18 = (f32[3,64,128]{2,1,0:T(8,128)S(1)}, f32[3,64,128]{2,1,0:T(8,128)}, u32[]{:S(2)}) copy-start(f32[3,64,128]{2,1,0:T(8,128)} %get-tuple-element.47) | copy-start | bytes 294916
  39.7 100.4 %copy-start.17 = (f32[512]{0:T(512)S(1)}, f32[512]{0:T(512)}, u32[]{:S(2)}) copy-start(f32[512]{0:T(512)} %param.11) | copy-start | bytes 6148
  77.9 62.1 %collective-permute-start.14 = (f32[256,8,128]{2,1,0:T(8,128)}, f32[256,8,128]{2,1,0:T(8,128)S(1)}, u32[]{:S(2)}, u32[]{:S(2)}) collective-permute-start(f32[256,8,128]{2,1,0:T(8,128)} %get-tuple-element.56), channel_id=1, source_target_pairs={{0,1},{1,0},{2,3},{3,2},{4,5},{5,4},{6,7},{7,6},{8,9},{9,8},{10,11... | collective-permute-start | bytes 3145736 | tf_op jit(solution)/shard_map/ppermute | solution.py:638
  78.4 15.6 %collective-permute-start.13 = (f32[128,512]{0,1:T(8,128)S(1)}, f32[128,512]{0,1:T(8,128)S(1)}, u32[]{:S(2)}, u32[]{:S(2)}) collective-permute-start(f32[128,512]{0,1:T(8,128)S(1)} %copy.21), channel_id=1, source_target_pairs={{0,3},{1,2},{2,1},{3,0},{4,7},{5,6},{6,5},{7,4},{8,11},{9,10},{10,... | collective-permute-start | bytes 786440 | tf_op jit(solution)/shard_map/ppermute | solution.py:638
  80.9 8.0 %collective-permute-start.6 = (f32[3,64,128]{2,1,0:T(8,128)S(1)}, f32[3,64,128]{2,1,0:T(8,128)S(1)}, u32[]{:S(2)}, u32[]{:S(2)}) collective-permute-start(f32[3,64,128]{2,1,0:T(8,128)S(1)} %copy-done.19), channel_id=1, source_target_pairs={{0,4},{4,8},{8,12},{12,16},{16,20},{20,24},{24,28},{28,0},{1,5},{5... | collective-permute-start | bytes 294920 | tf_op jit(solution)/shard_map/ppermute | solution.py:120
  82.4 107.5 %collective-permute-start.15 = (f32[256,8,128]{2,1,0:T(8,128)}, f32[256,8,128]{2,1,0:T(8,128)S(1)}, u32[]{:S(2)}, u32[]{:S(2)}) collective-permute-start(f32[256,8,128]{2,1,0:T(8,128)} %get-tuple-element.57), channel_id=1, source_target_pairs={{0,2},{1,3},{2,0},{3,1},{4,6},{5,7},{6,4},{7,5},{8,10},{9,11},{10,... | collective-permute-start | bytes 3145736 | tf_op jit(solution)/shard_map/ppermute | solution.py:638
  82.4 107.5 %collective-permute-start.16 = (f32[256,8,128]{2,1,0:T(8,128)}, f32[256,8,128]{2,1,0:T(8,128)}, u32[]{:S(2)}, u32[]{:S(2)}) collective-permute-start(f32[256,8,128]{2,1,0:T(8,128)} %get-tuple-element.58), channel_id=1, source_target_pairs={{0,3},{1,2},{2,1},{3,0},{4,7},{5,6},{6,5},{7,4},{8,11},{9,10},{10,... | collective-permute-start | bytes 3145736 | tf_op jit(solution)/shard_map/ppermute | solution.py:638
  88.9 52.1 %copy-start.12 = (f32[3,64,128]{2,1,0:T(8,128)}, f32[3,64,128]{2,1,0:T(8,128)S(1)}, u32[]{:S(2)}) copy-start(f32[3,64,128]{2,1,0:T(8,128)S(1)} %collective-permute-done.6.refs_19_) | copy-start | bytes 294916
  88.9 4.6 %collective-permute-start.7 = (f32[3,64,128]{2,1,0:T(8,128)S(1)}, f32[3,64,128]{2,1,0:T(8,128)S(1)}, u32[]{:S(2)}, u32[]{:S(2)}) collective-permute-start(f32[3,64,128]{2,1,0:T(8,128)S(1)} %copy-done.18), channel_id=1, source_target_pairs={{4,0},{8,4},{12,8},{16,12},{20,16},{24,20},{28,24},{0,28},{5,1},{9... | collective-permute-start | bytes 294920 | tf_op jit(solution)/shard_map/ppermute | solution.py:121
  93.5 47.5 %copy-start.13 = (f32[3,64,128]{2,1,0:T(8,128)}, f32[3,64,128]{2,1,0:T(8,128)S(1)}, u32[]{:S(2)}) copy-start(f32[3,64,128]{2,1,0:T(8,128)S(1)} %collective-permute-done.7.refs_20_) | copy-start | bytes 294916
  93.5 44.8 %collective-permute-start.12 = (f32[128,512]{0,1:T(8,128)S(1)}, f32[128,512]{0,1:T(8,128)S(1)}, u32[]{:S(2)}, u32[]{:S(2)}) collective-permute-start(f32[128,512]{0,1:T(8,128)S(1)} %copy.21), channel_id=1, source_target_pairs={{0,2},{1,3},{2,0},{3,1},{4,6},{5,7},{6,4},{7,5},{8,10},{9,11},{10,... | collective-permute-start | bytes 786440 | tf_op jit(solution)/shard_map/ppermute | solution.py:638
  93.9 44.4 %collective-permute-start.11 = (f32[128,512]{0,1:T(8,128)S(1)}, f32[128,512]{0,1:T(8,128)S(1)}, u32[]{:S(2)}, u32[]{:S(2)}) collective-permute-start(f32[128,512]{0,1:T(8,128)S(1)} %copy.21), channel_id=1, source_target_pairs={{0,1},{1,0},{2,3},{3,2},{4,5},{5,4},{6,7},{7,6},{8,9},{9,8},{10,11... | collective-permute-start | bytes 786440 | tf_op jit(solution)/shard_map/ppermute | solution.py:638
  138.3 68.8 %collective-permute-start.8 = (f32[256,8,128]{2,1,0:T(8,128)}, f32[256,8,128]{2,1,0:T(8,128)}, u32[]{:S(2)}, u32[]{:S(2)}) collective-permute-start(f32[256,8,128]{2,1,0:T(8,128)} %get-tuple-element.50), channel_id=1, source_target_pairs={{0,1},{1,0},{2,3},{3,2},{4,5},{5,4},{6,7},{7,6},{8,9},{9,8},{10,11... | collective-permute-start | bytes 3145736 | tf_op jit(solution)/shard_map/ppermute | solution.py:638
  138.3 68.8 %collective-permute-start.9 = (f32[256,8,128]{2,1,0:T(8,128)}, f32[256,8,128]{2,1,0:T(8,128)}, u32[]{:S(2)}, u32[]{:S(2)}) collective-permute-start(f32[256,8,128]{2,1,0:T(8,128)} %get-tuple-element.51), channel_id=1, source_target_pairs={{0,2},{1,3},{2,0},{3,1},{4,6},{5,7},{6,4},{7,5},{8,10},{9,11},{10,... | collective-permute-start | bytes 3145736 | tf_op jit(solution)/shard_map/ppermute | solution.py:638
  140.0 47.6 %copy-start.2 = (f32[256,8,128]{2,1,0:T(8,128)}, f32[256,8,128]{2,1,0:T(8,128)S(1)}, u32[]{:S(2)}) copy-start(f32[256,8,128]{2,1,0:T(8,128)S(1)} %collective-permute-done.14.refs_1_) | copy-start | bytes 3145732
  140.0 67.1 %collective-permute-start.10 = (f32[256,8,128]{2,1,0:T(8,128)}, f32[256,8,128]{2,1,0:T(8,128)}, u32[]{:S(2)}, u32[]{:S(2)}) collective-permute-start(f32[256,8,128]{2,1,0:T(8,128)} %get-tuple-element.52), channel_id=1, source_target_pairs={{0,3},{1,2},{2,1},{3,0},{4,7},{5,6},{6,5},{7,4},{8,11},{9,10},{10,... | collective-permute-start | bytes 3145736 | tf_op jit(solution)/shard_map/ppermute | solution.py:638
  187.7 29.3 %copy-start = (bf16[512,512]{0,1:T(8,128)(2,1)}, bf16[512,512]{0,1:T(8,128)(2,1)S(1)}, u32[]{:S(2)}) copy-start(bf16[512,512]{0,1:T(8,128)(2,1)S(1)} %get-tuple-element.75) | copy-start | bytes 1572868
  187.7 29.3 %copy-start.1 = (bf16[512,512]{0,1:T(8,128)(2,1)}, bf16[512,512]{0,1:T(8,128)(2,1)S(1)}, u32[]{:S(2)}) copy-start(bf16[512,512]{0,1:T(8,128)(2,1)S(1)} %get-tuple-element.76) | copy-start | bytes 1572868
  189.9 1.0 copy-start.3
  200.8 22.3 %copy-start.14 = (f32[8,128]{1,0:T(8,128)S(1)}, f32[8,128]{1,0:T(8,128)}, u32[]{:S(2)}) copy-start(f32[8,128]{1,0:T(8,128)} %get-tuple-element.63) | copy-start | bytes 12292
  200.8 22.3 %copy-start.15 = (f32[8,128]{1,0:T(8,128)S(1)}, f32[8,128]{1,0:T(8,128)}, u32[]{:S(2)}) copy-start(f32[8,128]{1,0:T(8,128)} %get-tuple-element.61) | copy-start | bytes 12292
  200.8 22.3 %copy-start.16 = (f32[8,128]{1,0:T(8,128)S(1)}, f32[8,128]{1,0:T(8,128)}, u32[]{:S(2)}) copy-start(f32[8,128]{1,0:T(8,128)} %get-tuple-element.62) | copy-start | bytes 12292
  200.8 16.2 %all-to-all-start.1 = ((f32[8,2,8,512]{3,2,1,0:T(8,128)}), f32[8,2,8,512]{3,2,1,0:T(8,128)S(1)}, u32[]{:S(2)}, u32[]{:S(2)}) async-start(f32[8,2,8,512]{3,2,1,0:T(8,128)} %get-tuple-element.60), calls=%async_computation.1 | async-start | bytes 524288 | tf_op jit(solution)/shard_map/all_to_all | solution.py:643
  217.0 6.8 %copy-start.7 = (f32[8,2,8,512]{3,2,1,0:T(8,128)}, f32[8,2,8,512]{3,2,1,0:T(8,128)S(1)}, u32[]{:S(2)}) copy-start(f32[8,2,8,512]{3,2,1,0:T(8,128)S(1)} %all-to-all-done.1.ends_ref) | copy-start | bytes 786436
  217.0 20.9 %all-to-all-start = ((f32[8,2,8,512]{3,2,1,0:T(8,128)}), f32[8,2,8,512]{3,2,1,0:T(8,128)S(1)}, u32[]{:S(2)}, u32[]{:S(2)}) async-start(f32[8,2,8,512]{3,2,1,0:T(8,128)} %get-tuple-element.54), calls=%async_computation | async-start | bytes 524288 | tf_op jit(solution)/shard_map/all_to_all | solution.py:643
  237.9 0.7 copy-start.8
  252.7 3.9 %collective-permute-start.20 = (f32[256,8,128]{2,1,0:T(8,128)}, f32[256,8,128]{2,1,0:T(8,128)S(1)}, u32[]{:S(2)}, u32[]{:S(2)}) collective-permute-start(f32[256,8,128]{2,1,0:T(8,128)} %get-tuple-element.71), channel_id=1, source_target_pairs={{0,1},{1,0},{2,3},{3,2},{4,5},{5,4},{6,7},{7,6},{8,9},{9,8},{10,11... | collective-permute-start | bytes 3145736 | tf_op jit(solution)/shard_map/ppermute | solution.py:638
  252.8 112.8 %collective-permute-start.21 = (f32[256,8,128]{2,1,0:T(8,128)}, f32[256,8,128]{2,1,0:T(8,128)S(1)}, u32[]{:S(2)}, u32[]{:S(2)}) collective-permute-start(f32[256,8,128]{2,1,0:T(8,128)} %get-tuple-element.72), channel_id=1, source_target_pairs={{0,2},{1,3},{2,0},{3,1},{4,6},{5,7},{6,4},{7,5},{8,10},{9,11},{10,... | collective-permute-start | bytes 3145736 | tf_op jit(solution)/shard_map/ppermute | solution.py:638
  254.4 111.1 %collective-permute-start.22 = (f32[256,8,128]{2,1,0:T(8,128)}, f32[256,8,128]{2,1,0:T(8,128)S(1)}, u32[]{:S(2)}, u32[]{:S(2)}) collective-permute-start(f32[256,8,128]{2,1,0:T(8,128)} %get-tuple-element.73), channel_id=1, source_target_pairs={{0,3},{1,2},{2,1},{3,0},{4,7},{5,6},{6,5},{7,4},{8,11},{9,10},{10,... | collective-permute-start | bytes 3145736 | tf_op jit(solution)/shard_map/ppermute | solution.py:638
  254.6 111.0 %collective-permute-start.17 = (f32[256,8,128]{2,1,0:T(8,128)}, f32[256,8,128]{2,1,0:T(8,128)}, u32[]{:S(2)}, u32[]{:S(2)}) collective-permute-start(f32[256,8,128]{2,1,0:T(8,128)} %get-tuple-element.67), channel_id=1, source_target_pairs={{0,1},{1,0},{2,3},{3,2},{4,5},{5,4},{6,7},{7,6},{8,9},{9,8},{10,11... | collective-permute-start | bytes 3145736 | tf_op jit(solution)/shard_map/ppermute | solution.py:638
  255.0 110.6 %collective-permute-start.18 = (f32[256,8,128]{2,1,0:T(8,128)}, f32[256,8,128]{2,1,0:T(8,128)}, u32[]{:S(2)}, u32[]{:S(2)}) collective-permute-start(f32[256,8,128]{2,1,0:T(8,128)} %get-tuple-element.68), channel_id=1, source_target_pairs={{0,2},{1,3},{2,0},{3,1},{4,6},{5,7},{6,4},{7,5},{8,10},{9,11},{10,... | collective-permute-start | bytes 3145736 | tf_op jit(solution)/shard_map/ppermute | solution.py:638
  256.6 109.0 %copy-start.4 = (f32[256,8,128]{2,1,0:T(8,128)}, f32[256,8,128]{2,1,0:T(8,128)S(1)}, u32[]{:S(2)}) copy-start(f32[256,8,128]{2,1,0:T(8,128)S(1)} %collective-permute-done.20.refs_5_) | copy-start | bytes 3145732
  256.6 109.0 %collective-permute-start.19 = (f32[256,8,128]{2,1,0:T(8,128)}, f32[256,8,128]{2,1,0:T(8,128)}, u32[]{:S(2)}, u32[]{:S(2)}) collective-permute-start(f32[256,8,128]{2,1,0:T(8,128)} %get-tuple-element.69), channel_id=1, source_target_pairs={{0,3},{1,2},{2,1},{3,0},{4,7},{5,6},{6,5},{7,4},{8,11},{9,10},{10,... | collective-permute-start | bytes 3145736 | tf_op jit(solution)/shard_map/ppermute | solution.py:638
  257.1 90.3 %all-to-all-start.2 = ((f32[32,8,128]{2,1,0:T(8,128)}), f32[32,8,128]{2,1,0:T(8,128)S(1)}, u32[]{:S(2)}, u32[]{:S(2)}) async-start(f32[32,8,128]{2,1,0:T(8,128)} %get-tuple-element.65), calls=%async_computation.2 | async-start | bytes 262144 | tf_op jit(solution)/shard_map/all_to_all | solution.py:643
  365.6 1.0 copy-start.5
  365.6 1.3 copy-start.6

commit v2 on v1

v2 whole, which is shorter than its diff:
```python
import functools
import math

import jax
import jax.numpy as jnp
from jax import lax
from jax.experimental import pallas as pl
from jax.experimental.pallas import tpu as pltpu
from jax.sharding import PartitionSpec as P


biot_coupling = 2.0
storage = 1.0

f32 = jnp.float32
bf16 = jnp.bfloat16


SLAB = 8
EDGE = 16
ROWS = 32
TILE = 64
HALVES = 2
CHUNKS = 2


def params(limit=56):
    return pltpu.CompilerParams(
        dimension_semantics=("arbitrary",), vmem_limit_bytes=limit * 1024 * 1024
    )


def lanes_of(shape):
    return lax.broadcasted_iota(jnp.int32, shape, len(shape) - 1)


def split(x):
    high = x.astype(bf16)
    low = (x - high.astype(f32)).astype(bf16)
    return high, low


def fold(x):
    total = x[0:8]
    for start in range(8, x.shape[0], 8):
        total = total + x[start : start + 8]
    return total


def split_table(x):
    rounded = lax.reduce_precision(x, exponent_bits=8, mantissa_bits=7)
    return rounded.astype(bf16), (x - rounded).astype(bf16)


def edges_kernel(state_ref, shear_ref, perm_ref, cols_ref, *rest):
    *row_refs, acc = rest
    step = pl.program_id(0)
    slab, count, width = shear_ref.shape
    rows = min(64, count // 2)
    places = (0, count // 2 - 1, count // 2, count - 1)
    lane = lanes_of((rows, width))
    for c in range(6):
        src = state_ref.at[c] if c < 4 else (shear_ref, perm_ref)[c - 4]
        for start in range(0, count, rows):
            value = acc[c, start : start + rows, :]
            for i in range(slab):
                h = step * slab + i
                x = src[i, start : start + rows, :].astype(f32)
                value = jnp.where((lane >> 1) == h, pltpu.roll(x, 2 * h + 1, 1), value)
                for place, row_ref in zip(places, row_refs):
                    if start <= place < start + rows:
                        row_ref[c, pl.ds(h, 1), :] = x[place - start : place - start + 1]
            acc[c, start : start + rows, :] = value

    @pl.when(step == pl.num_programs(0) - 1)
    def _():
        for c in range(6):
            for start in range(0, count, rows):
                v = acc[c, start : start + rows, :]
                swapped = jnp.where(lane % 2 == 0, pltpu.roll(v, width - 1, 1), pltpu.roll(v, 1, 1))
                cols_ref[c, start : start + rows, :] = swapped.astype(bf16)


def edges(state, shear, perm):
    _, height, count, width = state.shape
    whole = lambda *shape: pl.BlockSpec(shape, lambda i: (0,) * len(shape))
    return pl.pallas_call(
        edges_kernel,
        grid=(height // EDGE,),
        in_specs=[
            pl.BlockSpec((4, EDGE, count, width), lambda i: (0, i, 0, 0)),
            pl.BlockSpec((EDGE, count, width), lambda i: (i, 0, 0)),
            pl.BlockSpec((EDGE, count, width), lambda i: (i, 0, 0)),
        ],
        out_specs=[whole(6, count, width), *[whole(6, height, width)] * 4],
        out_shape=[
            jax.ShapeDtypeStruct((6, count, width), bf16),
            *[jax.ShapeDtypeStruct((6, height, width), f32)] * 4,
        ],
        scratch_shapes=[pltpu.VMEM((6, count, width), f32)],
        compiler_params=params(),
        name="edges",
    )(state, shear, perm)


def neighbours(cols, first, low, high, last):
    n_rad = lax.axis_size("rad")
    n_az = lax.axis_size("az")
    from_right = lax.ppermute(cols, "rad", [(i + 1, i) for i in range(n_rad - 1)])
    from_left = lax.ppermute(cols, "rad", [(i, i + 1) for i in range(n_rad - 1)])
    before = lax.ppermute(last, "az", [(i, (i + 1) % n_az) for i in range(n_az)])
    after = lax.ppermute(first, "az", [((i + 1) % n_az, i) for i in range(n_az)])
    beside = jnp.where(lanes_of(cols.shape) % 2 == 0, from_right, from_left)
    return beside, before, after, low, high


def stage(scratch, center, above, below, before, after, step, steps, slab, count):
    top = jnp.where(step > 0, 1.0, 0.0)
    bottom = jnp.where(step < steps - 1, 1.0, 0.0)
    scratch[0, 8 : 8 + count, :] = above[...].astype(f32) * top
    scratch[slab + 1, 8 : 8 + count, :] = below[...].astype(f32) * bottom
    for i in range(slab):
        scratch[i + 1, 8 : 8 + count, :] = center[i].astype(f32)
        if before is not None:
            h = step * slab + i
            scratch[i + 1, 7:8, :] = before[pl.ds(h, 1), :]
            scratch[i + 1, 8 + count : 9 + count, :] = after[pl.ds(h, 1), :]


def radial_pair(x, beside, shift, lane):
    width = x.shape[1]
    beside = pltpu.roll(beside, shift, 1)
    right = jnp.where(lane == width - 1, beside, pltpu.roll(x, width - 1, 1))
    left = jnp.where(lane == 0, beside, pltpu.roll(x, 1, 1))
    return right.astype(f32), left.astype(f32)


def weighted(center, faces, around):
    total = faces[1][0] * around[0]
    for face, other in zip(faces[1][1:], around[1:]):
        total = total + face * other
    return faces[0] * center - total


def total_of(values):
    total = values[0]
    for value in values[1:]:
        total = total + value
    return total


def fluid_kernel(
    shared, p_ref, p_up, p_dn, k_ref, k_up, k_dn, z_ref, z_up, z_dn, r_ref, t_ref, src_ref,
    beside_ref, before_ref, after_ref, cos_ref,
    *rest,
):
    outs, (sum_ref, ps, ks, zs, ts, res) = rest[shared:-6], rest[-6:]
    step = pl.program_id(0)
    slab, count, width = src_ref.shape
    height = before_ref.shape[1]
    steps = height // slab
    tile, levels, _ = outs[0].shape

    @pl.when(step == 0)
    def _():
        sum_ref[...] = jnp.zeros_like(sum_ref)

    @pl.when(step < steps)
    def _():
        stage(ps, p_ref.at[0], p_up.at[0, 0], p_dn.at[0, 0], before_ref.at[3], after_ref.at[3], step, steps, slab, count)
        stage(ks, k_ref, k_up.at[0], k_dn.at[0], before_ref.at[5], after_ref.at[5], step, steps, slab, count)
        stage(zs, z_ref.at[0], z_up.at[0, 0], z_dn.at[0, 0], None, None, step, steps, slab, count)
        for i in range(slab):
            h = step * slab + i
            ts[i, 8 : 8 + count, :] = t_ref[0, i].astype(f32)
            ts[i, 7:8, :] = before_ref[1, pl.ds(h, 1), :]
            ts[i, 8 + count : 9 + count, :] = after_ref[1, pl.ds(h, 1), :]
        lane = lanes_of((ROWS, width))

        def plane(i, total):
            h = step * slab + i
            shift = 2 * height - 1 - 2 * h
            for a in range(0, count, ROWS):
                at = slice(8 + a, 8 + a + ROWS)
                prev = slice(7 + a, 7 + a + ROWS)
                nxt = slice(9 + a, 9 + a + ROWS)
                own = slice(a, a + ROWS)
                p = ps[i + 1, at, :]
                k = ks[i + 1, at, :]
                p_r, p_l = radial_pair(p_ref[0, i, own, :], beside_ref[3, own, :], shift, lane)
                k_r, k_l = radial_pair(k_ref[i, own, :], beside_ref[5, own, :], shift, lane)
                others = [ks[i + 1, nxt, :], ks[i + 1, prev, :], ks[i + 2, at, :], ks[i, at, :]]
                faces = [k + other for other in (k_r, k_l, *others)]
                around = [ps[i + 1, nxt, :], ps[i + 1, prev, :], ps[i + 2, at, :], ps[i, at, :]]
                flux = weighted(p, (total_of(faces), faces), (p_r, p_l, *around))
                u_r, u_l = radial_pair(r_ref[0, i, own, :], beside_ref[0, own, :], shift, lane)
                spread = (u_r - u_l) + (ts[i, nxt, :] - ts[i, prev, :])
                spread += zs[i + 2, at, :] - zs[i, at, :]
                if biot_coupling != 2.0:
                    spread = (0.5 * biot_coupling) * spread
                value = (src_ref[i, own, :].astype(f32) + spread) + (storage * p + 0.5 * flux)
                res[h, own, :] = value
                total = total + fold(value * value)
            return total

        sum_ref[...] += lax.fori_loop(0, slab, plane, jnp.zeros((8, width), f32))

    @pl.when(step >= steps)
    def _():
        base = (step - steps) * tile

        def group(j, carry):
            start = pl.multiple_of(base + 8 * j, 8)
            columns = [
                jnp.swapaxes(res[h : h + 8, pl.ds(start, 8), :], 0, 1) for h in range(0, height, 8)
            ]
            for pair in range(4):
                highs, lows = [], []
                for s in range(2):
                    x = jnp.concatenate([column[2 * pair + s] for column in columns], axis=0)
                    high, low = split(x)
                    highs.append(high)
                    lows.append(low)
                high = jnp.concatenate(highs, axis=1)
                low = jnp.concatenate(lows, axis=1)
                stacked = jnp.concatenate([high, low, high], axis=0)
                y = jnp.dot(cos_ref[...], stacked, preferred_element_type=f32)
                for s in range(2):
                    for block, out in enumerate(outs):
                        out[8 * j + 2 * pair + s, :, :] = y[
                            block * levels : (block + 1) * levels, s * width : (s + 1) * width
                        ]
            return carry

        lax.fori_loop(0, tile // 8, group, 0)


def plane_specs(channel, slab, steps, count, width, base=0, part=0):
    at = lambda i: jnp.minimum(i + base, steps - 1)
    up = lambda i: jnp.maximum(at(i) * slab - 1, 0)
    down = lambda i: jnp.minimum(at(i) * slab + slab, steps * slab - 1)
    if channel is None:
        return [
            pl.BlockSpec((slab, count, width), lambda i: (at(i), part, 0)),
            pl.BlockSpec((1, count, width), lambda i: (up(i), part, 0)),
            pl.BlockSpec((1, count, width), lambda i: (down(i), part, 0)),
        ]
    return [
        pl.BlockSpec((1, slab, count, width), lambda i: (channel, at(i), part, 0)),
        pl.BlockSpec((1, 1, count, width), lambda i: (channel, up(i), part, 0)),
        pl.BlockSpec((1, 1, count, width), lambda i: (channel, down(i), part, 0)),
    ]


def fluid(state, source, perm, beside, before, after, table, parts, half, shared):
    _, height, whole_count, width = state.shape
    count = whole_count // HALVES
    steps = height // SLAB
    tile = min(TILE, count)
    pieces = parts * CHUNKS
    levels = height // pieces
    specs = lambda c: plane_specs(c, SLAB, steps, count, width, part=half)
    whole = lambda x: pl.BlockSpec(x.shape, lambda i: (0,) * x.ndim)
    at = lambda first: pl.BlockSpec(
        (tile, levels, width), lambda i: (first + jnp.maximum(i - steps, 0), 0, 0)
    )
    rest = pieces - parts
    return pl.pallas_call(
        functools.partial(fluid_kernel, len(shared)),
        grid=(steps + count // tile,),
        in_specs=[
            *specs(3), *specs(None), *specs(2), specs(0)[0], specs(1)[0], specs(None)[0],
            pl.BlockSpec((6, count, width), lambda i: (0, half, 0)), whole(before), whole(after), whole(table),
            *[pl.BlockSpec(memory_space=pl.ANY)] * len(shared),
        ],
        out_specs=[
            *[at(0)] * parts, *[at(half * (count // tile))] * rest,
            pl.BlockSpec((8, width), lambda i: (0, 0)),
        ],
        out_shape=[
            *[jax.ShapeDtypeStruct((count, levels, width), f32)] * parts,
            *[jax.ShapeDtypeStruct((whole_count, levels, width), f32)] * rest,
            jax.ShapeDtypeStruct((8, width), f32),
        ],
        scratch_shapes=[
            pltpu.VMEM((SLAB + 2, count + 16, width), f32),
            pltpu.VMEM((SLAB + 2, count + 16, width), f32),
            pltpu.VMEM((SLAB + 2, count + 16, width), f32),
            pltpu.VMEM((SLAB, count + 16, width), f32),
            pltpu.VMEM((height, count, width), f32),
        ],
        input_output_aliases={16 + i: pieces - len(shared) + i for i in range(len(shared))},
        compiler_params=params(),
        name="fluid",
    )(state, state, state, perm, perm, perm, state, state, state, state, state, source,
      beside, before, after, table, *shared)


def momentum_kernel(base, steps, priors, *refs):
    fields = [refs[3 * c : 3 * c + 3] for c in range(5)]
    beside_ref, before_ref, after_ref = refs[15:18]
    prior_refs = refs[18 : 18 + priors]
    *_, out_ref, rr_ref, rz_ref = refs[:-5]
    scratch = refs[-5:]
    step = pl.program_id(0) + base
    _, slab, count, width = out_ref.shape
    height = before_ref.shape[1]

    @pl.when(step == base)
    def _():
        rr_ref[...] = total_of([prior[...] for prior in prior_refs[::2]])
        rz_ref[...] = total_of([prior[...] for prior in prior_refs[1::2]])

    for c in range(5):
        center, up, down = fields[c]
        if c < 4:
            center, up, down = center.at[0], up.at[0, 0], down.at[0, 0]
        else:
            up, down = up.at[0], down.at[0]
        stage(scratch[c], center, up, down, before_ref.at[c], after_ref.at[c], step, steps, slab, count)
    lane = lanes_of((ROWS, width))

    def plane(i, totals):
        rr, rz = totals
        h = step * slab + i
        shift = 2 * height - 1 - 2 * h
        for a in range(0, count, ROWS):
            at = slice(8 + a, 8 + a + ROWS)
            prev = slice(7 + a, 7 + a + ROWS)
            nxt = slice(9 + a, 9 + a + ROWS)
            own = slice(a, a + ROWS)

            def around(c):
                s = scratch[c]
                center = fields[c][0].at[0] if c < 4 else fields[c][0]
                right, left = radial_pair(center[i, own, :], beside_ref[c, own, :], shift, lane)
                others = [s[i + 1, nxt, :], s[i + 1, prev, :], s[i + 2, at, :], s[i, at, :]]
                return s[i + 1, at, :], (right, left, *others)

            g, g_around = around(4)
            faces = [g + other for other in g_around]
            diagonal = total_of(faces)
            inverse = -1.0 / diagonal
            _, p = around(3)
            squares = None
            for c in range(3):
                u, u_around = around(c)
                value = weighted(u, (diagonal, faces), u_around)
                value = value + biot_coupling * (p[2 * c] - p[2 * c + 1])
                out_ref[c, i, own, :] = value * inverse
                squares = value * value if squares is None else squares + value * value
            rr = rr + fold(squares)
            rz = rz + fold(squares * inverse)
        return rr, rz

    zero = jnp.zeros((8, width), f32)
    rr, rz = lax.fori_loop(0, slab, plane, (zero, zero))
    rr_ref[...] += 0.25 * rr
    rz_ref[...] -= 0.5 * rz


def momentum(state, shear, beside, before, after, piece, prior, rows=None):
    _, height, count, width = state.shape
    steps = height // SLAB
    base, end = ((eighth * steps) // 8 for eighth in piece)
    specs = lambda c: plane_specs(c, SLAB, steps, count, width, base=base)
    whole = lambda x: pl.BlockSpec(x.shape, lambda i: (0,) * x.ndim)
    operands = [*[state] * 12, shear, shear, shear, beside, before, after, *prior]
    in_specs = [
        *specs(0), *specs(1), *specs(2), *specs(3), *specs(None),
        *[whole(x) for x in operands[15:]],
    ]
    aliases = {}
    if rows is not None:
        aliases = {len(operands): 0}
        operands.append(rows)
        in_specs.append(pl.BlockSpec(memory_space=pl.ANY))
    return pl.pallas_call(
        functools.partial(momentum_kernel, base, steps, len(prior)),
        grid=(end - base,),
        in_specs=in_specs,
        out_specs=[
            pl.BlockSpec((3, SLAB, count, width), lambda i: (0, i + base, 0, 0)),
            pl.BlockSpec((8, width), lambda i: (0, 0)),
            pl.BlockSpec((8, width), lambda i: (0, 0)),
        ],
        out_shape=[
            jax.ShapeDtypeStruct((3, height, count, width), f32),
            jax.ShapeDtypeStruct((8, width), f32),
            jax.ShapeDtypeStruct((8, width), f32),
        ],
        scratch_shapes=[pltpu.VMEM((SLAB + 2, count + 16, width), f32)] * 5,
        input_output_aliases=aliases,
        compiler_params=params(),
        name="momentum",
    )(*operands)


def product(x, high_ref, low_ref):
    high, low = split(x)
    y = jnp.dot(high, high_ref[...], preferred_element_type=f32)
    y = y + jnp.dot(low, high_ref[...], preferred_element_type=f32)
    return y + jnp.dot(high, low_ref[...], preferred_element_type=f32)


def modes_kernel(groups, *refs):
    slabs, (high_ref, low_ref, ratio_ref, x_ref, all_ref, ends_ref, power) = refs[:-7], refs[-7:]
    step = pl.program_id(0)
    tile, levels, width = slabs[0].shape

    @pl.when(step == 0)
    def _():
        ends_ref[...] = jnp.zeros_like(ends_ref)
        power[...] = jnp.ones_like(power)

    each = len(slabs) // groups
    span = pl.num_programs(0) // groups
    for half in range(groups):

        @pl.when((step >= half * span) & (step < (half + 1) * span))
        def _():
            mine = slabs[half * each : (half + 1) * each]
            lines = jnp.concatenate([slab[...].reshape(tile * levels, width) for slab in mine], axis=1)
            x_ref[...] = product(lines, high_ref, low_ref).reshape(x_ref.shape)

    ratio = ratio_ref[...]

    def scan(a, carry):
        forward, backward, weight = carry
        x = x_ref[a]
        return x + ratio * forward, backward + weight * x, weight * ratio

    forward, backward, weight = lax.fori_loop(
        0, tile, scan, (ends_ref[0], ends_ref[1], power[...]), unroll=4
    )
    ends_ref[0] = forward
    ends_ref[1] = backward
    power[...] = weight

    @pl.when(step == pl.num_programs(0) - 1)
    def _():
        for shard in range(all_ref.shape[0]):
            all_ref[shard] = ends_ref[...]


def modes(groups, high, low, ratio, shards):
    slabs = sum(groups, [])
    span, levels, width = slabs[0].shape
    count = span * len(groups)
    tile = min(TILE, span)
    total = high.shape[1]
    steps = span // tile
    at = lambda half: pl.BlockSpec(
        (tile, levels, width), lambda i: (jnp.clip(i - half * steps, 0, steps - 1), 0, 0)
    )
    whole = lambda x: pl.BlockSpec(x.shape, lambda i: (0,) * x.ndim)
    return pl.pallas_call(
        functools.partial(modes_kernel, len(groups)),
        grid=(count // tile,),
        in_specs=[
            *[at(half) for half, group in enumerate(groups) for _ in group],
            whole(high), whole(low), whole(ratio),
        ],
        out_specs=[
            pl.BlockSpec((tile, levels, total), lambda i: (i, 0, 0)),
            pl.BlockSpec((shards, 2, levels, total), lambda i: (0, 0, 0, 0)),
        ],
        out_shape=[
            jax.ShapeDtypeStruct((count, levels, total), f32),
            jax.ShapeDtypeStruct((shards, 2, levels, total), f32),
        ],
        scratch_shapes=[pltpu.VMEM((2, levels, total), f32), pltpu.VMEM((levels, total), f32)],
        compiler_params=params(),
        name="modes",
    )(*slabs, high, low, ratio)


def solve_kernel(
    last, place_ref, x_ref, ends_ref, ratio_ref, gain_ref, span_ref, high_ref, low_ref,
    rr_ref, rz_ref, prior_ref, *rest,
):
    outs, (all_ref, sum_ref, lines, tail, carry_ref, block) = rest[:-6], rest[-6:]
    step = pl.program_id(0)
    half = pl.num_programs(0) // 2
    shards = ends_ref.shape[0]
    tile, levels, total = x_ref.shape
    width = outs[0].shape[2]
    ratio = ratio_ref[...]

    @pl.when(step == 0)
    def _():
        span = span_ref[...]
        place = place_ref[0]
        weight = jnp.ones_like(span)
        forward = jnp.zeros_like(span)
        backward = jnp.zeros_like(span)
        for j in range(1, shards + 1):
            forward += weight * ends_ref[lax.rem(place - j + shards, shards), 0]
            backward += weight * ends_ref[lax.rem(place + j, shards), 1]
            weight = weight * span
        carry_ref[...] = forward / (1.0 - weight)
        tail[...] = backward / (1.0 - weight)
        sum_ref[...] = jnp.zeros_like(sum_ref)

    @pl.when(step < half)
    def _():
        def scan(a, y):
            y = x_ref[a] + ratio * y
            lines[step * tile + a] = y
            return y

        carry_ref[...] = lax.fori_loop(0, tile, scan, carry_ref[...], unroll=4)

    @pl.when(step == half)
    def _():
        carry_ref[...] = gain_ref[...] * (ratio * carry_ref[...] + tail[...])

    @pl.when(step >= half)
    def _():
        base = (2 * half - 1 - step) * tile

        def scan(j, carry):
            q, dot = carry
            a = tile - 1 - j
            q = ratio * (lines[base + a] + q)
            block[a] = q
            return q, dot + x_ref[a] * q

        zero = jnp.zeros((levels, total), f32)
        q, dot = lax.fori_loop(0, tile, scan, (carry_ref[...], zero), unroll=4)
        carry_ref[...] = q
        sum_ref[...] += dot
        back = product(block[...].reshape(tile * levels, total), high_ref, low_ref)
        for part, out in enumerate(outs):
            out[...] = back[:, part * width : (part + 1) * width].reshape(tile, levels, width)

    @pl.when(step == 2 * half - 1)
    def _():
        dots = fold(sum_ref[...])
        lanes = dots[:, :width]
        for start in range(width, total, width):
            lanes = lanes + dots[:, start : start + width]
        sums = lanes + prior_ref[...]
        if last:
            row = lax.broadcasted_iota(jnp.int32, (8, width), 0)
            rr = jnp.sum(rr_ref[...], axis=0, keepdims=True)
            rz = jnp.sum(rz_ref[...] + sums, axis=0, keepdims=True)
            sums = jnp.where(row == 0, rr, jnp.where(row == 1, rz, 0.0))
        for device in range(all_ref.shape[0]):
            all_ref[device] = sums


def solve(place, x, ends, ratio, gain, span, high, low, rr, rz, prior, parts, copies, last):
    count, levels, total = x.shape
    tile = min(TILE, count)
    half = count // tile
    width = total // parts
    whole = lambda v: pl.BlockSpec(v.shape, lambda i, s: (0,) * v.ndim)
    back = lambda i: jnp.minimum(2 * half - 1 - i, half - 1)
    return pl.pallas_call(
        functools.partial(solve_kernel, last),
        grid_spec=pltpu.PrefetchScalarGridSpec(
            num_scalar_prefetch=1,
            grid=(2 * half,),
            in_specs=[
                pl.BlockSpec((tile, levels, total), lambda i, s: (jnp.minimum(i, 2 * half - 1 - i), 0, 0)),
                whole(ends), whole(ratio), whole(gain), whole(span), whole(high), whole(low), whole(rr), whole(rz), whole(prior),
            ],
            out_specs=[
                *[pl.BlockSpec((tile, levels, width), lambda i, s: (back(i), 0, 0))] * parts,
                pl.BlockSpec((copies, 8, width), lambda i, s: (0, 0, 0)),
            ],
            scratch_shapes=[
                pltpu.VMEM((levels, total), f32),
                pltpu.VMEM((count, levels, total), f32),
                pltpu.VMEM((levels, total), f32),
                pltpu.VMEM((levels, total), f32),
                pltpu.VMEM((tile, levels, total), f32),
            ],
        ),
        out_shape=[
            *[jax.ShapeDtypeStruct((count, levels, width), f32)] * parts,
            jax.ShapeDtypeStruct((copies, 8, width), f32),
        ],
        compiler_params=params(),
        name="solve",
    )(place, x, ends, ratio, gain, span, high, low, rr, rz, prior)


def scale_kernel(alpha_ref, in_ref, out_ref):
    out_ref[...] = (alpha_ref[0] * in_ref[...]).astype(bf16)


def scale_rows(alpha, moment):
    _, height, count, width = moment.shape
    return pl.pallas_call(
        scale_kernel,
        grid_spec=pltpu.PrefetchScalarGridSpec(
            num_scalar_prefetch=1,
            grid=(3 * height // 16,),
            in_specs=[pl.BlockSpec((1, 16, count, width), lambda i, s: (i // (height // 16), i % (height // 16), 0, 0))],
            out_specs=pl.BlockSpec((1, 16, count, width), lambda i, s: (i // (height // 16), i % (height // 16), 0, 0)),
        ),
        out_shape=jax.ShapeDtypeStruct((4, height, count, width), bf16),
        compiler_params=params(),
        name="scale_rows",
    )(alpha, moment)


def pressure_kernel(alpha_ref, *refs):
    pieces, (cos_ref, rest_ref, out_ref) = refs[:-3], refs[-3:]
    tile, levels, width = pieces[0].shape
    height = levels * len(pieces)
    alpha = alpha_ref[0]

    def group(j, carry):
        planes = []
        for pair in range(8):
            highs, lows = [], []
            for s in range(2):
                a = 16 * j + 2 * pair + s
                x = jnp.concatenate([piece[a] for piece in pieces], axis=0)
                high, low = split(x)
                highs.append(high)
                lows.append(low)
            high = jnp.concatenate(highs, axis=1)
            low = jnp.concatenate(lows, axis=1)
            stacked = jnp.concatenate([high, low, high], axis=0)
            y = alpha * jnp.dot(cos_ref[...], stacked, preferred_element_type=f32)
            planes += [y[:, :width], y[:, width:]]
        start = pl.multiple_of(16 * j, 16)
        for h in range(0, height, 8):
            low = jnp.swapaxes(jnp.stack([y[h : h + 8] for y in planes[:8]]), 0, 1)
            high = jnp.swapaxes(jnp.stack([y[h : h + 8] for y in planes[8:]]), 0, 1)
            block = jnp.concatenate([low, high], axis=1)
            out_ref[0, h : h + 8, pl.ds(start, 16), :] = block.astype(bf16)
        return carry

    lax.fori_loop(0, tile // 16, group, 0)


def pressure_rows(alpha, planes, cosine, rest):
    count, levels, width = planes[0].shape
    height = levels * len(planes)
    tile = min(TILE, count)
    high, low = split_table(cosine)
    table = jnp.concatenate([high, high, low], axis=1)
    return pl.pallas_call(
        pressure_kernel,
        grid_spec=pltpu.PrefetchScalarGridSpec(
            num_scalar_prefetch=1,
            grid=(count // tile,),
            in_specs=[
                *[pl.BlockSpec((tile, levels, width), lambda i, s: (i, 0, 0))] * len(planes),
                pl.BlockSpec(table.shape, lambda i, s: (0, 0)),
                pl.BlockSpec(memory_space=pl.ANY),
            ],
            out_specs=pl.BlockSpec((1, height, tile, width), lambda i, s: (3, 0, i, 0)),
        ),
        out_shape=jax.ShapeDtypeStruct(rest.shape, bf16),
        input_output_aliases={len(planes) + 2: 0},
        compiler_params=params(),
        name="pressure_rows",
    )(alpha, *planes, table, rest)


def cosine_table(extent):
    row_ids = jnp.arange(extent, dtype=f32)[:, None]
    col_ids = jnp.arange(extent, dtype=f32)[None, :]
    scaled = jnp.where(row_ids == 0, math.sqrt(1.0 / extent), math.sqrt(2.0 / extent))
    return scaled * jnp.cos(math.pi * (col_ids + 0.5) * row_ids / extent)


def pairwise(pieces, axis):
    count = lax.axis_size(axis)
    return [pieces[0]] + [
        lax.ppermute(pieces[s], axis, [(i, i ^ s) for i in range(count)]) for s in range(1, count)
    ]


def exchanged(copies, axis):
    return lax.all_to_all(copies, axis, split_axis=0, concat_axis=0, tiled=True)


def fence(*values):
    return lax.optimization_barrier(values)


def step(state, source, shear, permeability, radial_basis, radial_eigen):
    _, height, count, width = state.shape
    parts = lax.axis_size("rad")
    levels = height // parts // CHUNKS
    owner = lax.axis_index("rad") ^ jnp.arange(parts, dtype=jnp.int32)
    cosine = cosine_table(height).reshape(parts, CHUNKS, levels, height)
    cosine = jnp.swapaxes(jnp.take(cosine, owner, axis=0), 0, 1).reshape(height, height)
    high, low = split_table(cosine)
    table = jnp.concatenate([high, high, low], axis=1)

    cols, first, *others = edges(state, shear, permeability)
    first, radial_basis = fence(first, radial_basis)
    beside, before, after, mid_low, mid_high = neighbours(cols, first, *others)
    blocks = pairwise([radial_basis] * parts, "rad")
    sent, priors, shared = [], [], []
    for half, ends in enumerate(((before, mid_high), (mid_low, after))):
        *heights, fluid_rr = fluid(
            state, source, permeability, beside, *ends, table, parts, half, shared
        )
        shared = heights[parts:]
        sent.append(pairwise(heights[:parts], "rad"))
        priors += [fluid_rr, jnp.zeros_like(fluid_rr)]
    slabs = [sent]
    for chunk in range(1, CHUNKS):
        slabs.append([pairwise(shared[(chunk - 1) * parts : chunk * parts], "rad")])
    high, low = split_table(jnp.concatenate(blocks))
    around = (beside, before, after)
    moment, rr, rz = momentum(state, shear, *around, (0, 2), priors)

    place = lax.axis_index("az").reshape(1)
    shards = lax.axis_size("az")
    sums = jnp.zeros((8, width), f32)
    planes = []
    for chunk in range(CHUNKS):
        first = (lax.axis_index("rad") * CHUNKS + chunk) * levels
        level = (first + jnp.arange(levels, dtype=jnp.int32)).astype(f32)
        height_eigen = 4.0 * jnp.sin(math.pi * level / (2.0 * height)) ** 2
        center = storage + radial_eigen[None, :] + height_eigen[:, None]
        root = jnp.sqrt(center * (center + 4.0))
        ratio = 2.0 / (center + 2.0 + root)
        span = lax.integer_pow(ratio, count)
        x, ends = modes(slabs[chunk], high, low, ratio, shards)
        ends = exchanged(ends, "az")
        piece = ((2, 3), (6, 8))[chunk]
        moment, rr, rz = momentum(state, shear, *around, piece, (rr, rz), moment)
        last = chunk == CHUNKS - 1
        copies = shards * parts if last else 1
        *back, sums = solve(
            place, x, ends, ratio, 1.0 / root, span, high.T, low.T, rr, rz, sums, parts, copies, last
        )
        if last:
            sums = exchanged(sums, ("az", "rad"))
        else:
            sums = sums[0]
            moment, rr, rz = momentum(state, shear, *around, (3, 6), (rr, rz), moment)
        planes += pairwise(back, "rad")
    totals = jnp.sum(sums, axis=(0, 2))
    alpha = (totals[0] / totals[1]).reshape(1)
    out = scale_rows(alpha, moment)
    return pressure_rows(alpha, planes, cosine.T, out)


def solution(mesh):
    placed = (
        P(None, None, "az", "rad"),
        P(None, "az", "rad"),
        P(None, "az", "rad"),
        P(None, "az", "rad"),
        P("rad", None),
        P(),
    )
    return jax.shard_map(
        step, mesh=mesh, in_specs=placed, out_specs=P(None, None, "az", "rad"), check_vma=False
    )
```

time: 382 us -> 336 us (0.88)
  waiting for transfers between devices: 139 us -> 109 us
  Pallas kernels: 181 us -> 168 us
  starting transfers between devices: 46.8 us -> 42.3 us
    ppermute x15 -> x18, waiting for transfers between devices: 44.3 us -> 27.4 us  [pairwise(): lax.ppermute(pieces[s], axis, [(i, i ^ s) for i in range(count)])]
    all_to_all x3, waiting for transfers between devices: 83.7 us -> 72.6 us  [exchanged(): return lax.all_to_all(copies, axis, split_axis=0, concat_axis=0, tiled=True)]
    pallas_call x8 -> x11, Pallas kernels: 151 us -> 143 us  [the longest x4 51.5 us: momentum(): pl.pallas_call(functools.partial(momentum_kernel, base, steps, len(prior)...]
    ppermute x2 -> x1, starting transfers between devices: 7.54 us -> 2.41 us  [neighbours(): lax.ppermute(cols, 'rad', [(i, i + 1) for i in range(n_rad - 1)])]
    pallas_call x1, Pallas kernels: 13.2 us -> 8.61 us  [pressure_rows(): pl.pallas_call(pressure_kernel, grid_spec=pltpu.PrefetchScalarGridSpec(nu...]
    ppermute x15 -> x18, starting transfers between devices: 10.5 us -> 13.5 us  [pairwise(): lax.ppermute(pieces[s], axis, [(i, i ^ s) for i in range(count)])]
  transfers between devices with their start and end apart: 26 -> 25, of which waited for: 6 -> 7; matrix products, arithmetic and copies ran while one was open for 2% -> 2% of each run, Pallas kernels for 28% -> 38%
where the time goes in v2:
time: 336 us; the launch traced here: 335 us
  Pallas kernels  168 us (50%)
  waiting for transfers between devices  109 us (32%)
  starting transfers between devices  42.3 us (13%)
  local copies, waits for them, and re-layouts  10.5 us (3%)
  other arithmetic  3.62 us (1%)
    all_to_all x3, waiting for transfers between devices, exchanged(): return lax.all_to_all(copies, axis, split_axis=0, concat_axis=0, tiled=True)  72.6 us
    pallas_call x4, Pallas kernels, momentum(): pl.pallas_call(functools.partial(momentum_kernel, base, steps, len(prior)...  51.5 us
    pallas_call x2, Pallas kernels, fluid(): pl.pallas_call(functools.partial(fluid_kernel, len(shared)), grid=(steps...  42.1 us
    ppermute x18, waiting for transfers between devices, pairwise(): lax.ppermute(pieces[s], axis, [(i, i ^ s) for i in range(count)])  27.4 us
    pallas_call x2, Pallas kernels, solve(): pl.pallas_call(functools.partial(solve_kernel, last), grid_spec=pltpu.Pre...  20.6 us
    all_to_all x3, starting transfers between devices, exchanged(): return lax.all_to_all(copies, axis, split_axis=0, concat_axis=0, tiled=True)  18.7 us
    pallas_call x2, Pallas kernels, modes(): pl.pallas_call(functools.partial(modes_kernel, len(groups)), grid=(count...  16.4 us
    pallas_call x1, Pallas kernels, scale_rows(): pl.pallas_call(scale_kernel, grid_spec=pltpu.PrefetchScalarGridSpec(num_s...  16.2 us
  transfers between devices with their start and end apart: 25, of which 7 were waited for; matrix products, arithmetic and copies ran while one was open for 2% of the time, Pallas kernels for 38%

profile of v2, /device:TPU:0, one launch (start us, length us, event | category | flops | bytes accessed | tf_op | source)
XLA Modules:
  0.0 335.1 jit_solution(513989713905226974)
XLA Ops:
  0.0 12.3 %edges.1 = (bf16[6,256,128]{2,1,0:T(8,128)(2,1)}, f32[6,64,128]{2,1,0:T(8,128)}, f32[6,64,128]{2,1,0:T(8,128)}, f32[6,64,128]{2,1,0:T(8,128)}, f32[6,64,128]{2,1,0:T(8,128)}) custom-call(bf16[4,64,256,128]{3,2,1,0:T(8,128)(2,1)} %refs_11_.7, bf16[64,256,128]{2,1,0:T(8,128)(2,1)} %refs_14_.7, bf16[64,256,128]{2,1,0:T(8,128)(2,1)} %k_dn.3), custom_call_target="tpu_custom_call" | custom-call | tf_op jit(solution)/shard_map/edges/pallas_call | solution.py:87
  12.3 2.4 collective-permute-start.1
  14.7 1.3 collective-permute-start
  16.0 2.4 collective-permute-start.3
  19.3 0.7 pad_maximum_fusion.1.cos_ref
  20.6 0.9 fusion.1.beside_ref.refs_15_
  21.5 4.1 %collective-permute-done.3.before_ref.refs_16_ = f32[6,64,128]{2,1,0:T(8,128)S(1)} collective-permute-done((f32[6,64,128]{2,1,0:T(8,128)}, f32[6,64,128]{2,1,0:T(8,128)S(1)}, u32[]{:S(2)}, u32[]{:S(2)}) %collective-permute-start.3) | collective-permute-done | bytes 196640 | tf_op jit(solution)/shard_map/ppermute | solution.py:111
  25.6 0.7 copy-done.2
  26.3 21.0 %fluid.2 = (f32[128,8,128]{2,1,0:T(8,128)}, f32[128,8,128]{2,1,0:T(8,128)}, f32[128,8,128]{2,1,0:T(8,128)}, f32[128,8,128]{2,1,0:T(8,128)}, f32[256,8,128]{2,1,0...) custom-call(bf16[4,64,256,128]{3,2,1,0:T(8,128)(2,1)} %refs_11_.7, ...), custom_call_target="tpu_custom_call" | custom-call | tf_op jit(solution)/shard_map/fluid/pallas_call | solution.py:268
  47.3 1.9 collective-permute-start.10
  49.3 2.2 collective-permute-start.9
  51.7 4.1 %collective-permute-start.2 = (f32[6,64,128]{2,1,0:T(8,128)S(1)}, f32[6,64,128]{2,1,0:T(8,128)S(1)}, u32[]{:S(2)}, u32[]{:S(2)}) collective-permute-start(f32[6,64,128]{2,1,0:T(8,128)S(1)} %copy-done.18), channel_id=1, source_target_pairs={{4,0},{8,4},{12,8},{16,12},{20,16},{24,20},{28,24},{0,28},{5,1},{9... | collective-permute-start | bytes 589832 | tf_op jit(solution)/shard_map/ppermute | solution.py:112
  55.8 4.6 %collective-permute-done.2.after_ref.refs_17_ = f32[6,64,128]{2,1,0:T(8,128)S(1)} collective-permute-done((f32[6,64,128]{2,1,0:T(8,128)S(1)}, f32[6,64,128]{2,1,0:T(8,128)S(1)}, u32[]{:S(2)}, u32[]{:S(2)}) %collective-permute-start.2) | collective-permute-done | bytes 196640 | tf_op jit(solution)/shard_map/ppermute | solution.py:112
  61.1 21.1 %fluid.3 = (f32[128,8,128]{2,1,0:T(8,128)}, f32[128,8,128]{2,1,0:T(8,128)}, f32[128,8,128]{2,1,0:T(8,128)}, f32[128,8,128]{2,1,0:T(8,128)}, f32[256,8,128]{2,1,0...) custom-call(bf16[4,64,256,128]{3,2,1,0:T(8,128)(2,1)} %refs_11_.7, ...), custom_call_target="tpu_custom_call", output_to_operand_aliasing={{4}: (16, {}), {5}: (17, {}), {6}: (18, {}), {7}: (19, {})} | custom-call | tf_op jit(solution)/shard_map/fluid/pallas_call | solution.py:268
  82.4 1.3 collective-permute-start.13
  83.8 0.7 collective-permute-start.14
  84.4 0.7 collective-permute-start.15
  85.3 0.7 multiply_multiply_fusion
  86.1 1.2 copy.31.refs_5_.refs_9_
  87.3 1.0 copy.30.refs_4_.refs_8_
  88.3 0.8 copy-done.12
  89.1 0.7 collective-permute-start.4
  89.8 6.9 %collective-permute-done.12.refs_3_ = f32[128,8,128]{2,1,0:T(8,128)S(1)} collective-permute-done((f32[128,8,128]{2,1,0:T(8,128)}, f32[128,8,128]{2,1,0:T(8,128)S(1)}, u32[]{:S(2)}, u32[]{:S(2)}) %collective-permute-start.12) | collective-permute-done | bytes 524320 | tf_op jit(solution)/shard_map/ppermute | solution.py:677
  96.7 0.8 copy-done.13
  97.5 1.3 collective-permute-start.5
  98.9 9.0 %collective-permute-done.14.refs_6_ = f32[128,8,128]{2,1,0:T(8,128)} collective-permute-done((f32[128,8,128]{2,1,0:T(8,128)}, f32[128,8,128]{2,1,0:T(8,128)}, u32[]{:S(2)}, u32[]{:S(2)}) %collective-permute-start.14) | collective-permute-done | bytes 524320 | tf_op jit(solution)/shard_map/ppermute | solution.py:677
  107.9 11.4 %collective-permute-done.15.refs_7_ = f32[128,8,128]{2,1,0:T(8,128)} collective-permute-done((f32[128,8,128]{2,1,0:T(8,128)}, f32[128,8,128]{2,1,0:T(8,128)}, u32[]{:S(2)}, u32[]{:S(2)}) %collective-permute-start.15) | collective-permute-done | bytes 524320 | tf_op jit(solution)/shard_map/ppermute | solution.py:677
  119.3 8.4 %modes.3 = (f32[256,8,512]{2,1,0:T(8,128)}, f32[8,2,8,512]{3,2,1,0:T(8,128)}) custom-call(f32[128,8,128]{2,1,0:T(8,128)} %get-tuple-element.86.refs_0_, f32[128,8,128]{2,1,0:T(8,128)} %copy-done.11, f32[128,8,128]{2,1,0:T(8,128)} %copy-done.12, f32[128,8,128]{2,1,0:T(8,128)} %copy-done.13, f32[128,8,128]{2,1,0:T(8,128)} %get-tuple-element.90.refs_4_, ...), custom_call_target="tpu_custom_call" | custom-call | tf_op jit(solution)/shard_map/modes/pallas_call | solution.py:457
  127.7 6.5 %all-to-all-start.1 = ((f32[8,2,8,512]{3,2,1,0:T(8,128)}), f32[8,2,8,512]{3,2,1,0:T(8,128)S(1)}, u32[]{:S(2)}, u32[]{:S(2)}) async-start(f32[8,2,8,512]{3,2,1,0:T(8,128)} %get-tuple-element.95), calls=%async_computation.1 | async-start | bytes 524288 | tf_op jit(solution)/shard_map/all_to_all | solution.py:682
  134.7 13.4 %momentum.4 = (f32[3,64,256,128]{3,2,1,0:T(8,128)}, f32[8,128]{1,0:T(8,128)}, f32[8,128]{1,0:T(8,128)}) custom-call(bf16[4,64,256,128]{3,2,1,0:T(8,128)(2,1)} %refs_11_.7, bf16[4,64,256,128]{3,2,1,0:T(8,128)(2,1)} %refs_11_.7, bf16[4,64,256,128]{3,2,1,0:T(8,128)(2,1)} %refs_11_.7, bf16[4,64,256,128]{3,2,1,0:T(8,128)(2,1)} %refs_11_.7, ...), custom_call_target="tpu_custom_call" | custom-call | tf_op jit(solution)/shard_map/momentum/pallas_call | solution.py:378
  148.1 8.1 %momentum.5 = (f32[3,64,256,128]{3,2,1,0:T(8,128)}, f32[8,128]{1,0:T(8,128)}, f32[8,128]{1,0:T(8,128)}) custom-call(bf16[4,64,256,128]{3,2,1,0:T(8,128)(2,1)} %refs_11_.7, bf16[4,64,256,128]{3,2,1,0:T(8,128)(2,1)} %refs_11_.7, bf16[4,64,256,128]{3,2,1,0:T(8,128)(2,1)} %refs_11_.7, ...), custom_call_target="tpu_custom_call", output_to_operand_aliasing={{0}: (20, {})} | custom-call | tf_op jit(solution)/shard_map/momentum/pallas_call | solution.py:378
  156.2 0.7 copy-done.10
  156.9 10.3 %solve.2 = (f32[256,8,128]{2,1,0:T(8,128)}, f32[256,8,128]{2,1,0:T(8,128)}, f32[256,8,128]{2,1,0:T(8,128)}, f32[256,8,128]{2,1,0:T(8,128)}, f32[1,8,128]{2,1,0:T(8,128)}) custom-call(s32[1]{0:T(128)} %bitcast.place_ref, f32[256,8,512]{2,1,0:T(8,128)} %get-tuple-element.94.x_ref, f32[8,2,8,512]{3,2,1,0:T(8,128)} %copy-done.10, ...), custom_call_target="tpu_custom_call" | custom-call | tf_op jit(solution)/shard_map/solve/pallas_call | solution.py:560
  167.3 1.0 copy-done.5
  168.6 8.0 %modes.2 = (f32[256,8,512]{2,1,0:T(8,128)}, f32[8,2,8,512]{3,2,1,0:T(8,128)}) custom-call(f32[256,8,128]{2,1,0:T(8,128)} %get-tuple-element.66.refs_0_, f32[256,8,128]{2,1,0:T(8,128)} %copy-done.5, f32[256,8,128]{2,1,0:T(8,128)} %copy-done.8, f32[256,8,128]{2,1,0:T(8,128)} %collective-permute-done.6.refs_3_, bf16[512,512]{1,0:T(8,128)(2,1)} %copy.30.refs_4_.refs_8_, ...), custom_call_target="tpu_custom_call" | custom-call | tf_op jit(solution)/shard_map/modes/pallas_call | solution.py:457
  176.6 6.0 %all-to-all-start = ((f32[8,2,8,512]{3,2,1,0:T(8,128)}), f32[8,2,8,512]{3,2,1,0:T(8,128)S(1)}, u32[]{:S(2)}, u32[]{:S(2)}) async-start(f32[8,2,8,512]{3,2,1,0:T(8,128)} %get-tuple-element.72), calls=%async_computation | async-start | bytes 524288 | tf_op jit(solution)/shard_map/all_to_all | solution.py:682
  182.6 17.2 %momentum.6 = (f32[3,64,256,128]{3,2,1,0:T(8,128)}, f32[8,128]{1,0:T(8,128)}, f32[8,128]{1,0:T(8,128)}) custom-call(bf16[4,64,256,128]{3,2,1,0:T(8,128)(2,1)} %refs_11_.7, bf16[4,64,256,128]{3,2,1,0:T(8,128)(2,1)} %refs_11_.7, bf16[4,64,256,128]{3,2,1,0:T(8,128)(2,1)} %refs_11_.7, ...), custom_call_target="tpu_custom_call", output_to_operand_aliasing={{0}: (20, {})} | custom-call | tf_op jit(solution)/shard_map/momentum/pallas_call | solution.py:378
  199.8 12.8 %momentum.7 = (f32[3,64,256,128]{3,2,1,0:T(8,128)}, f32[8,128]{1,0:T(8,128)}, f32[8,128]{1,0:T(8,128)}) custom-call(bf16[4,64,256,128]{3,2,1,0:T(8,128)(2,1)} %refs_11_.7, bf16[4,64,256,128]{3,2,1,0:T(8,128)(2,1)} %refs_11_.7, bf16[4,64,256,128]{3,2,1,0:T(8,128)(2,1)} %refs_11_.7, ...), custom_call_target="tpu_custom_call", output_to_operand_aliasing={{0}: (20, {})} | custom-call | tf_op jit(solution)/shard_map/momentum/pallas_call | solution.py:378
  212.6 1.4 collective-permute-start.17
  214.2 0.7 copy-done.9
  214.9 10.3 %solve.3 = (f32[256,8,128]{2,1,0:T(8,128)}, f32[256,8,128]{2,1,0:T(8,128)}, f32[256,8,128]{2,1,0:T(8,128)}, f32[256,8,128]{2,1,0:T(8,128)}, f32[32,8,128]{2,1,0:T(8,128)}) custom-call(s32[1]{0:T(128)} %bitcast.place_ref, f32[256,8,512]{2,1,0:T(8,128)} %get-tuple-element.71.x_ref, f32[8,2,8,512]{3,2,1,0:T(8,128)} %copy-done.9, ...), custom_call_target="tpu_custom_call" | custom-call | tf_op jit(solution)/shard_map/solve/pallas_call | solution.py:560
  225.9 1.3 collective-permute-start.20
  227.4 6.2 %all-to-all-start.2 = ((f32[32,8,128]{2,1,0:T(8,128)}), f32[32,8,128]{2,1,0:T(8,128)S(1)}, u32[]{:S(2)}, u32[]{:S(2)}) async-start(f32[32,8,128]{2,1,0:T(8,128)} %get-tuple-element.97), calls=%async_computation.2 | async-start | bytes 262144 | tf_op jit(solution)/shard_map/all_to_all | solution.py:682
  233.6 0.7 pad_maximum_fusion.2.refs_8_
  234.3 72.6 %all-to-all-done.2 = f32[32,8,128]{2,1,0:T(8,128)S(1)} async-done(((f32[32,8,128]{2,1,0:T(8,128)}), f32[32,8,128]{2,1,0:T(8,128)S(1)}, u32[]{:S(2)}, u32[]{:S(2)}) %all-to-all-start.2) | async-done | bytes 131104 | tf_op jit(solution)/shard_map/all_to_all | solution.py:682
  309.0 16.2 %scale_rows.1.refs_9_ = bf16[4,64,256,128]{3,2,1,0:T(8,128)(2,1)} custom-call(f32[1]{0:T(128)S(6)} %div.39.alpha_ref, f32[3,64,256,128]{3,2,1,0:T(8,128)} %get-tuple-element.106.in_ref), custom_call_target="tpu_custom_call" | custom-call | tf_op jit(solution)/shard_map/scale_rows/pallas_call | solution.py:596
  325.2 0.9 copy-done.6
  326.5 8.6 %pressure_rows.1 = bf16[4,64,256,128]{3,2,1,0:T(8,128)(2,1)} custom-call(f32[1]{0:T(128)S(6)} %div.39.alpha_ref, f32[256,8,128]{2,1,0:T(8,128)} %get-tuple-element.98.refs_0_, f32[256,8,128]{2,1,0:T(8,128)} %copy-done.4, f32[256,8,128]{2,1,0:T(8,128)} %copy-done.6, f32[256,8,128]{2,1,0:T(8,128)} %copy-done.7, ...), custom_call_target="tpu_custom_call", output_to_operand_aliasing={{}: (10, {})} | custom-call | tf_op jit(solution)/shard_map/pressure_rows/pallas_call | solution.py:648
  (80 shorter events, 6.1 us)
Async XLA Ops:
  12.3 7.7 %collective-permute-start.1 = (bf16[6,256,128]{2,1,0:T(8,128)(2,1)}, bf16[6,256,128]{2,1,0:T(8,128)(2,1)S(1)}, u32[]{:S(2)}, u32[]{:S(2)}) collective-permute-start(bf16[6,256,128]{2,1,0:T(8,128)(2,1)} %get-tuple-element.56), channel_id=1, source_target_pairs={{0,1},{1,2},{2,3},{4,5},{5,6},{6,7},{8,9},{9,10},{10,11},{12,13},{... | collective-permute-start | bytes 1179656 | tf_op jit(solution)/shard_map/ppermute | solution.py:110
  14.7 5.9 %collective-permute-start = (bf16[6,256,128]{2,1,0:T(8,128)(2,1)}, bf16[6,256,128]{2,1,0:T(8,128)(2,1)S(1)}, u32[]{:S(2)}, u32[]{:S(2)}) collective-permute-start(bf16[6,256,128]{2,1,0:T(8,128)(2,1)} %get-tuple-element.56), channel_id=1, source_target_pairs={{1,0},{2,1},{3,2},{5,4},{6,5},{7,6},{9,8},{10,9},{11,10},{13,12},{... | collective-permute-start | bytes 1179656 | tf_op jit(solution)/shard_map/ppermute | solution.py:109
  16.0 9.6 %collective-permute-start.3 = (f32[6,64,128]{2,1,0:T(8,128)}, f32[6,64,128]{2,1,0:T(8,128)S(1)}, u32[]{:S(2)}, u32[]{:S(2)}) collective-permute-start(f32[6,64,128]{2,1,0:T(8,128)} %get-tuple-element.60), channel_id=1, source_target_pairs={{0,4},{4,8},{8,12},{12,16},{16,20},{20,24},{24,28},{28,0},{1,5},{5... | collective-permute-start | bytes 589832 | tf_op jit(solution)/shard_map/ppermute | solution.py:111
  19.3 28.0 %copy-start.14 = (f32[2,4,8,64]{3,2,1,0:T(8,128)}, f32[2,4,8,64]{3,2,1,0:T(8,128)S(1)}, u32[]{:S(2)}) copy-start(f32[2,4,8,64]{3,2,1,0:T(8,128)S(1)} %copy.25) | copy-start | bytes 49156
  25.6 0.7 copy-start.2
  26.3 22.9 %copy-start.16 = (f32[128,512]{1,0:T(8,128)S(1)}, f32[128,512]{1,0:T(8,128)}, u32[]{:S(2)}) copy-start(f32[128,512]{1,0:T(8,128)} %param.10) | copy-start | bytes 786436
  26.3 25.4 %copy-start.18 = (f32[6,64,128]{2,1,0:T(8,128)S(1)}, f32[6,64,128]{2,1,0:T(8,128)}, u32[]{:S(2)}) copy-start(f32[6,64,128]{2,1,0:T(8,128)} %get-tuple-element.59) | copy-start | bytes 589828
  47.3 37.1 %collective-permute-start.10 = (f32[128,8,128]{2,1,0:T(8,128)}, f32[128,8,128]{2,1,0:T(8,128)S(1)}, u32[]{:S(2)}, u32[]{:S(2)}) collective-permute-start(f32[128,8,128]{2,1,0:T(8,128)} %get-tuple-element.87), channel_id=1, source_target_pairs={{0,1},{1,0},{2,3},{3,2},{4,5},{5,4},{6,7},{7,6},{8,9},{9,8},{10,11... | collective-permute-start | bytes 1572872 | tf_op jit(solution)/shard_map/ppermute | solution.py:677
  49.3 32.9 %collective-permute-start.9 = (f32[128,512]{0,1:T(8,128)S(1)}, f32[128,512]{0,1:T(8,128)S(1)}, u32[]{:S(2)}, u32[]{:S(2)}) collective-permute-start(f32[128,512]{0,1:T(8,128)S(1)} %copy.29), channel_id=1, source_target_pairs={{0,3},{1,2},{2,1},{3,0},{4,7},{5,6},{6,5},{7,4},{8,11},{9,10},{10,... | collective-permute-start | bytes 786440 | tf_op jit(solution)/shard_map/ppermute | solution.py:677
  51.5 30.9 %collective-permute-start.8 = (f32[128,512]{0,1:T(8,128)S(1)}, f32[128,512]{0,1:T(8,128)S(1)}, u32[]{:S(2)}, u32[]{:S(2)}) collective-permute-start(f32[128,512]{0,1:T(8,128)S(1)} %copy.29), channel_id=1, source_target_pairs={{0,2},{1,3},{2,0},{3,1},{4,6},{5,7},{6,4},{7,5},{8,10},{9,11},{10,... | collective-permute-start | bytes 786440 | tf_op jit(solution)/shard_map/ppermute | solution.py:677
  51.5 32.2 %collective-permute-start.7 = (f32[128,512]{0,1:T(8,128)S(1)}, f32[128,512]{0,1:T(8,128)S(1)}, u32[]{:S(2)}, u32[]{:S(2)}) collective-permute-start(f32[128,512]{0,1:T(8,128)S(1)} %copy.29), channel_id=1, source_target_pairs={{0,1},{1,0},{2,3},{3,2},{4,5},{5,4},{6,7},{7,6},{8,9},{9,8},{10,11... | collective-permute-start | bytes 786440 | tf_op jit(solution)/shard_map/ppermute | solution.py:677
  51.7 8.7 %collective-permute-start.2 = (f32[6,64,128]{2,1,0:T(8,128)S(1)}, f32[6,64,128]{2,1,0:T(8,128)S(1)}, u32[]{:S(2)}, u32[]{:S(2)}) collective-permute-start(f32[6,64,128]{2,1,0:T(8,128)S(1)} %copy-done.18), channel_id=1, source_target_pairs={{4,0},{8,4},{12,8},{16,12},{20,16},{24,20},{28,24},{0,28},{5,1},{9... | collective-permute-start | bytes 589832 | tf_op jit(solution)/shard_map/ppermute | solution.py:112
  60.4 0.7 copy-start.3
  60.4 27.9 %collective-permute-start.11 = (f32[128,8,128]{2,1,0:T(8,128)}, f32[128,8,128]{2,1,0:T(8,128)S(1)}, u32[]{:S(2)}, u32[]{:S(2)}) collective-permute-start(f32[128,8,128]{2,1,0:T(8,128)} %get-tuple-element.88), channel_id=1, source_target_pairs={{0,2},{1,3},{2,0},{3,1},{4,6},{5,7},{6,4},{7,5},{8,10},{9,11},{10,... | collective-permute-start | bytes 1572872 | tf_op jit(solution)/shard_map/ppermute | solution.py:677
  61.1 24.1 %copy-start.17 = (f32[512]{0:T(512)S(1)}, f32[512]{0:T(512)}, u32[]{:S(2)}) copy-start(f32[512]{0:T(512)} %param.11) | copy-start | bytes 6148
  82.2 14.5 %collective-permute-start.12 = (f32[128,8,128]{2,1,0:T(8,128)}, f32[128,8,128]{2,1,0:T(8,128)S(1)}, u32[]{:S(2)}, u32[]{:S(2)}) collective-permute-start(f32[128,8,128]{2,1,0:T(8,128)} %get-tuple-element.89), channel_id=1, source_target_pairs={{0,3},{1,2},{2,1},{3,0},{4,7},{5,6},{6,5},{7,4},{8,11},{9,10},{10,... | collective-permute-start | bytes 1572872 | tf_op jit(solution)/shard_map/ppermute | solution.py:677
  82.4 16.5 %collective-permute-start.13 = (f32[128,8,128]{2,1,0:T(8,128)}, f32[128,8,128]{2,1,0:T(8,128)}, u32[]{:S(2)}, u32[]{:S(2)}) collective-permute-start(f32[128,8,128]{2,1,0:T(8,128)} %get-tuple-element.91), channel_id=1, source_target_pairs={{0,1},{1,0},{2,3},{3,2},{4,5},{5,4},{6,7},{7,6},{8,9},{9,8},{10,11... | collective-permute-start | bytes 1572872 | tf_op jit(solution)/shard_map/ppermute | solution.py:677
  83.8 24.1 %collective-permute-start.14 = (f32[128,8,128]{2,1,0:T(8,128)}, f32[128,8,128]{2,1,0:T(8,128)}, u32[]{:S(2)}, u32[]{:S(2)}) collective-permute-start(f32[128,8,128]{2,1,0:T(8,128)} %get-tuple-element.92), channel_id=1, source_target_pairs={{0,2},{1,3},{2,0},{3,1},{4,6},{5,7},{6,4},{7,5},{8,10},{9,11},{10,... | collective-permute-start | bytes 1572872 | tf_op jit(solution)/shard_map/ppermute | solution.py:677
  84.4 0.8 copy-start.11
  84.4 34.9 %collective-permute-start.15 = (f32[128,8,128]{2,1,0:T(8,128)}, f32[128,8,128]{2,1,0:T(8,128)}, u32[]{:S(2)}, u32[]{:S(2)}) collective-permute-start(f32[128,8,128]{2,1,0:T(8,128)} %get-tuple-element.93), channel_id=1, source_target_pairs={{0,3},{1,2},{2,1},{3,0},{4,7},{5,6},{6,5},{7,4},{8,11},{9,10},{10,... | collective-permute-start | bytes 1572872 | tf_op jit(solution)/shard_map/ppermute | solution.py:677
  86.1 62.0 %copy-start = (bf16[512,512]{0,1:T(8,128)(2,1)}, bf16[512,512]{0,1:T(8,128)(2,1)S(1)}, u32[]{:S(2)}) copy-start(bf16[512,512]{0,1:T(8,128)(2,1)S(1)} %get-tuple-element.107) | copy-start | bytes 1572868
  86.1 62.0 %copy-start.1 = (bf16[512,512]{0,1:T(8,128)(2,1)}, bf16[512,512]{0,1:T(8,128)(2,1)S(1)}, u32[]{:S(2)}) copy-start(bf16[512,512]{0,1:T(8,128)(2,1)S(1)} %get-tuple-element.108) | copy-start | bytes 1572868
  88.3 0.8 copy-start.12
  89.1 78.2 %collective-permute-start.4 = (f32[256,8,128]{2,1,0:T(8,128)}, f32[256,8,128]{2,1,0:T(8,128)S(1)}, u32[]{:S(2)}, u32[]{:S(2)}) collective-permute-start(f32[256,8,128]{2,1,0:T(8,128)} %get-tuple-element.67), channel_id=1, source_target_pairs={{0,1},{1,0},{2,3},{3,2},{4,5},{5,4},{6,7},{7,6},{8,9},{9,8},{10,11... | collective-permute-start | bytes 3145736 | tf_op jit(solution)/shard_map/ppermute | solution.py:677
  96.7 0.8 copy-start.13
  97.5 69.8 %collective-permute-start.5 = (f32[256,8,128]{2,1,0:T(8,128)}, f32[256,8,128]{2,1,0:T(8,128)S(1)}, u32[]{:S(2)}, u32[]{:S(2)}) collective-permute-start(f32[256,8,128]{2,1,0:T(8,128)} %get-tuple-element.68), channel_id=1, source_target_pairs={{0,2},{1,3},{2,0},{3,1},{4,6},{5,7},{6,4},{7,5},{8,10},{9,11},{10,... | collective-permute-start | bytes 3145736 | tf_op jit(solution)/shard_map/ppermute | solution.py:677
  98.9 68.4 %collective-permute-start.6 = (f32[256,8,128]{2,1,0:T(8,128)}, f32[256,8,128]{2,1,0:T(8,128)}, u32[]{:S(2)}, u32[]{:S(2)}) collective-permute-start(f32[256,8,128]{2,1,0:T(8,128)} %get-tuple-element.69), channel_id=1, source_target_pairs={{0,3},{1,2},{2,1},{3,0},{4,7},{5,6},{6,5},{7,4},{8,11},{9,10},{10,... | collective-permute-start | bytes 3145736 | tf_op jit(solution)/shard_map/ppermute | solution.py:677
  127.7 28.5 %all-to-all-start.1 = ((f32[8,2,8,512]{3,2,1,0:T(8,128)}), f32[8,2,8,512]{3,2,1,0:T(8,128)S(1)}, u32[]{:S(2)}, u32[]{:S(2)}) async-start(f32[8,2,8,512]{3,2,1,0:T(8,128)} %get-tuple-element.95), calls=%async_computation.1 | async-start | bytes 524288 | tf_op jit(solution)/shard_map/all_to_all | solution.py:682
  156.2 0.7 copy-start.10
  167.2 60.0 %collective-permute-start.16 = (f32[256,8,128]{2,1,0:T(8,128)}, f32[256,8,128]{2,1,0:T(8,128)S(1)}, u32[]{:S(2)}, u32[]{:S(2)}) collective-permute-start(f32[256,8,128]{2,1,0:T(8,128)} %get-tuple-element.99), channel_id=1, source_target_pairs={{0,1},{1,0},{2,3},{3,2},{4,5},{5,4},{6,7},{7,6},{8,9},{9,8},{10,11... | collective-permute-start | bytes 3145736 | tf_op jit(solution)/shard_map/ppermute | solution.py:677
  167.3 1.0 copy-start.5
  167.3 1.3 copy-start.8
  176.6 37.7 %all-to-all-start = ((f32[8,2,8,512]{3,2,1,0:T(8,128)}), f32[8,2,8,512]{3,2,1,0:T(8,128)S(1)}, u32[]{:S(2)}, u32[]{:S(2)}) async-start(f32[8,2,8,512]{3,2,1,0:T(8,128)} %get-tuple-element.72), calls=%async_computation | async-start | bytes 524288 | tf_op jit(solution)/shard_map/all_to_all | solution.py:682
  199.8 27.5 %copy-start.15 = (f32[2,4,8,64]{3,2,1,0:T(8,128)S(1)}, f32[2,4,8,64]{3,2,1,0:T(8,128)}, u32[]{:S(2)}) copy-start(f32[2,4,8,64]{3,2,1,0:T(8,128)} %copy-done.14) | copy-start | bytes 49156
  212.6 112.5 %collective-permute-start.17 = (f32[256,8,128]{2,1,0:T(8,128)}, f32[256,8,128]{2,1,0:T(8,128)S(1)}, u32[]{:S(2)}, u32[]{:S(2)}) collective-permute-start(f32[256,8,128]{2,1,0:T(8,128)} %get-tuple-element.100), channel_id=1, source_target_pairs={{0,2},{1,3},{2,0},{3,1},{4,6},{5,7},{6,4},{7,5},{8,10},{9,11},{10,... | collective-permute-start | bytes 3145736 | tf_op jit(solution)/shard_map/ppermute | solution.py:677
  214.0 111.2 %collective-permute-start.18 = (f32[256,8,128]{2,1,0:T(8,128)}, f32[256,8,128]{2,1,0:T(8,128)S(1)}, u32[]{:S(2)}, u32[]{:S(2)}) collective-permute-start(f32[256,8,128]{2,1,0:T(8,128)} %get-tuple-element.101), channel_id=1, source_target_pairs={{0,3},{1,2},{2,1},{3,0},{4,7},{5,6},{6,5},{7,4},{8,11},{9,10},{10,... | collective-permute-start | bytes 3145736 | tf_op jit(solution)/shard_map/ppermute | solution.py:677
  214.2 0.7 copy-start.9
  225.2 100.0 %collective-permute-start.19 = (f32[256,8,128]{2,1,0:T(8,128)}, f32[256,8,128]{2,1,0:T(8,128)}, u32[]{:S(2)}, u32[]{:S(2)}) collective-permute-start(f32[256,8,128]{2,1,0:T(8,128)} %get-tuple-element.103), channel_id=1, source_target_pairs={{0,1},{1,0},{2,3},{3,2},{4,5},{5,4},{6,7},{7,6},{8,9},{9,8},{10,11... | collective-permute-start | bytes 3145736 | tf_op jit(solution)/shard_map/ppermute | solution.py:677
  225.9 99.3 %collective-permute-start.20 = (f32[256,8,128]{2,1,0:T(8,128)}, f32[256,8,128]{2,1,0:T(8,128)}, u32[]{:S(2)}, u32[]{:S(2)}) collective-permute-start(f32[256,8,128]{2,1,0:T(8,128)} %get-tuple-element.104), channel_id=1, source_target_pairs={{0,2},{1,3},{2,0},{3,1},{4,6},{5,7},{6,4},{7,5},{8,10},{9,11},{10,... | collective-permute-start | bytes 3145736 | tf_op jit(solution)/shard_map/ppermute | solution.py:677
  227.2 97.9 %copy-start.4 = (f32[256,8,128]{2,1,0:T(8,128)}, f32[256,8,128]{2,1,0:T(8,128)S(1)}, u32[]{:S(2)}) copy-start(f32[256,8,128]{2,1,0:T(8,128)S(1)} %collective-permute-done.16.refs_1_) | copy-start | bytes 3145732
  227.2 98.0 %collective-permute-start.21 = (f32[256,8,128]{2,1,0:T(8,128)}, f32[256,8,128]{2,1,0:T(8,128)}, u32[]{:S(2)}, u32[]{:S(2)}) collective-permute-start(f32[256,8,128]{2,1,0:T(8,128)} %get-tuple-element.105), channel_id=1, source_target_pairs={{0,3},{1,2},{2,1},{3,0},{4,7},{5,6},{6,5},{7,4},{8,11},{9,10},{10,... | collective-permute-start | bytes 3145736 | tf_op jit(solution)/shard_map/ppermute | solution.py:677
  227.4 79.5 %all-to-all-start.2 = ((f32[32,8,128]{2,1,0:T(8,128)}), f32[32,8,128]{2,1,0:T(8,128)S(1)}, u32[]{:S(2)}, u32[]{:S(2)}) async-start(f32[32,8,128]{2,1,0:T(8,128)} %get-tuple-element.97), calls=%async_computation.2 | async-start | bytes 262144 | tf_op jit(solution)/shard_map/all_to_all | solution.py:682
  325.2 1.0 copy-start.6
  325.2 1.3 copy-start.7

commit v3 on v2

--- a/solution.py
+++ b/solution.py
@@ -17,6 +17,8 @@
 
 
 SLAB = 8
+FLUID = 16
+PICKED = (1, 2, 4)
 EDGE = 16
 ROWS = 32
 TILE = 64
@@ -53,14 +55,41 @@
 
 
 def edges_kernel(state_ref, shear_ref, perm_ref, cols_ref, *rest):
-    *row_refs, acc = rest
+    *row_refs, acc, chosen = rest
     step = pl.program_id(0)
     slab, count, width = shear_ref.shape
     rows = min(64, count // 2)
     places = (0, count // 2 - 1, count // 2, count - 1)
     lane = lanes_of((rows, width))
+    sources = [state_ref.at[c] if c < 4 else (shear_ref, perm_ref)[c - 4] for c in range(6)]
+
+    @pl.when(step == 0)
+    def _():
+        row = lax.broadcasted_iota(jnp.int32, (slab * width, width), 0)
+        plane = lax.div(row, width)
+        spot = lax.rem(row, width)
+        column = lanes_of((slab * width, width))
+        wanted = (spot == 0) & (column == 2 * plane + 1) | (spot == width - 1) & (column == 2 * plane)
+        chosen[...] = jnp.where(wanted, 1.0, 0.0).astype(bf16)
+        for c in PICKED:
+            acc[c] = jnp.zeros_like(acc[c])
+
+    for c in PICKED:
+        src = sources[c]
+        planes = jnp.concatenate([src[i] for i in range(slab)], axis=1)
+        packed = jnp.dot(planes, chosen[...], preferred_element_type=f32)
+        acc[c] += pltpu.roll(packed, 2 * slab * step, 1)
+        for i in range(slab):
+            h = step * slab + i
+            for place, row_ref in zip(places, row_refs):
+                start = place // 16 * 16
+                x = src[i, start : start + 16, :].astype(f32)
+                row_ref[c, pl.ds(h, 1), :] = x[place - start : place - start + 1]
+
     for c in range(6):
-        src = state_ref.at[c] if c < 4 else (shear_ref, perm_ref)[c - 4]
+        if c in PICKED:
+            continue
+        src = sources[c]
         for start in range(0, count, rows):
             value = acc[c, start : start + rows, :]
             for i in range(slab):
@@ -97,7 +126,7 @@
             jax.ShapeDtypeStruct((6, count, width), bf16),
             *[jax.ShapeDtypeStruct((6, height, width), f32)] * 4,
         ],
-        scratch_shapes=[pltpu.VMEM((6, count, width), f32)],
+        scratch_shapes=[pltpu.VMEM((6, count, width), f32), pltpu.VMEM((EDGE * width, width), bf16)],
         compiler_params=params(),
         name="edges",
     )(state, shear, perm)
@@ -203,7 +232,7 @@
                 total = total + fold(value * value)
             return total
 
-        sum_ref[...] += lax.fori_loop(0, slab, plane, jnp.zeros((8, width), f32))
+        sum_ref[...] += lax.fori_loop(0, slab, plane, jnp.zeros((8, width), f32), unroll=4)
 
     @pl.when(step >= steps)
     def _():
@@ -255,11 +284,11 @@
 def fluid(state, source, perm, beside, before, after, table, parts, half, shared):
     _, height, whole_count, width = state.shape
     count = whole_count // HALVES
-    steps = height // SLAB
+    steps = height // FLUID
     tile = min(TILE, count)
     pieces = parts * CHUNKS
     levels = height // pieces
-    specs = lambda c: plane_specs(c, SLAB, steps, count, width, part=half)
+    specs = lambda c: plane_specs(c, FLUID, steps, count, width, part=half)
     whole = lambda x: pl.BlockSpec(x.shape, lambda i: (0,) * x.ndim)
     at = lambda first: pl.BlockSpec(
         (tile, levels, width), lambda i: (first + jnp.maximum(i - steps, 0), 0, 0)
@@ -283,10 +312,10 @@
             jax.ShapeDtypeStruct((8, width), f32),
         ],
         scratch_shapes=[
-            pltpu.VMEM((SLAB + 2, count + 16, width), f32),
-            pltpu.VMEM((SLAB + 2, count + 16, width), f32),
-            pltpu.VMEM((SLAB + 2, count + 16, width), f32),
-            pltpu.VMEM((SLAB, count + 16, width), f32),
+            pltpu.VMEM((FLUID + 2, count + 16, width), f32),
+            pltpu.VMEM((FLUID + 2, count + 16, width), f32),
+            pltpu.VMEM((FLUID + 2, count + 16, width), f32),
+            pltpu.VMEM((FLUID, count + 16, width), f32),
             pltpu.VMEM((height, count, width), f32),
         ],
         input_output_aliases={16 + i: pieces - len(shared) + i for i in range(len(shared))},
@@ -354,7 +383,7 @@
         return rr, rz
 
     zero = jnp.zeros((8, width), f32)
-    rr, rz = lax.fori_loop(0, slab, plane, (zero, zero))
+    rr, rz = lax.fori_loop(0, slab, plane, (zero, zero), unroll=2)
     rr_ref[...] += 0.25 * rr
     rz_ref[...] -= 0.5 * rz
 
@@ -531,8 +560,13 @@
         carry_ref[...] = q
         sum_ref[...] += dot
         back = product(block[...].reshape(tile * levels, total), high_ref, low_ref)
-        for part, out in enumerate(outs):
-            out[...] = back[:, part * width : (part + 1) * width].reshape(tile, levels, width)
+        span = half // (len(outs) * width // total)
+        for index, out in enumerate(outs):
+            group, part = divmod(index, total // width)
+
+            @pl.when((base >= group * span * tile) & (base < (group + 1) * span * tile))
+            def _():
+                out[...] = back[:, part * width : (part + 1) * width].reshape(tile, levels, width)
 
     @pl.when(step == 2 * half - 1)
     def _():
@@ -551,12 +585,17 @@
 
 
 def solve(place, x, ends, ratio, gain, span, high, low, rr, rz, prior, parts, copies, last):
+    groups = HALVES if last else 1
     count, levels, total = x.shape
-    tile = min(TILE, count)
+    tile = min(TILE, count // groups)
     half = count // tile
     width = total // parts
     whole = lambda v: pl.BlockSpec(v.shape, lambda i, s: (0,) * v.ndim)
     back = lambda i: jnp.minimum(2 * half - 1 - i, half - 1)
+    share = half // groups
+    out_at = lambda group: pl.BlockSpec(
+        (tile, levels, width), lambda i, s: (jnp.clip(back(i) - group * share, 0, share - 1), 0, 0)
+    )
     return pl.pallas_call(
         functools.partial(solve_kernel, last),
         grid_spec=pltpu.PrefetchScalarGridSpec(
@@ -567,7 +606,7 @@
                 whole(ends), whole(ratio), whole(gain), whole(span), whole(high), whole(low), whole(rr), whole(rz), whole(prior),
             ],
             out_specs=[
-                *[pl.BlockSpec((tile, levels, width), lambda i, s: (back(i), 0, 0))] * parts,
+                *[out_at(group) for group in range(groups) for _ in range(parts)],
                 pl.BlockSpec((copies, 8, width), lambda i, s: (0, 0, 0)),
             ],
             scratch_shapes=[
@@ -579,7 +618,7 @@
             ],
         ),
         out_shape=[
-            *[jax.ShapeDtypeStruct((count, levels, width), f32)] * parts,
+            *[jax.ShapeDtypeStruct((count // groups, levels, width), f32)] * (parts * groups),
             jax.ShapeDtypeStruct((copies, 8, width), f32),
         ],
         compiler_params=params(),
@@ -639,29 +678,31 @@
     lax.fori_loop(0, tile // 16, group, 0)
 
 
-def pressure_rows(alpha, planes, cosine, rest):
-    count, levels, width = planes[0].shape
-    height = levels * len(planes)
+def pressure_rows(alpha, planes, table, out, half):
+    _, height, whole_count, width = out.shape
+    count = whole_count // HALVES
     tile = min(TILE, count)
-    high, low = split_table(cosine)
-    table = jnp.concatenate([high, high, low], axis=1)
+    first = half * (count // tile)
+    at = lambda x: pl.BlockSpec(
+        (tile, *x.shape[1:]), lambda i, s: (i if x.shape[0] == count else first + i, 0, 0)
+    )
     return pl.pallas_call(
         pressure_kernel,
         grid_spec=pltpu.PrefetchScalarGridSpec(
             num_scalar_prefetch=1,
             grid=(count // tile,),
             in_specs=[
-                *[pl.BlockSpec((tile, levels, width), lambda i, s: (i, 0, 0))] * len(planes),
+                *[at(x) for x in planes],
                 pl.BlockSpec(table.shape, lambda i, s: (0, 0)),
                 pl.BlockSpec(memory_space=pl.ANY),
             ],
-            out_specs=pl.BlockSpec((1, height, tile, width), lambda i, s: (3, 0, i, 0)),
+            out_specs=pl.BlockSpec((1, height, tile, width), lambda i, s: (3, 0, first + i, 0)),
         ),
-        out_shape=jax.ShapeDtypeStruct(rest.shape, bf16),
+        out_shape=jax.ShapeDtypeStruct(out.shape, bf16),
         input_output_aliases={len(planes) + 2: 0},
         compiler_params=params(),
         name="pressure_rows",
-    )(alpha, *planes, table, rest)
+    )(alpha, *planes, table, out)
 
 
 def cosine_table(extent):
@@ -741,11 +782,20 @@
         else:
             sums = sums[0]
             moment, rr, rz = momentum(state, shear, *around, (3, 6), (rr, rz), moment)
-        planes += pairwise(back, "rad")
+        if last:
+            backs = [None] * HALVES
+            for half in reversed(range(HALVES)):
+                backs[half] = pairwise(back[half * parts : (half + 1) * parts], "rad")
+        else:
+            planes += pairwise(back, "rad")
     totals = jnp.sum(sums, axis=(0, 2))
     alpha = (totals[0] / totals[1]).reshape(1)
     out = scale_rows(alpha, moment)
-    return pressure_rows(alpha, planes, cosine.T, out)
+    high, low = split_table(cosine.T)
+    table = jnp.concatenate([high, high, low], axis=1)
+    for half in reversed(range(HALVES)):
+        out = pressure_rows(alpha, planes + backs[half], table, out, half)
+    return out
 
 
 def solution(mesh):

time: 336 us -> 285 us (0.85)
  waiting for transfers between devices: 109 us -> 66.8 us
  Pallas kernels: 168 us -> 157 us
  starting transfers between devices: 42.3 us -> 45.8 us
    all_to_all x3, waiting for transfers between devices: 72.6 us -> 39 us  [exchanged(): return lax.all_to_all(copies, axis, split_axis=0, concat_axis=0, tiled=True)]
    ppermute x18 -> x21, starting transfers between devices: 13.5 us -> 22.6 us  [pairwise(): lax.ppermute(pieces[s], axis, [(i, i ^ s) for i in range(count)])]
    pallas_call x2, Pallas kernels: 42.1 us -> 33.8 us  [fluid(): pl.pallas_call(functools.partial(fluid_kernel, len(shared)), grid=(steps...]
    ppermute x18 -> x21, waiting for transfers between devices: 27.4 us -> 20.2 us  [pairwise(): lax.ppermute(pieces[s], axis, [(i, i ^ s) for i in range(count)])]
    ppermute x1, waiting for transfers between devices: 4.63 us -> 0.01 us  [neighbours(): lax.ppermute(first, 'az', [((i + 1) % n_az, i) for i in range(n_az)])]
    pallas_call x4, Pallas kernels: 51.5 us -> 47.5 us  [momentum(): pl.pallas_call(functools.partial(momentum_kernel, base, steps, len(prior)...]
    all_to_all x3, starting transfers between devices: 18.7 us -> 15 us  [exchanged(): return lax.all_to_all(copies, axis, split_axis=0, concat_axis=0, tiled=True)]
    ppermute x1, waiting for transfers between devices: 4.15 us -> 7.69 us  [neighbours(): lax.ppermute(last, 'az', [(i, (i + 1) % n_az) for i in range(n_az)])]
  transfers between devices with their start and end apart: 25 -> 28, of which waited for: 7 -> 6; matrix products, arithmetic and copies ran while one was open for 2% -> 3% of each run, Pallas kernels for 38% -> 50%
where the time goes in v3:
time: 285 us; the launch traced here: 284 us
  Pallas kernels  157 us (55%)
  waiting for transfers between devices  66.8 us (23%)
  starting transfers between devices  45.8 us (16%)
  local copies, waits for them, and re-layouts  8.95 us (3%)
  other arithmetic  3.62 us (1%)
    pallas_call x4, Pallas kernels, momentum(): pl.pallas_call(functools.partial(momentum_kernel, base, steps, len(prior)...  47.5 us
    all_to_all x3, waiting for transfers between devices, exchanged(): return lax.all_to_all(copies, axis, split_axis=0, concat_axis=0, tiled=True)  39 us
    pallas_call x2, Pallas kernels, fluid(): pl.pallas_call(functools.partial(fluid_kernel, len(shared)), grid=(steps...  33.8 us
    ppermute x21, starting transfers between devices, pairwise(): lax.ppermute(pieces[s], axis, [(i, i ^ s) for i in range(count)])  22.6 us
    pallas_call x2, Pallas kernels, solve(): pl.pallas_call(functools.partial(solve_kernel, last), grid_spec=pltpu.Pre...  21.4 us
    ppermute x21, waiting for transfers between devices, pairwise(): lax.ppermute(pieces[s], axis, [(i, i ^ s) for i in range(count)])  20.2 us
    pallas_call x2, Pallas kernels, modes(): pl.pallas_call(functools.partial(modes_kernel, len(groups)), grid=(count...  16.4 us
    pallas_call x1, Pallas kernels, scale_rows(): pl.pallas_call(scale_kernel, grid_spec=pltpu.PrefetchScalarGridSpec(num_s...  16.2 us
  transfers between devices with their start and end apart: 28, of which 6 were waited for; matrix products, arithmetic and copies ran while one was open for 3% of the time, Pallas kernels for 50%

profile of v3, /device:TPU:0, one launch (start us, length us, event | category | flops | bytes accessed | tf_op | source)
XLA Modules:
  0.0 283.8 jit_solution(8901939132050756521)
XLA Ops:
  0.0 11.2 %edges.1 = (bf16[6,256,128]{2,1,0:T(8,128)(2,1)}, f32[6,64,128]{2,1,0:T(8,128)}, f32[6,64,128]{2,1,0:T(8,128)}, f32[6,64,128]{2,1,0:T(8,128)}, f32[6,64,128]{2,1,0:T(8,128)}) custom-call(bf16[4,64,256,128]{3,2,1,0:T(8,128)(2,1)} %refs_11_.7, bf16[64,256,128]{2,1,0:T(8,128)(2,1)} %refs_14_.7, bf16[64,256,128]{2,1,0:T(8,128)(2,1)} %k_dn.3), custom_call_target="tpu_custom_call" | custom-call | tf_op jit(solution)/shard_map/edges/pallas_call | solution.py:116
  11.3 2.5 collective-permute-start.9
  13.8 0.6 collective-permute-start.8
  14.5 2.0 collective-permute-start.1
  16.4 1.3 collective-permute-start
  17.7 4.8 %collective-permute-start.2 = (f32[6,64,128]{2,1,0:T(8,128)}, f32[6,64,128]{2,1,0:T(8,128)S(1)}, u32[]{:S(2)}, u32[]{:S(2)}) collective-permute-start(f32[6,64,128]{2,1,0:T(8,128)} %get-tuple-element.63), channel_id=1, source_target_pairs={{4,0},{8,4},{12,8},{16,12},{20,16},{24,20},{28,24},{0,28},{5,1},{9... | collective-permute-start | bytes 589832 | tf_op jit(solution)/shard_map/ppermute | solution.py:141
  23.5 0.7 pad_maximum_fusion.1.cos_ref
  24.2 0.9 fusion.1.beside_ref.refs_15_
  25.1 7.7 %collective-permute-done.3.before_ref.refs_16_ = f32[6,64,128]{2,1,0:T(8,128)S(1)} collective-permute-done((f32[6,64,128]{2,1,0:T(8,128)}, f32[6,64,128]{2,1,0:T(8,128)S(1)}, u32[]{:S(2)}, u32[]{:S(2)}) %collective-permute-start.3) | collective-permute-done | bytes 196640 | tf_op jit(solution)/shard_map/ppermute | solution.py:140
  32.8 0.7 copy-done.3
  33.4 16.8 %fluid.2 = (f32[128,8,128]{2,1,0:T(8,128)}, f32[128,8,128]{2,1,0:T(8,128)}, f32[128,8,128]{2,1,0:T(8,128)}, f32[128,8,128]{2,1,0:T(8,128)}, f32[256,8,128]{2,1,0...) custom-call(bf16[4,64,256,128]{3,2,1,0:T(8,128)(2,1)} %refs_11_.7, ...), custom_call_target="tpu_custom_call" | custom-call | tf_op jit(solution)/shard_map/fluid/pallas_call | solution.py:297
  50.3 5.4 %collective-permute-start.10 = (f32[128,8,128]{2,1,0:T(8,128)}, f32[128,8,128]{2,1,0:T(8,128)S(1)}, u32[]{:S(2)}, u32[]{:S(2)}) collective-permute-start(f32[128,8,128]{2,1,0:T(8,128)} %get-tuple-element.91), channel_id=1, source_target_pairs={{0,1},{1,0},{2,3},{3,2},{4,5},{5,4},{6,7},{7,6},{8,9},{9,8},{10,11... | collective-permute-start | bytes 1572872 | tf_op jit(solution)/shard_map/ppermute | solution.py:718
  55.6 3.4 %collective-permute-start.11 = (f32[128,8,128]{2,1,0:T(8,128)}, f32[128,8,128]{2,1,0:T(8,128)S(1)}, u32[]{:S(2)}, u32[]{:S(2)}) collective-permute-start(f32[128,8,128]{2,1,0:T(8,128)} %get-tuple-element.92), channel_id=1, source_target_pairs={{0,2},{1,3},{2,0},{3,1},{4,6},{5,7},{6,4},{7,5},{8,10},{9,11},{10,... | collective-permute-start | bytes 1572872 | tf_op jit(solution)/shard_map/ppermute | solution.py:718
  59.7 16.9 %fluid.3 = (f32[128,8,128]{2,1,0:T(8,128)}, f32[128,8,128]{2,1,0:T(8,128)}, f32[128,8,128]{2,1,0:T(8,128)}, f32[128,8,128]{2,1,0:T(8,128)}, f32[256,8,128]{2,1,0...) custom-call(bf16[4,64,256,128]{3,2,1,0:T(8,128)(2,1)} %refs_11_.7, ...), custom_call_target="tpu_custom_call", output_to_operand_aliasing={{4}: (16, {}), {5}: (17, {}), {6}: (18, {}), {7}: (19, {})} | custom-call | tf_op jit(solution)/shard_map/fluid/pallas_call | solution.py:297
  77.3 2.0 collective-permute-done.7
  79.3 1.1 collective-permute-start.14
  81.2 0.8 copy-done.11
  82.2 0.7 collective-permute-done.12.refs_3_
  82.9 1.4 collective-permute-start.5
  84.9 0.7 multiply_multiply_fusion
  85.8 1.2 copy.32.refs_5_.refs_9_
  86.9 1.0 copy.31.refs_4_.refs_8_
  87.9 6.7 %collective-permute-done.14.refs_6_ = f32[128,8,128]{2,1,0:T(8,128)} collective-permute-done((f32[128,8,128]{2,1,0:T(8,128)}, f32[128,8,128]{2,1,0:T(8,128)}, u32[]{:S(2)}, u32[]{:S(2)}) %collective-permute-start.14) | collective-permute-done | bytes 524320 | tf_op jit(solution)/shard_map/ppermute | solution.py:718
  94.6 10.8 %collective-permute-done.15.refs_7_ = f32[128,8,128]{2,1,0:T(8,128)} collective-permute-done((f32[128,8,128]{2,1,0:T(8,128)}, f32[128,8,128]{2,1,0:T(8,128)}, u32[]{:S(2)}, u32[]{:S(2)}) %collective-permute-start.15) | collective-permute-done | bytes 524320 | tf_op jit(solution)/shard_map/ppermute | solution.py:718
  105.4 8.4 %modes.3 = (f32[256,8,512]{2,1,0:T(8,128)}, f32[8,2,8,512]{3,2,1,0:T(8,128)}) custom-call(f32[128,8,128]{2,1,0:T(8,128)} %get-tuple-element.90.refs_0_, f32[128,8,128]{2,1,0:T(8,128)} %copy-done.10, f32[128,8,128]{2,1,0:T(8,128)} %copy-done.11, f32[128,8,128]{2,1,0:T(8,128)} %collective-permute-done.12.refs_3_, f32[128,8,128]{2,1,0:T(8,128)} %get-tuple-element.94.refs_4_, ...), custom_call_target="tpu_custom_call" | custom-call | tf_op jit(solution)/shard_map/modes/pallas_call | solution.py:486
  113.8 3.6 %all-to-all-start.1 = ((f32[8,2,8,512]{3,2,1,0:T(8,128)}), f32[8,2,8,512]{3,2,1,0:T(8,128)S(1)}, u32[]{:S(2)}, u32[]{:S(2)}) async-start(f32[8,2,8,512]{3,2,1,0:T(8,128)} %get-tuple-element.99), calls=%async_computation.1 | async-start | bytes 524288 | tf_op jit(solution)/shard_map/all_to_all | solution.py:723
  117.4 0.6 broadcast_25_refs_19__refs_21__prior_ref.2.refs_19_.refs_21_.prior_ref
  118.0 12.4 %momentum.4 = (f32[3,64,256,128]{3,2,1,0:T(8,128)}, f32[8,128]{1,0:T(8,128)}, f32[8,128]{1,0:T(8,128)}) custom-call(bf16[4,64,256,128]{3,2,1,0:T(8,128)(2,1)} %refs_11_.7, bf16[4,64,256,128]{3,2,1,0:T(8,128)(2,1)} %refs_11_.7, bf16[4,64,256,128]{3,2,1,0:T(8,128)(2,1)} %refs_11_.7, bf16[4,64,256,128]{3,2,1,0:T(8,128)(2,1)} %refs_11_.7, ...), custom_call_target="tpu_custom_call" | custom-call | tf_op jit(solution)/shard_map/momentum/pallas_call | solution.py:407
  130.4 7.6 %momentum.5 = (f32[3,64,256,128]{3,2,1,0:T(8,128)}, f32[8,128]{1,0:T(8,128)}, f32[8,128]{1,0:T(8,128)}) custom-call(bf16[4,64,256,128]{3,2,1,0:T(8,128)(2,1)} %refs_11_.7, bf16[4,64,256,128]{3,2,1,0:T(8,128)(2,1)} %refs_11_.7, bf16[4,64,256,128]{3,2,1,0:T(8,128)(2,1)} %refs_11_.7, ...), custom_call_target="tpu_custom_call", output_to_operand_aliasing={{0}: (20, {})} | custom-call | tf_op jit(solution)/shard_map/momentum/pallas_call | solution.py:407
  138.0 0.7 copy-done.9
  138.7 10.4 %solve.2 = (f32[256,8,128]{2,1,0:T(8,128)}, f32[256,8,128]{2,1,0:T(8,128)}, f32[256,8,128]{2,1,0:T(8,128)}, f32[256,8,128]{2,1,0:T(8,128)}, f32[1,8,128]{2,1,0:T(8,128)}) custom-call(s32[1]{0:T(128)} %bitcast.place_ref, f32[256,8,512]{2,1,0:T(8,128)} %get-tuple-element.98.x_ref, f32[8,2,8,512]{3,2,1,0:T(8,128)} %copy-done.9, ...), custom_call_target="tpu_custom_call" | custom-call | tf_op jit(solution)/shard_map/solve/pallas_call | solution.py:599
  149.5 2.0 collective-permute-start.17
  151.5 1.0 copy-done.7
  152.5 8.0 %modes.2 = (f32[256,8,512]{2,1,0:T(8,128)}, f32[8,2,8,512]{3,2,1,0:T(8,128)}) custom-call(f32[256,8,128]{2,1,0:T(8,128)} %get-tuple-element.70.refs_0_, f32[256,8,128]{2,1,0:T(8,128)} %copy-done.7, f32[256,8,128]{2,1,0:T(8,128)} %collective-permute-done.5.refs_2_, f32[256,8,128]{2,1,0:T(8,128)} %collective-permute-done.6.refs_3_, ...), custom_call_target="tpu_custom_call" | custom-call | tf_op jit(solution)/shard_map/modes/pallas_call | solution.py:486
  160.5 5.5 %all-to-all-start = ((f32[8,2,8,512]{3,2,1,0:T(8,128)}), f32[8,2,8,512]{3,2,1,0:T(8,128)S(1)}, u32[]{:S(2)}, u32[]{:S(2)}) async-start(f32[8,2,8,512]{3,2,1,0:T(8,128)} %get-tuple-element.76), calls=%async_computation | async-start | bytes 524288 | tf_op jit(solution)/shard_map/all_to_all | solution.py:723
  166.0 15.7 %momentum.6 = (f32[3,64,256,128]{3,2,1,0:T(8,128)}, f32[8,128]{1,0:T(8,128)}, f32[8,128]{1,0:T(8,128)}) custom-call(bf16[4,64,256,128]{3,2,1,0:T(8,128)(2,1)} %refs_11_.7, bf16[4,64,256,128]{3,2,1,0:T(8,128)(2,1)} %refs_11_.7, bf16[4,64,256,128]{3,2,1,0:T(8,128)(2,1)} %refs_11_.7, ...), custom_call_target="tpu_custom_call", output_to_operand_aliasing={{0}: (20, {})} | custom-call | tf_op jit(solution)/shard_map/momentum/pallas_call | solution.py:407
  181.7 11.8 %momentum.7 = (f32[3,64,256,128]{3,2,1,0:T(8,128)}, f32[8,128]{1,0:T(8,128)}, f32[8,128]{1,0:T(8,128)}) custom-call(bf16[4,64,256,128]{3,2,1,0:T(8,128)(2,1)} %refs_11_.7, bf16[4,64,256,128]{3,2,1,0:T(8,128)(2,1)} %refs_11_.7, bf16[4,64,256,128]{3,2,1,0:T(8,128)(2,1)} %refs_11_.7, ...), custom_call_target="tpu_custom_call", output_to_operand_aliasing={{0}: (20, {})} | custom-call | tf_op jit(solution)/shard_map/momentum/pallas_call | solution.py:407
  193.5 0.7 copy-done.8
  194.2 10.9 %solve.3 = (f32[128,8,128]{2,1,0:T(8,128)}, f32[128,8,128]{2,1,0:T(8,128)}, f32[128,8,128]{2,1,0:T(8,128)}, f32[128,8,128]{2,1,0:T(8,128)}, f32[128,8,128]{2,1,0...) custom-call(s32[1]{0:T(128)} %bitcast.place_ref, ...), custom_call_target="tpu_custom_call" | custom-call | tf_op jit(solution)/shard_map/solve/pallas_call | solution.py:599
  205.7 1.4 collective-permute-start.23
  207.3 1.7 collective-permute-start.20
  209.3 6.0 %all-to-all-start.2 = ((f32[32,8,128]{2,1,0:T(8,128)}), f32[32,8,128]{2,1,0:T(8,128)S(1)}, u32[]{:S(2)}, u32[]{:S(2)}) async-start(f32[32,8,128]{2,1,0:T(8,128)} %get-tuple-element.101), calls=%async_computation.2 | async-start | bytes 262144 | tf_op jit(solution)/shard_map/all_to_all | solution.py:723
  215.3 0.7 pad_maximum_fusion.2.refs_8_
  216.0 39.0 %all-to-all-done.2 = f32[32,8,128]{2,1,0:T(8,128)S(1)} async-done(((f32[32,8,128]{2,1,0:T(8,128)}), f32[32,8,128]{2,1,0:T(8,128)S(1)}, u32[]{:S(2)}, u32[]{:S(2)}) %all-to-all-start.2) | async-done | bytes 131104 | tf_op jit(solution)/shard_map/all_to_all | solution.py:723
  255.1 0.6 fusion.13
  256.9 16.2 %scale_rows.1.refs_9_ = bf16[4,64,256,128]{3,2,1,0:T(8,128)(2,1)} custom-call(f32[1]{0:T(128)S(6)} %div.39.alpha_ref, f32[3,64,256,128]{3,2,1,0:T(8,128)} %get-tuple-element.114.in_ref), custom_call_target="tpu_custom_call" | custom-call | tf_op jit(solution)/shard_map/scale_rows/pallas_call | solution.py:635
  273.1 5.4 %pressure_rows.2.refs_9_ = bf16[4,64,256,128]{3,2,1,0:T(8,128)(2,1)} custom-call(f32[1]{0:T(128)S(6)} %div.39.alpha_ref, f32[256,8,128]{2,1,0:T(8,128)} %get-tuple-element.102.refs_0_, f32[256,8,128]{2,1,0:T(8,128)} %copy-done.4, f32[256,8,128]{2,1,0:T(8,128)} %copy-done.5, f32[256,8,128]{2,1,0:T(8,128)} %copy-done.6, ...), custom_call_target="tpu_custom_call", output_to_operand_aliasing={{}: (10, {})} | custom-call | tf_op jit(solution)/shard_map/pressure_rows/pallas_call | solution.py:689
  278.5 5.3 %pressure_rows.3 = bf16[4,64,256,128]{3,2,1,0:T(8,128)(2,1)} custom-call(f32[1]{0:T(128)S(6)} %div.39.alpha_ref, f32[256,8,128]{2,1,0:T(8,128)} %get-tuple-element.102.refs_0_, f32[256,8,128]{2,1,0:T(8,128)} %copy-done.4, f32[256,8,128]{2,1,0:T(8,128)} %copy-done.5, f32[256,8,128]{2,1,0:T(8,128)} %copy-done.6, ...), custom_call_target="tpu_custom_call", output_to_operand_aliasing={{}: (10, {})} | custom-call | tf_op jit(solution)/shard_map/pressure_rows/pallas_call | solution.py:689
  (81 shorter events, 5.7 us)
Async XLA Ops:
  0.0 11.2 %copy-start.14 = (f32[128,512]{1,0:T(8,128)S(1)}, f32[128,512]{1,0:T(8,128)}, u32[]{:S(2)}) copy-start(f32[128,512]{1,0:T(8,128)} %param.10) | copy-start | bytes 786436
  11.3 65.4 %collective-permute-start.9 = (f32[128,512]{0,1:T(8,128)S(1)}, f32[128,512]{0,1:T(8,128)S(1)}, u32[]{:S(2)}, u32[]{:S(2)}) collective-permute-start(f32[128,512]{0,1:T(8,128)S(1)} %copy.30), channel_id=1, source_target_pairs={{0,3},{1,2},{2,1},{3,0},{4,7},{5,6},{6,5},{7,4},{8,11},{9,10},{10,... | collective-permute-start | bytes 786440 | tf_op jit(solution)/shard_map/ppermute | solution.py:718
  13.8 63.1 %collective-permute-start.8 = (f32[128,512]{0,1:T(8,128)S(1)}, f32[128,512]{0,1:T(8,128)S(1)}, u32[]{:S(2)}, u32[]{:S(2)}) collective-permute-start(f32[128,512]{0,1:T(8,128)S(1)} %copy.30), channel_id=1, source_target_pairs={{0,2},{1,3},{2,0},{3,1},{4,6},{5,7},{6,4},{7,5},{8,10},{9,11},{10,... | collective-permute-start | bytes 786440 | tf_op jit(solution)/shard_map/ppermute | solution.py:718
  14.5 9.7 %collective-permute-start.1 = (bf16[6,256,128]{2,1,0:T(8,128)(2,1)}, bf16[6,256,128]{2,1,0:T(8,128)(2,1)S(1)}, u32[]{:S(2)}, u32[]{:S(2)}) collective-permute-start(bf16[6,256,128]{2,1,0:T(8,128)(2,1)} %get-tuple-element.60), channel_id=1, source_target_pairs={{0,1},{1,2},{2,3},{4,5},{5,6},{6,7},{8,9},{9,10},{10,11},{12,13},{... | collective-permute-start | bytes 1179656 | tf_op jit(solution)/shard_map/ppermute | solution.py:139
  16.4 7.8 %collective-permute-start = (bf16[6,256,128]{2,1,0:T(8,128)(2,1)}, bf16[6,256,128]{2,1,0:T(8,128)(2,1)S(1)}, u32[]{:S(2)}, u32[]{:S(2)}) collective-permute-start(bf16[6,256,128]{2,1,0:T(8,128)(2,1)} %get-tuple-element.60), channel_id=1, source_target_pairs={{1,0},{2,1},{3,2},{5,4},{6,5},{7,6},{9,8},{10,9},{11,10},{13,12},{... | collective-permute-start | bytes 1179656 | tf_op jit(solution)/shard_map/ppermute | solution.py:138
  17.7 41.3 %collective-permute-start.2 = (f32[6,64,128]{2,1,0:T(8,128)}, f32[6,64,128]{2,1,0:T(8,128)S(1)}, u32[]{:S(2)}, u32[]{:S(2)}) collective-permute-start(f32[6,64,128]{2,1,0:T(8,128)} %get-tuple-element.63), channel_id=1, source_target_pairs={{4,0},{8,4},{12,8},{16,12},{20,16},{24,20},{28,24},{0,28},{5,1},{9... | collective-permute-start | bytes 589832 | tf_op jit(solution)/shard_map/ppermute | solution.py:141
  23.4 0.7 copy-start.12
  24.2 8.6 %collective-permute-start.3 = (f32[6,64,128]{2,1,0:T(8,128)}, f32[6,64,128]{2,1,0:T(8,128)S(1)}, u32[]{:S(2)}, u32[]{:S(2)}) collective-permute-start(f32[6,64,128]{2,1,0:T(8,128)} %get-tuple-element.64), channel_id=1, source_target_pairs={{0,4},{4,8},{8,12},{12,16},{16,20},{20,24},{24,28},{28,0},{1,5},{5... | collective-permute-start | bytes 589832 | tf_op jit(solution)/shard_map/ppermute | solution.py:140
  32.8 0.7 copy-start.3
  50.3 30.1 %collective-permute-start.10 = (f32[128,8,128]{2,1,0:T(8,128)}, f32[128,8,128]{2,1,0:T(8,128)S(1)}, u32[]{:S(2)}, u32[]{:S(2)}) collective-permute-start(f32[128,8,128]{2,1,0:T(8,128)} %get-tuple-element.91), channel_id=1, source_target_pairs={{0,1},{1,0},{2,3},{3,2},{4,5},{5,4},{6,7},{7,6},{8,9},{9,8},{10,11... | collective-permute-start | bytes 1572872 | tf_op jit(solution)/shard_map/ppermute | solution.py:718
  55.6 25.1 %collective-permute-start.11 = (f32[128,8,128]{2,1,0:T(8,128)}, f32[128,8,128]{2,1,0:T(8,128)S(1)}, u32[]{:S(2)}, u32[]{:S(2)}) collective-permute-start(f32[128,8,128]{2,1,0:T(8,128)} %get-tuple-element.92), channel_id=1, source_target_pairs={{0,2},{1,3},{2,0},{3,1},{4,6},{5,7},{6,4},{7,5},{8,10},{9,11},{10,... | collective-permute-start | bytes 1572872 | tf_op jit(solution)/shard_map/ppermute | solution.py:718
  59.0 0.7 copy-start.2
  59.0 23.9 %collective-permute-start.12 = (f32[128,8,128]{2,1,0:T(8,128)}, f32[128,8,128]{2,1,0:T(8,128)}, u32[]{:S(2)}, u32[]{:S(2)}) collective-permute-start(f32[128,8,128]{2,1,0:T(8,128)} %get-tuple-element.93), channel_id=1, source_target_pairs={{0,3},{1,2},{2,1},{3,0},{4,7},{5,6},{6,5},{7,4},{8,11},{9,10},{10,... | collective-permute-start | bytes 1572872 | tf_op jit(solution)/shard_map/ppermute | solution.py:718
  59.7 25.1 %copy-start.15 = (f32[512]{0:T(512)S(1)}, f32[512]{0:T(512)}, u32[]{:S(2)}) copy-start(f32[512]{0:T(512)} %param.11) | copy-start | bytes 6148
  76.7 7.6 %collective-permute-start.13 = (f32[128,8,128]{2,1,0:T(8,128)}, f32[128,8,128]{2,1,0:T(8,128)}, u32[]{:S(2)}, u32[]{:S(2)}) collective-permute-start(f32[128,8,128]{2,1,0:T(8,128)} %get-tuple-element.95), channel_id=1, source_target_pairs={{0,1},{1,0},{2,3},{3,2},{4,5},{5,4},{6,7},{7,6},{8,9},{9,8},{10,11... | collective-permute-start | bytes 1572872 | tf_op jit(solution)/shard_map/ppermute | solution.py:718
  76.9 2.3 collective-permute-start.7
  79.3 15.4 %collective-permute-start.14 = (f32[128,8,128]{2,1,0:T(8,128)}, f32[128,8,128]{2,1,0:T(8,128)}, u32[]{:S(2)}, u32[]{:S(2)}) collective-permute-start(f32[128,8,128]{2,1,0:T(8,128)} %get-tuple-element.96), channel_id=1, source_target_pairs={{0,2},{1,3},{2,0},{3,1},{4,6},{5,7},{6,4},{7,5},{8,10},{9,11},{10,... | collective-permute-start | bytes 1572872 | tf_op jit(solution)/shard_map/ppermute | solution.py:718
  80.4 0.8 copy-start.10
  80.4 25.0 %collective-permute-start.15 = (f32[128,8,128]{2,1,0:T(8,128)}, f32[128,8,128]{2,1,0:T(8,128)}, u32[]{:S(2)}, u32[]{:S(2)}) collective-permute-start(f32[128,8,128]{2,1,0:T(8,128)} %get-tuple-element.97), channel_id=1, source_target_pairs={{0,3},{1,2},{2,1},{3,0},{4,7},{5,6},{6,5},{7,4},{8,11},{9,10},{10,... | collective-permute-start | bytes 1572872 | tf_op jit(solution)/shard_map/ppermute | solution.py:718
  81.2 0.8 copy-start.11
  82.0 69.5 %collective-permute-start.4 = (f32[256,8,128]{2,1,0:T(8,128)}, f32[256,8,128]{2,1,0:T(8,128)S(1)}, u32[]{:S(2)}, u32[]{:S(2)}) collective-permute-start(f32[256,8,128]{2,1,0:T(8,128)} %get-tuple-element.71), channel_id=1, source_target_pairs={{0,1},{1,0},{2,3},{3,2},{4,5},{5,4},{6,7},{7,6},{8,9},{9,8},{10,11... | collective-permute-start | bytes 3145736 | tf_op jit(solution)/shard_map/ppermute | solution.py:718
  82.9 69.6 %collective-permute-start.5 = (f32[256,8,128]{2,1,0:T(8,128)}, f32[256,8,128]{2,1,0:T(8,128)}, u32[]{:S(2)}, u32[]{:S(2)}) collective-permute-start(f32[256,8,128]{2,1,0:T(8,128)} %get-tuple-element.72), channel_id=1, source_target_pairs={{0,2},{1,3},{2,0},{3,1},{4,6},{5,7},{6,4},{7,5},{8,10},{9,11},{10,... | collective-permute-start | bytes 3145736 | tf_op jit(solution)/shard_map/ppermute | solution.py:718
  84.3 68.2 %collective-permute-start.6 = (f32[256,8,128]{2,1,0:T(8,128)}, f32[256,8,128]{2,1,0:T(8,128)}, u32[]{:S(2)}, u32[]{:S(2)}) collective-permute-start(f32[256,8,128]{2,1,0:T(8,128)} %get-tuple-element.73), channel_id=1, source_target_pairs={{0,3},{1,2},{2,1},{3,0},{4,7},{5,6},{6,5},{7,4},{8,11},{9,10},{10,... | collective-permute-start | bytes 3145736 | tf_op jit(solution)/shard_map/ppermute | solution.py:718
  85.7 44.6 %copy-start = (bf16[512,512]{0,1:T(8,128)(2,1)}, bf16[512,512]{0,1:T(8,128)(2,1)S(1)}, u32[]{:S(2)}) copy-start(bf16[512,512]{0,1:T(8,128)(2,1)S(1)} %get-tuple-element.115) | copy-start | bytes 1572868
  85.8 44.6 %copy-start.1 = (bf16[512,512]{0,1:T(8,128)(2,1)}, bf16[512,512]{0,1:T(8,128)(2,1)S(1)}, u32[]{:S(2)}) copy-start(bf16[512,512]{0,1:T(8,128)(2,1)S(1)} %get-tuple-element.116) | copy-start | bytes 1572868
  113.8 24.3 %all-to-all-start.1 = ((f32[8,2,8,512]{3,2,1,0:T(8,128)}), f32[8,2,8,512]{3,2,1,0:T(8,128)S(1)}, u32[]{:S(2)}, u32[]{:S(2)}) async-start(f32[8,2,8,512]{3,2,1,0:T(8,128)} %get-tuple-element.99), calls=%async_computation.1 | async-start | bytes 524288 | tf_op jit(solution)/shard_map/all_to_all | solution.py:723
  138.0 0.7 copy-start.9
  149.1 56.6 %collective-permute-start.16 = (f32[256,8,128]{2,1,0:T(8,128)}, f32[256,8,128]{2,1,0:T(8,128)S(1)}, u32[]{:S(2)}, u32[]{:S(2)}) collective-permute-start(f32[256,8,128]{2,1,0:T(8,128)} %get-tuple-element.103), channel_id=1, source_target_pairs={{0,1},{1,0},{2,3},{3,2},{4,5},{5,4},{6,7},{7,6},{8,9},{9,8},{10,11... | collective-permute-start | bytes 3145736 | tf_op jit(solution)/shard_map/ppermute | solution.py:718
  149.5 57.7 %collective-permute-start.17 = (f32[256,8,128]{2,1,0:T(8,128)}, f32[256,8,128]{2,1,0:T(8,128)S(1)}, u32[]{:S(2)}, u32[]{:S(2)}) collective-permute-start(f32[256,8,128]{2,1,0:T(8,128)} %get-tuple-element.104), channel_id=1, source_target_pairs={{0,2},{1,3},{2,0},{3,1},{4,6},{5,7},{6,4},{7,5},{8,10},{9,11},{10,... | collective-permute-start | bytes 3145736 | tf_op jit(solution)/shard_map/ppermute | solution.py:718
  151.5 1.0 copy-start.7
  152.5 54.8 %collective-permute-start.18 = (f32[256,8,128]{2,1,0:T(8,128)}, f32[256,8,128]{2,1,0:T(8,128)S(1)}, u32[]{:S(2)}, u32[]{:S(2)}) collective-permute-start(f32[256,8,128]{2,1,0:T(8,128)} %get-tuple-element.105), channel_id=1, source_target_pairs={{0,3},{1,2},{2,1},{3,0},{4,7},{5,6},{6,5},{7,4},{8,11},{9,10},{10,... | collective-permute-start | bytes 3145736 | tf_op jit(solution)/shard_map/ppermute | solution.py:718
  160.5 33.0 %all-to-all-start = ((f32[8,2,8,512]{3,2,1,0:T(8,128)}), f32[8,2,8,512]{3,2,1,0:T(8,128)S(1)}, u32[]{:S(2)}, u32[]{:S(2)}) async-start(f32[8,2,8,512]{3,2,1,0:T(8,128)} %get-tuple-element.76), calls=%async_computation | async-start | bytes 524288 | tf_op jit(solution)/shard_map/all_to_all | solution.py:723
  181.7 27.6 %copy-start.13 = (f32[2,4,8,64]{3,2,1,0:T(8,128)S(1)}, f32[2,4,8,64]{3,2,1,0:T(8,128)}, u32[]{:S(2)}) copy-start(f32[2,4,8,64]{3,2,1,0:T(8,128)} %copy-done.12) | copy-start | bytes 49156
  193.5 0.7 copy-start.8
  205.1 3.8 %collective-permute-start.22 = (f32[128,8,128]{2,1,0:T(8,128)}, f32[128,8,128]{2,1,0:T(8,128)}, u32[]{:S(2)}, u32[]{:S(2)}) collective-permute-start(f32[128,8,128]{2,1,0:T(8,128)} %get-tuple-element.111), channel_id=1, source_target_pairs={{0,1},{1,0},{2,3},{3,2},{4,5},{5,4},{6,7},{7,6},{8,9},{9,8},{10,11... | collective-permute-start | bytes 1572872 | tf_op jit(solution)/shard_map/ppermute | solution.py:718
  205.2 73.3 %collective-permute-start.19 = (f32[128,8,128]{2,1,0:T(8,128)}, f32[128,8,128]{2,1,0:T(8,128)}, u32[]{:S(2)}, u32[]{:S(2)}) collective-permute-start(f32[128,8,128]{2,1,0:T(8,128)} %get-tuple-element.107), channel_id=1, source_target_pairs={{0,1},{1,0},{2,3},{3,2},{4,5},{5,4},{6,7},{7,6},{8,9},{9,8},{10,11... | collective-permute-start | bytes 1572872 | tf_op jit(solution)/shard_map/ppermute | solution.py:718
  205.7 67.4 %copy-start.4 = (f32[256,8,128]{2,1,0:T(8,128)}, f32[256,8,128]{2,1,0:T(8,128)S(1)}, u32[]{:S(2)}) copy-start(f32[256,8,128]{2,1,0:T(8,128)S(1)} %collective-permute-done.16.refs_1_) | copy-start | bytes 3145732
  205.7 67.4 %collective-permute-start.23 = (f32[128,8,128]{2,1,0:T(8,128)}, f32[128,8,128]{2,1,0:T(8,128)}, u32[]{:S(2)}, u32[]{:S(2)}) collective-permute-start(f32[128,8,128]{2,1,0:T(8,128)} %get-tuple-element.112), channel_id=1, source_target_pairs={{0,2},{1,3},{2,0},{3,1},{4,6},{5,7},{6,4},{7,5},{8,10},{9,11},{10,... | collective-permute-start | bytes 1572872 | tf_op jit(solution)/shard_map/ppermute | solution.py:718
  207.2 66.0 %copy-start.5 = (f32[256,8,128]{2,1,0:T(8,128)}, f32[256,8,128]{2,1,0:T(8,128)S(1)}, u32[]{:S(2)}) copy-start(f32[256,8,128]{2,1,0:T(8,128)S(1)} %collective-permute-done.17.refs_2_) | copy-start | bytes 3145732
  207.2 66.0 %collective-permute-start.24 = (f32[128,8,128]{2,1,0:T(8,128)}, f32[128,8,128]{2,1,0:T(8,128)}, u32[]{:S(2)}, u32[]{:S(2)}) collective-permute-start(f32[128,8,128]{2,1,0:T(8,128)} %get-tuple-element.113), channel_id=1, source_target_pairs={{0,3},{1,2},{2,1},{3,0},{4,7},{5,6},{6,5},{7,4},{8,11},{9,10},{10,... | collective-permute-start | bytes 1572872 | tf_op jit(solution)/shard_map/ppermute | solution.py:718
  207.3 65.8 %copy-start.6 = (f32[256,8,128]{2,1,0:T(8,128)}, f32[256,8,128]{2,1,0:T(8,128)S(1)}, u32[]{:S(2)}) copy-start(f32[256,8,128]{2,1,0:T(8,128)S(1)} %collective-permute-done.18.refs_3_) | copy-start | bytes 3145732
  207.3 71.2 %collective-permute-start.20 = (f32[128,8,128]{2,1,0:T(8,128)}, f32[128,8,128]{2,1,0:T(8,128)}, u32[]{:S(2)}, u32[]{:S(2)}) collective-permute-start(f32[128,8,128]{2,1,0:T(8,128)} %get-tuple-element.108), channel_id=1, source_target_pairs={{0,2},{1,3},{2,0},{3,1},{4,6},{5,7},{6,4},{7,5},{8,10},{9,11},{10,... | collective-permute-start | bytes 1572872 | tf_op jit(solution)/shard_map/ppermute | solution.py:718
  208.9 69.6 %collective-permute-start.21 = (f32[128,8,128]{2,1,0:T(8,128)}, f32[128,8,128]{2,1,0:T(8,128)}, u32[]{:S(2)}, u32[]{:S(2)}) collective-permute-start(f32[128,8,128]{2,1,0:T(8,128)} %get-tuple-element.109), channel_id=1, source_target_pairs={{0,3},{1,2},{2,1},{3,0},{4,7},{5,6},{6,5},{7,4},{8,11},{9,10},{10,... | collective-permute-start | bytes 1572872 | tf_op jit(solution)/shard_map/ppermute | solution.py:718
  209.3 45.6 %all-to-all-start.2 = ((f32[32,8,128]{2,1,0:T(8,128)}), f32[32,8,128]{2,1,0:T(8,128)S(1)}, u32[]{:S(2)}, u32[]{:S(2)}) async-start(f32[32,8,128]{2,1,0:T(8,128)} %get-tuple-element.101), calls=%async_computation.2 | async-start | bytes 262144 | tf_op jit(solution)/shard_map/all_to_all | solution.py:723
